TPU v7x, 32 devices: a whole 2x2x4 slice. The times are simulated.
32 devices in a mesh: seq: 8 (over y, x, core), batch: 4 (over z).
Axes of the slice: x: 2, y: 2, z: 4, core: 2. Of those that a mesh axis runs over, the one named last changes fastest.
Arguments:
- inputs: bfloat16 [4, 1536, 1024], P('batch', 'seq'), may hold values from -6 to 6
- cotangent: bfloat16 [4, 1536, 1024], P('batch', 'seq'), may hold values from -6 to 6
- lengths: int32 [4, 1], P('batch'), may hold values from 384 to 1536, as said below
- rand_owners: int32 [4, 24, 3], P('batch'), may hold values from 0 to 7, all different within a row; in each aligned block of 3 rows (0 to 2, 3 to 5, ..., all dimensions but the last counted through in order) at most 2 rows name the same one
- rand_offsets: int32 [4, 24, 3], P('batch'), may hold values from 0 to 2
- global_ids: int32 [4, 1, 2], P('batch'), may hold values from 0 to 5
- ln1_gain: bfloat16 [1024], replicated, may hold values from 0.5 to 1.5
- ln1_shift: bfloat16 [1024], replicated, may hold values from -3 to 3
- w_query: bfloat16 [1024, 1024], replicated, may hold values from -0.1875 to 0.1875
- w_key: bfloat16 [1024, 1024], replicated, may hold values from -0.1875 to 0.1875
- w_value: bfloat16 [1024, 1024], replicated, may hold values from -0.1875 to 0.1875
- w_out: bfloat16 [1024, 1024], replicated, may hold values from -2 to 2
- ln2_gain: bfloat16 [1024], replicated, may hold values from 0.5 to 1.5
- ln2_shift: bfloat16 [1024], replicated, may hold values from -3 to 3
- w_in: bfloat16 [1024, 4096], replicated, may hold values from -0.1875 to 0.1875
- b_in: bfloat16 [4096], replicated, may hold values from -3 to 3
- w_back: bfloat16 [4096, 1024], replicated, may hold values from -0.09375 to 0.09375
- b_back: bfloat16 [1024], replicated, may hold values from -3 to 3
Outputs:
- output: bfloat16 [4, 1536, 1024], P('batch', 'seq')
- input_grad: bfloat16 [4, 1536, 1024], P('batch', 'seq')
- ln1_gain_grad: float32 [1024], P(('seq', 'batch'))
- ln1_shift_grad: float32 [1024], P(('seq', 'batch'))
- query_grad: float32 [1024, 1024], P(('seq', 'batch'))
- key_grad: float32 [1024, 1024], P(('seq', 'batch'))
- value_grad: float32 [1024, 1024], P(('seq', 'batch'))
- out_grad: float32 [1024, 1024], P(('seq', 'batch'))
- ln2_gain_grad: float32 [1024], P(('seq', 'batch'))
- ln2_shift_grad: float32 [1024], P(('seq', 'batch'))
- in_grad: float32 [1024, 4096], P(('seq', 'batch'))
- in_bias_grad: float32 [4096], P(('seq', 'batch'))
- back_grad: float32 [4096, 1024], P(('seq', 'batch'))
- back_bias_grad: float32 [1024], P(('seq', 'batch'))
Inputs may be any that keep to these rules, and one draw needn't show every extreme that they name: `rand_owners`: each row names 3 different groups of the item, numbered 0 .. 7; among the 3 rows of one group no group is named more than 2 times, and 2 is reached in every draw. `lengths`: most items are about a quarter of 1536 long; some item has exactly 1536 tokens.
All inputs are finite; a program needn't handle non-finite values.
Results may differ from a plain program's by a relative error of at most 0.015.
Values may be sent and summed in bfloat16 or wider, within the bound.
No kernel may reach another device: no remote copies, remote signals or barrier semaphores. Data moves between devices by JAX's collectives and lax.ppermute only.
A program may use at most 320 MiB of HBM per device.

v0:
```python
import jax
import jax.numpy as jnp
from jax import lax
from jax.sharding import PartitionSpec as P

HEADS = 16
BLK = 64
RAND = 3


norm_eps = 1e-05
masked_score = -1e30
highest = lax.Precision.HIGHEST


def with_halo(cells, sides, width):
    for axis, dim in sides:
        count = lax.axis_size(axis)
        ends = count - 1
        head = lax.slice_in_dim(cells, 0, width, axis=dim)
        tail = lax.slice_in_dim(cells, cells.shape[dim] - width, cells.shape[dim], axis=dim)
        cells = jnp.concatenate(
            [
                lax.ppermute(tail, axis, [(i, (i + 1) % count) for i in range(ends)]),
                cells,
                lax.ppermute(head, axis, [((i + 1) % count, i) for i in range(ends)]),
            ],
            axis=dim,
        )
    return cells


def matmul(left, right):
    return jnp.dot(left, right, preferred_element_type=jnp.float32)


def matmul_left(left, right):
    return lax.dot_general(
        left, right, (((0,), (0,)), ((), ())), preferred_element_type=jnp.float32
    )


def matmul_right(left, right):
    return lax.dot_general(
        left, right, (((1,), (1,)), ((), ())), preferred_element_type=jnp.float32
    )


def normalize(values, ln_gain, ln_shift):
    average = jnp.mean(values, axis=-1, keepdims=True)
    centered = values - average
    variance = jnp.mean(centered * centered, axis=-1, keepdims=True)
    inverse = lax.rsqrt(variance + norm_eps)
    scaled = centered * inverse
    return (scaled * ln_gain + ln_shift, scaled, inverse)


def normalize_back(grad_normed, scaled, inverse, ln_gain):
    grad_scaled = grad_normed * ln_gain
    inner_mean = jnp.mean(grad_scaled, axis=-1, keepdims=True)
    along_mean = jnp.mean(grad_scaled * scaled, axis=-1, keepdims=True)
    return inverse * (grad_scaled - inner_mean - scaled * along_mean)


def slot_tables(owners, offsets, seq_index, block_count, slot_count):
    requests = owners.shape[1]
    prior_blocks = (jnp.arange(requests)[None, :] < jnp.arange(requests)[:, None]).astype(jnp.int32)
    same_owner = (owners[:, :, None] == owners[:, None, :]).astype(jnp.int32)
    ranks = jnp.sum(same_owner * prior_blocks[None], axis=2)
    chosen = (
        (owners[:, None, :] == seq_index)
        & (ranks[:, None, :] == jnp.arange(slot_count)[None, :, None])
    ).astype(jnp.int32)
    block_onehot = (offsets[:, :, None] == jnp.arange(block_count)[None, None, :]).astype(jnp.int32)
    send_table = jnp.einsum("rmj,rjb->rmb", chosen, block_onehot)
    my_owners = lax.dynamic_index_in_dim(owners, seq_index, 0, keepdims=False)
    my_ranks = lax.dynamic_index_in_dim(ranks, seq_index, 0, keepdims=False)
    my_offsets = lax.dynamic_index_in_dim(offsets, seq_index, 0, keepdims=False)
    return (send_table, my_owners * slot_count + my_ranks, my_owners, my_offsets)


def fill_slots(send_table, kv_blocks):
    return jnp.einsum(
        "rmb,bkc->rmkc",
        send_table.astype(jnp.bfloat16),
        kv_blocks,
        preferred_element_type=jnp.float32,
    ).astype(jnp.bfloat16)


def score_blocks(query_heads, key_heads, valid, scale):
    score_values = (
        jnp.einsum("bqhd,bkhd->bhqk", query_heads, key_heads, preferred_element_type=jnp.float32)
        * scale
    )
    return jnp.where(valid[:, None, None, :], score_values, masked_score)


def shards(
    inputs,
    cotangent,
    lengths,
    rand_owners,
    rand_offsets,
    global_ids,
    ln1_gain,
    ln1_shift,
    w_query,
    w_key,
    w_value,
    w_out,
    ln2_gain,
    ln2_shift,
    w_in,
    b_in,
    w_back,
    b_back,
):
    seq_count = lax.axis_size("seq")
    seq_index = lax.axis_index("seq")
    token_count = inputs.shape[1]
    model_width = inputs.shape[2]
    double_width = 2 * model_width
    block_count = token_count // BLK
    head_dim = model_width // HEADS
    scale = head_dim ** (-0.5)
    pack_count = seq_count // seq_count
    pack_index = seq_index // seq_count
    local_index = seq_index - pack_index * seq_count
    slot_count = max(2, (block_count * RAND + seq_count - 1) // seq_count)
    length = lax.dynamic_index_in_dim(lengths[0], pack_index, 0, keepdims=False)
    global_list = lax.dynamic_index_in_dim(global_ids[0], pack_index, 0, keepdims=False)
    global_count = global_list.shape[0]
    key_blocks = 3 + RAND + global_count
    key_count = key_blocks * BLK
    gain_one = ln1_gain.astype(jnp.float32)
    gain_two = ln2_gain.astype(jnp.float32)
    pack_onehot = (jnp.arange(pack_count, dtype=jnp.int32) == pack_index).astype(jnp.float32)
    residual_in = inputs[0].astype(jnp.float32)
    normed, scaled_one, inverse_one = normalize(
        residual_in, gain_one, ln1_shift.astype(jnp.float32)
    )
    normed_low = normed.astype(jnp.bfloat16)
    queries = matmul(normed_low, w_query).astype(jnp.bfloat16)
    keyvals = jnp.concatenate(
        [matmul(normed_low, w_key), matmul(normed_low, w_value)], axis=1
    ).astype(jnp.bfloat16)
    kv_blocks = keyvals.reshape(block_count, BLK, double_width)
    owners_local = rand_owners[0].reshape(seq_count, block_count * RAND)
    group_base = (jnp.arange(seq_count, dtype=jnp.int32) // seq_count * seq_count)[:, None]
    owners_all = owners_local + group_base
    offsets_all = rand_offsets[0].reshape(seq_count, block_count * RAND)
    send_table, slot_index, my_owners, my_offsets = slot_tables(
        owners_all, offsets_all, seq_index, block_count, slot_count
    )
    received = lax.all_to_all(
        fill_slots(send_table, kv_blocks), "seq", split_axis=0, concat_axis=0, tiled=True
    )
    fetched = jnp.take(
        received.reshape(seq_count * slot_count, BLK, double_width), slot_index, axis=0
    ).reshape(block_count, RAND, BLK, double_width)
    padded = with_halo(keyvals, (("seq", 0),), BLK).reshape(block_count + 2, BLK, double_width)
    window = jnp.stack([padded[:-2], padded[1:-1], padded[2:]], axis=1)
    global_table = (
        global_list[:, None] - local_index * block_count == jnp.arange(block_count)[None, :]
    ).astype(jnp.float32)
    global_terms = jnp.einsum(
        "gb,bkc->gkc",
        global_table.astype(jnp.bfloat16),
        kv_blocks,
        preferred_element_type=jnp.float32,
    )
    packed_terms = pack_onehot[:, None, None, None] * global_terms[None]
    global_all = lax.psum(packed_terms.astype(jnp.bfloat16), "seq").astype(jnp.float32)
    global_kv = lax.dynamic_index_in_dim(global_all, pack_index, 0, keepdims=False).astype(
        jnp.bfloat16
    )
    own_blocks = local_index * block_count + jnp.arange(block_count, dtype=jnp.int32)
    window_ids = own_blocks[:, None] + jnp.arange(3, dtype=jnp.int32)[None, :] - 1
    random_ids = ((my_owners - pack_index * seq_count) * block_count + my_offsets).reshape(
        block_count, RAND
    )
    block_ids = jnp.concatenate(
        [
            window_ids,
            random_ids,
            jnp.broadcast_to(global_list[None, :], (block_count, global_count)),
        ],
        axis=1,
    )
    positions = (block_ids[:, :, None] * BLK + jnp.arange(BLK, dtype=jnp.int32)).reshape(
        block_count, key_count
    )
    valid = (positions >= 0) & (positions < length)

    def assemble(fetched_blocks):
        shared = jnp.broadcast_to(global_kv[None], (block_count, global_count, BLK, double_width))
        gathered = jnp.concatenate([window, fetched_blocks, shared], axis=1).reshape(
            block_count, key_count, double_width
        )
        key_heads = gathered[:, :, :model_width].reshape(block_count, key_count, HEADS, head_dim)
        value_heads = gathered[:, :, model_width:].reshape(block_count, key_count, HEADS, head_dim)
        return (key_heads, value_heads)

    key_heads, value_heads = assemble(fetched)
    query_heads = queries.reshape(block_count, BLK, HEADS, head_dim)
    score_values = score_blocks(query_heads, key_heads, valid, scale)
    top = jnp.max(score_values, axis=-1, keepdims=True)
    raised = jnp.exp(score_values - top)
    total = jnp.sum(raised, axis=-1, keepdims=True)
    log_total = top + jnp.log(total)
    attention_weights = (raised / total).astype(jnp.bfloat16)
    attended = jnp.einsum(
        "bhqk,bkhd->bqhd", attention_weights, value_heads, preferred_element_type=jnp.float32
    )
    attended = attended.reshape(token_count, model_width).astype(jnp.bfloat16)
    middle = residual_in + matmul(attended, w_out)
    normed_two, scaled_two, inverse_two = normalize(middle, gain_two, ln2_shift.astype(jnp.float32))
    normed_two_low = normed_two.astype(jnp.bfloat16)
    inner = matmul(normed_two_low, w_in) + b_in.astype(jnp.float32)
    activated = jax.nn.gelu(inner, approximate=False).astype(jnp.bfloat16)
    output = (middle + matmul(activated, w_back) + b_back.astype(jnp.float32)).astype(jnp.bfloat16)
    grad_out = cotangent[0]
    grad_out_full = grad_out.astype(jnp.float32)
    grad_w_back = matmul_left(activated, grad_out)
    grad_b_back = jnp.sum(grad_out_full, axis=0)
    grad_activated = matmul_right(grad_out, w_back)
    gelu_value, gelu_pull = jax.vjp(lambda values: jax.nn.gelu(values, approximate=False), inner)
    grad_inner = gelu_pull(grad_activated)[0].astype(jnp.bfloat16)
    grad_w_in = matmul_left(normed_two_low, grad_inner)
    grad_b_in = jnp.sum(grad_inner.astype(jnp.float32), axis=0)
    grad_normed_two = matmul_right(grad_inner, w_in)
    grad_ln2_gain = jnp.sum(grad_normed_two * scaled_two, axis=0)
    grad_ln2_shift = jnp.sum(grad_normed_two, axis=0)
    grad_middle = grad_out_full + normalize_back(grad_normed_two, scaled_two, inverse_two, gain_two)
    grad_middle_low = grad_middle.astype(jnp.bfloat16)
    grad_w_out = matmul_left(attended, grad_middle_low)
    grad_attended = matmul_right(grad_middle_low, w_out).astype(jnp.bfloat16)
    received_again = lax.all_to_all(
        fill_slots(send_table, kv_blocks), "seq", split_axis=0, concat_axis=0, tiled=True
    )
    fetched_again = jnp.take(
        received_again.reshape(seq_count * slot_count, BLK, double_width), slot_index, axis=0
    ).reshape(block_count, RAND, BLK, double_width)
    key_heads, value_heads = assemble(fetched_again)
    scores_again = score_blocks(query_heads, key_heads, valid, scale)
    weights_full = jnp.exp(scores_again - log_total)
    grad_heads = grad_attended.reshape(block_count, BLK, HEADS, head_dim)
    grad_value_heads = jnp.einsum(
        "bhqk,bqhd->bkhd",
        weights_full.astype(jnp.bfloat16),
        grad_heads,
        preferred_element_type=jnp.float32,
    )
    grad_weights = jnp.einsum(
        "bqhd,bkhd->bhqk", grad_heads, value_heads, preferred_element_type=jnp.float32
    )
    correction = jnp.sum(weights_full * grad_weights, axis=-1, keepdims=True)
    grad_scores = (weights_full * (grad_weights - correction)).astype(jnp.bfloat16)
    grad_queries = (
        jnp.einsum("bhqk,bkhd->bqhd", grad_scores, key_heads, preferred_element_type=jnp.float32)
        * scale
    )
    grad_queries = grad_queries.reshape(token_count, model_width).astype(jnp.bfloat16)
    grad_key_heads = (
        jnp.einsum("bhqk,bqhd->bkhd", grad_scores, query_heads, preferred_element_type=jnp.float32)
        * scale
    )
    grad_lists = jnp.concatenate(
        [
            grad_key_heads.reshape(block_count, key_count, model_width),
            grad_value_heads.reshape(block_count, key_count, model_width),
        ],
        axis=2,
    )
    grad_lists = grad_lists.reshape(block_count, key_blocks, BLK, double_width)
    zero_block = jnp.zeros((1, BLK, double_width), jnp.float32)
    padded_grads = (
        jnp.concatenate([grad_lists[:, 0], zero_block, zero_block], axis=0)
        + jnp.concatenate([zero_block, grad_lists[:, 1], zero_block], axis=0)
        + jnp.concatenate([zero_block, zero_block, grad_lists[:, 2]], axis=0)
    )
    rims = jnp.concatenate([padded_grads[0], padded_grads[-1]], axis=0)
    returned_rims = with_halo(rims.astype(jnp.bfloat16), (("seq", 0),), BLK).astype(rims.dtype)
    grad_blocks = padded_grads[1:-1]
    grad_blocks = grad_blocks.at[0].add(returned_rims[:BLK]).at[-1].add(returned_rims[3 * BLK :])
    random_grads = grad_lists[:, 3 : 3 + RAND].reshape(block_count * RAND, BLK, double_width)
    slot_grads = (
        jnp.zeros((seq_count * slot_count, BLK, double_width), jnp.float32)
        .at[slot_index]
        .add(random_grads)
    )
    returned_slots = lax.all_to_all(
        slot_grads.reshape(seq_count, slot_count, BLK, double_width).astype(jnp.bfloat16),
        "seq",
        split_axis=0,
        concat_axis=0,
        tiled=True,
    ).astype(jnp.float32)
    grad_blocks = grad_blocks + jnp.einsum(
        "rmb,rmkc->bkc", send_table.astype(jnp.float32), returned_slots, precision=highest
    )
    global_grads = jnp.sum(grad_lists[:, 3 + RAND :], axis=0)
    packed_grads = pack_onehot[:, None, None, None] * global_grads[None]
    global_sums = lax.psum(packed_grads.astype(jnp.bfloat16), "seq").astype(jnp.float32)
    global_total = lax.dynamic_index_in_dim(global_sums, pack_index, 0, keepdims=False)
    grad_blocks = grad_blocks + jnp.einsum(
        "gb,gkc->bkc", global_table, global_total, precision=highest
    )
    grad_keyvals = grad_blocks.reshape(token_count, double_width).astype(jnp.bfloat16)
    grad_keys = grad_keyvals[:, :model_width]
    grad_values = grad_keyvals[:, model_width:]
    grad_w_query = matmul_left(normed_low, grad_queries)
    grad_w_key = matmul_left(normed_low, grad_keys)
    grad_w_value = matmul_left(normed_low, grad_values)
    grad_normed = (
        matmul_right(grad_queries, w_query)
        + matmul_right(grad_keys, w_key)
        + matmul_right(grad_values, w_value)
    )
    grad_ln1_gain = jnp.sum(grad_normed * scaled_one, axis=0)
    grad_ln1_shift = jnp.sum(grad_normed, axis=0)
    input_grad = (
        grad_middle + normalize_back(grad_normed, scaled_one, inverse_one, gain_one)
    ).astype(jnp.bfloat16)
    summed = (
        lax.psum_scatter(grad_ln1_gain, ("seq", "batch"), scatter_dimension=0, tiled=True),
        lax.psum_scatter(grad_ln1_shift, ("seq", "batch"), scatter_dimension=0, tiled=True),
        lax.psum_scatter(grad_w_query, ("seq", "batch"), scatter_dimension=0, tiled=True),
        lax.psum_scatter(grad_w_key, ("seq", "batch"), scatter_dimension=0, tiled=True),
        lax.psum_scatter(grad_w_value, ("seq", "batch"), scatter_dimension=0, tiled=True),
        lax.psum_scatter(grad_w_out, ("seq", "batch"), scatter_dimension=0, tiled=True),
        lax.psum_scatter(grad_w_in, ("seq", "batch"), scatter_dimension=0, tiled=True),
        lax.psum_scatter(grad_b_in, ("seq", "batch"), scatter_dimension=0, tiled=True),
        lax.psum_scatter(grad_w_back, ("seq", "batch"), scatter_dimension=0, tiled=True),
        lax.psum_scatter(grad_b_back, ("seq", "batch"), scatter_dimension=0, tiled=True),
        lax.psum_scatter(grad_ln2_gain, ("seq", "batch"), scatter_dimension=0, tiled=True),
        lax.psum_scatter(grad_ln2_shift, ("seq", "batch"), scatter_dimension=0, tiled=True),
    )
    return (
        output[None],
        input_grad[None],
        summed[0],
        summed[1],
        summed[2],
        summed[3],
        summed[4],
        summed[5],
        summed[10],
        summed[11],
        summed[6],
        summed[7],
        summed[8],
        summed[9],
    )


def solution(mesh):
    return jax.shard_map(
        shards,
        mesh=mesh,
        in_specs=(
            P("batch", "seq", None),
            P("batch", "seq", None),
            P("batch", None),
            P("batch", None, None),
            P("batch", None, None),
            P("batch", None, None),
            P(),
            P(),
            P(),
            P(),
            P(),
            P(),
            P(),
            P(),
            P(),
            P(),
            P(),
            P(),
        ),
        out_specs=(
            P("batch", "seq", None),
            P("batch", "seq", None),
            P(("seq", "batch")),
            P(("seq", "batch")),
            P(("seq", "batch"), None),
            P(("seq", "batch"), None),
            P(("seq", "batch"), None),
            P(("seq", "batch"), None),
            P(("seq", "batch")),
            P(("seq", "batch")),
            P(("seq", "batch"), None),
            P(("seq", "batch")),
            P(("seq", "batch"), None),
            P(("seq", "batch")),
        ),
        check_vma=False,
    )
```

profile of v0, /device:TPU:0, one launch (start us, length us, event | category | flops | bytes accessed | tf_op | source)
XLA Modules:
  0.0 1663.9 jit_solution(14246572509431281664)
XLA Ops:
  51.2 57.9 %all-reduce.12.cloned.1.call-done = bf16[2,64,2048]{2,0,1:T(2,128)(2,1)} async-done(((bf16[2,64,2048]{2,0,1:T(2,128)(2,1)}), bf16[2,64,2048]{2,0,1:T(2,128)(2,1)}) %all-reduce.12.cloned.1.call-update) | async-done | bytes 524304 | tf_op jit(solution)/shard_map/psum | solution.py:174
  125.0 6.9 fusion.109
  157.4 12.7 multiply_convert_fusion.1
  170.1 8.7 convert_reduce_fusion
  191.1 6.5 multiply_reduce_fusion
  197.6 6.5 fusion.18
  218.8 10.3 reshape.519
  229.0 9.8 copy.206
  238.8 10.3 reshape.520
  249.1 9.8 copy.207
  280.4 13.0 scatter_fusion
  299.4 8.4 copy.211
  331.2 10.5 scatter-add.18
  341.7 24.1 %all-to-all-done.1 = bf16[8,2,64,2048]{3,1,2,0:T(2,128)(2,1)} async-done(((bf16[8,2,64,2048]{3,1,2,0:T(2,128)(2,1)}), bf16[8,2,64,2048]{3,1,2,0:T(2,128)(2,1)}, u32[]{:S(2)}, u32[]{:S(2)}) %all-to-all-start.1) | async-done | bytes 4194336 | tf_op jit(solution)/shard_map/all_to_all | solution.py:293
  365.8 8.6 fusion.22
  386.0 9.6 fusion.99
  396.0 9.6 fusion.61
  409.0 6.2 fusion.32
  418.0 61.4 %all-reduce.8 = (f32[1024]{0:T(1024)S(1)}, f32[1024]{0:T(1024)S(1)}, f32[1024]{0:T(1024)S(1)}, f32[1024]{0:T(1024)S(1)}, f32[4096]{0:T(1024)S(1)}, /*index=5*/f32[1024]{0:T(1024)S(1)}) all-reduce(f32[1024]{0:T(1024)S(1)} %get-tuple-element.41, ...), channel_id=2, replica_groups=mesh['seq'=8,'batch'=4] {'seq','batch'}, use_global_device_ids=true, to_apply=%region_17.19.clone | all-reduce | flops 9216 | bytes 73728
  485.1 142.4 %reduce-scatter.13.cloned.1.call-done = f32[32,1024]{1,0:T(8,128)} async-done(((f32[1024,1024]{1,0:T(8,128)}), f32[32,1024]{1,0:T(8,128)}) %reduce-scatter.13.cloned.1.call-update) | async-done | bytes 131088 | tf_op jit(solution)/shard_map/reduce_scatter | solution.py:332
  627.5 149.2 %reduce-scatter.9.cloned.1.call-done = f32[32,1024]{1,0:T(8,128)} async-done(((f32[1024,1024]{1,0:T(8,128)}), f32[32,1024]{1,0:T(8,128)}) %reduce-scatter.9.cloned.1.call-update) | async-done | bytes 131088 | tf_op jit(solution)/shard_map/reduce_scatter | solution.py:330
  776.7 148.8 %reduce-scatter.11.cloned.1.call-done = f32[32,1024]{1,0:T(8,128)} async-done(((f32[1024,1024]{1,0:T(8,128)}), f32[32,1024]{1,0:T(8,128)}) %reduce-scatter.11.cloned.1.call-update) | async-done | bytes 131088 | tf_op jit(solution)/shard_map/reduce_scatter | solution.py:331
  925.5 366.1 %reduce-scatter.15.cloned.1.call-done = f32[32,4096]{1,0:T(8,128)} async-done(((f32[1024,4096]{1,0:T(8,128)}), f32[32,4096]{1,0:T(8,128)}) %reduce-scatter.15.cloned.1.call-update) | async-done | bytes 524304 | tf_op jit(solution)/shard_map/reduce_scatter | solution.py:333
  1291.6 365.1 %reduce-scatter.17.cloned.1.call-done = f32[128,1024]{1,0:T(8,128)} async-done(((f32[4096,1024]{1,0:T(8,128)}), f32[128,1024]{1,0:T(8,128)}) %reduce-scatter.17.cloned.1.call-update) | async-done | bytes 524304 | tf_op jit(solution)/shard_map/reduce_scatter | solution.py:335
  (249 shorter events, 185.7 us)
Async XLA Ops:
  8.5 32.6 %copy-start.25 = (f32[192]{0:T(256)}, f32[192]{0:T(256)S(1)}, u32[]{:S(2)}) copy-start(f32[192]{0:T(256)S(1)} %broadcast_multiply_fusion.5) | copy-start | bytes 2308
  15.2 13.2 copy-start.11
  23.2 92.3 %all-to-all-start = ((bf16[8,2,64,2048]{3,2,1,0:T(8,128)(2,1)}), bf16[8,2,64,2048]{3,2,1,0:T(8,128)(2,1)}, u32[]{:S(2)}, u32[]{:S(2)}) async-start(bf16[8,2,64,2048]{3,2,1,0:T(8,128)(2,1)} %copy.192), calls=%async_computation | async-start | bytes 8388608 | tf_op jit(solution)/shard_map/all_to_all | solution.py:156
  28.3 80.8 %all-reduce.12.cloned.1.call-start = ((), (), s32[]{:S(2)}) async-start(), calls=%async_computation.8 | async-start | bytes 1048576 | tf_op jit(solution)/shard_map/psum | solution.py:174
  29.2 82.0 %collective-permute-start.1 = (bf16[64,2048]{1,0:T(8,128)(2,1)}, bf16[64,2048]{1,0:T(8,128)(2,1)}, u32[]{:S(2)}, u32[]{:S(2)}) collective-permute-start(bf16[64,2048]{1,0:T(8,128)(2,1)} %get-tuple-element.70), channel_id=1, source_target_pairs={{4,0},{8,4},{12,8},{16,12},{20,16},{24,20},{28,24},{5,1},{9,5},{13... | collective-permute-start | bytes 786440 | tf_op jit(solution)/shard_map/ppermute | solution.py:26
  30.4 80.7 %collective-permute-start = (bf16[64,2048]{1,0:T(8,128)(2,1)S(1)}, bf16[64,2048]{1,0:T(8,128)(2,1)}, u32[]{:S(2)}, u32[]{:S(2)}) collective-permute-start(bf16[64,2048]{1,0:T(8,128)(2,1)S(1)} %get-tuple-element.71), channel_id=1, source_target_pairs={{0,4},{4,8},{8,12},{12,16},{16,20},{20,24},{24,28},{1,5},{5,9},{9,... | collective-permute-start | bytes 786440 | tf_op jit(solution)/shard_map/ppermute | solution.py:24
  37.7 336.7 %all-reduce.14.cloned.1.call-start = ((), (), s32[]{:S(2)}) async-start(), calls=%async_computation.9 | async-start | bytes 1048576 | tf_op jit(solution)/shard_map/psum | solution.py:305
  49.9 91.5 %copy-start.8 = (bf16[3,64,16,64]{1,3,2,0:T(8,128)(2,1)}, bf16[3,64,16,64]{1,3,2,0:T(8,128)(2,1)S(1)}, u32[]{:S(2)}) copy-start(bf16[3,64,16,64]{1,3,2,0:T(8,128)(2,1)S(1)} %copy.202) | copy-start | bytes 1179652
  154.6 24.3 %slice-start = ((s8[8388608]{0:T(1024)(128)(4,1)}), s8[4194304]{0:T(1024)(128)(4,1)S(1)}, s32[]{:S(2)}) async-start(s8[8388608]{0:T(1024)(128)(4,1)} %bitcast.199), calls=%async_computation.16 | async-start | bytes 8388608
  157.1 25.4 %copy-start.28 = (f32[192]{0:T(256)}, f32[192]{0:T(256)S(1)}, u32[]{:S(2)}) copy-start(f32[192]{0:T(256)S(1)} %broadcast_multiply_fusion.4) | copy-start | bytes 2308
  157.4 25.1 %copy-start.33 = (f32[192]{0:T(256)}, f32[192]{0:T(256)S(1)}, u32[]{:S(2)}) copy-start(f32[192]{0:T(256)S(1)} %add_rsqrt_fusion) | copy-start | bytes 2308
  157.4 12.7 copy-start.22
  157.4 21.5 %slice-start.1 = ((s8[8388608]{0:T(1024)(128)(4,1)}), s8[4194304]{0:T(1024)(128)(4,1)S(1)}, s32[]{:S(2)}) async-start(s8[8388608]{0:T(1024)(128)(4,1)} %bitcast.199), calls=%async_computation.17 | async-start | bytes 8388608
  262.8 222.4 %reduce-scatter.7.cloned.1.call-start = ((), (), s32[]{:S(2)}) async-start(), calls=%async_computation.10 | async-start | bytes 4325376 | tf_op jit(solution)/shard_map/reduce_scatter | solution.py:329
  266.8 360.8 %reduce-scatter.13.cloned.1.call-start = ((), (), s32[]{:S(2)}) async-start(), calls=%async_computation.13 | async-start | bytes 4325376 | tf_op jit(solution)/shard_map/reduce_scatter | solution.py:332
  307.9 57.9 %all-to-all-start.1 = ((bf16[8,2,64,2048]{3,1,2,0:T(2,128)(2,1)}), bf16[8,2,64,2048]{3,1,2,0:T(2,128)(2,1)}, u32[]{:S(2)}, u32[]{:S(2)}) async-start(bf16[8,2,64,2048]{3,1,2,0:T(2,128)(2,1)} %copy.211), calls=%async_computation.1 | async-start | bytes 8388608 | tf_op jit(solution)/shard_map/all_to_all | solution.py:293
  312.5 464.3 %reduce-scatter.9.cloned.1.call-start = ((), (), s32[]{:S(2)}) async-start(), calls=%async_computation.11 | async-start | bytes 4325376 | tf_op jit(solution)/shard_map/reduce_scatter | solution.py:330
  318.0 7.1 collective-permute-start.2
  320.9 4.2 collective-permute-start.3
  341.7 32.7 %copy-start.49 = (s32[2]{0:T(128)S(1)}, s32[2]{0:T(128)}, u32[]{:S(2)}) copy-start(s32[2]{0:T(128)} %copy-done.48) | copy-start | bytes 28
  381.6 543.9 %reduce-scatter.11.cloned.1.call-start = ((), (), s32[]{:S(2)}) async-start(), calls=%async_computation.12 | async-start | bytes 4325376 | tf_op jit(solution)/shard_map/reduce_scatter | solution.py:331
  385.4 906.1 %reduce-scatter.15.cloned.1.call-start = ((), (), s32[]{:S(2)}) async-start(), calls=%async_computation.14 | async-start | bytes 17301504 | tf_op jit(solution)/shard_map/reduce_scatter | solution.py:333
  395.7 1260.9 %reduce-scatter.17.cloned.1.call-start = ((), (), s32[]{:S(2)}) async-start(), calls=%async_computation.15 | async-start | bytes 17301504 | tf_op jit(solution)/shard_map/reduce_scatter | solution.py:335
  416.0 66.9 %copy-start.6 = (f32[192,1024]{1,0:T(8,128)S(1)}, f32[192,1024]{1,0:T(8,128)}, u32[]{:S(2)}) copy-start(f32[192,1024]{1,0:T(8,128)} %copy-done.5) | copy-start | bytes 2359300
  (42 other events, 174.7 us)
Sparse Core Ops, SparseCore 0:
  37.8 71.2 all-reduce.11
  262.9 53.8 all-reduce.13
  319.7 157.9 reduce-scatter.6
  480.4 147.0 reduce-scatter.12
  630.2 146.4 reduce-scatter.8
  779.4 146.0 reduce-scatter.10
  928.4 363.1 reduce-scatter.14
  1294.4 362.1 reduce-scatter.16
where the time goes:
time: 1670 us; the launch traced here: 1660 us
  waiting for transfers between devices  1250 us (75%)
  local copies, waits for them, and re-layouts  135 us (8%)
  matrix products  120 us (7%)
  blocking collectives  61.4 us (4%)
  other arithmetic  58.3 us (3%)
  starting transfers between devices  19.5 us (1%)
    reduce_scatter x1, waiting for transfers between devices, shards(): lax.psum_scatter(grad_w_in, ('seq', 'batch'), scatter_dimension=0, tiled=...  366 us
    reduce_scatter x1, waiting for transfers between devices, shards(): lax.psum_scatter(grad_w_back, ('seq', 'batch'), scatter_dimension=0, tile...  365 us
    reduce_scatter x1, waiting for transfers between devices, shards(): lax.psum_scatter(grad_w_key, ('seq', 'batch'), scatter_dimension=0, tiled...  149 us
    reduce_scatter x1, waiting for transfers between devices, shards(): lax.psum_scatter(grad_w_value, ('seq', 'batch'), scatter_dimension=0, til...  149 us
    reduce_scatter x1, waiting for transfers between devices, shards(): lax.psum_scatter(grad_w_out, ('seq', 'batch'), scatter_dimension=0, tiled...  142 us
    unnamed x1, blocking collectives  61.4 us
    psum x1, waiting for transfers between devices, shards(): lax.psum(packed_terms.astype(jnp.bfloat16), 'seq').astype(jnp.float32)  57.9 us
    concatenate x4, local copies, waits for them, and re-layouts, shards(): jnp.concatenate([grad_key_heads.reshape(block_count, key_count, model_wid...  40.1 us
  transfers between devices with their start and end apart: 14, of which 7 were waited for; matrix products, arithmetic and copies ran while one was open for 9% of the time, Pallas kernels for 0%

commit v1 on v0

v1 whole, which is shorter than its diff:
```python
import functools

import jax
import jax.numpy as jnp
from jax import lax
from jax.experimental import pallas as pl
from jax.experimental.pallas import tpu as pltpu
from jax.sharding import PartitionSpec as P

HEADS = 16
BLK = 64
RAND = 3

norm_eps = 1e-05
masked_score = -1e30
low = jnp.bfloat16
full = jnp.float32


def matmul(left, right):
    return jnp.dot(left, right, preferred_element_type=full)


def matmul_left(left, right):
    return lax.dot_general(left, right, (((0,), (0,)), ((), ())), preferred_element_type=full)


def matmul_right(left, right):
    return lax.dot_general(left, right, (((1,), (1,)), ((), ())), preferred_element_type=full)


def normalize(values, ln_gain, ln_shift):
    average = jnp.mean(values, axis=-1, keepdims=True)
    centered = values - average
    variance = jnp.mean(centered * centered, axis=-1, keepdims=True)
    inverse = lax.rsqrt(variance + norm_eps)
    scaled = centered * inverse
    return (scaled * ln_gain + ln_shift, scaled, inverse)


def normalize_back(grad_normed, scaled, inverse, ln_gain):
    grad_scaled = grad_normed * ln_gain
    inner_mean = jnp.mean(grad_scaled, axis=-1, keepdims=True)
    along_mean = jnp.mean(grad_scaled * scaled, axis=-1, keepdims=True)
    return inverse * (grad_scaled - inner_mean - scaled * along_mean)


def key_list(step, block_count, total_blocks, lens, owners, offsets, globals_):
    length = lens[0, 0]
    ids = [step - 1, step, step + 1]
    ids += [owners[0, step, r] * block_count + offsets[0, step, r] for r in range(RAND)]
    ids += [globals_[0, 0, g] for g in range(globals_.shape[2])]
    starts, limits = [], []
    for block in ids:
        inside = jnp.logical_and(block >= 0, block < total_blocks)
        clamped = jnp.clip(block, 0, total_blocks - 1)
        starts.append(pl.multiple_of(clamped * BLK, BLK))
        limits.append(jnp.where(inside, length - clamped * BLK, 0))
    return starts, limits


def stack_heads(rows, lanes, head_count):
    if head_count == 1:
        return rows
    zero = jnp.zeros_like(rows)
    return jnp.concatenate([jnp.where(lanes == h, rows, zero) for h in range(head_count)], axis=0)


def merge_heads(stacked, lanes, head_count):
    merged = stacked[:BLK]
    for h in range(1, head_count):
        merged = jnp.where(lanes == h, stacked[h * BLK : (h + 1) * BLK], merged)
    return merged


def masked_scores(keys, query_rows, limits, inner_rows):
    score_values = matmul_right(keys, query_rows)
    parts = [
        jnp.where(inner_rows < limit, score_values[j * BLK : (j + 1) * BLK], masked_score)
        for j, limit in enumerate(limits)
    ]
    return jnp.concatenate(parts, axis=0)


def attend_kernel(
    block_count, head_count, scale, unroll, lens, owners, offsets, globals_, qkv, attended, log_total
):
    total_blocks = qkv.shape[0] // BLK
    width = qkv.shape[1] // 3
    lanes = lax.broadcasted_iota(jnp.int32, (BLK, width), 1) // (width // head_count)
    inner_rows = lax.broadcasted_iota(jnp.int32, (BLK, head_count * BLK), 0)

    def one(step):
        starts, limits = key_list(step, block_count, total_blocks, lens, owners, offsets, globals_)
        row = pl.multiple_of(step * BLK, BLK)
        queries = qkv[pl.ds(row, BLK), 0:width] * jnp.asarray(scale, low)
        query_rows = stack_heads(queries, lanes, head_count)
        keys = jnp.concatenate([qkv[pl.ds(s, BLK), width : 2 * width] for s in starts], axis=0)
        values = jnp.concatenate([qkv[pl.ds(s, BLK), 2 * width :] for s in starts], axis=0)
        score_values = masked_scores(keys, query_rows, limits, inner_rows)
        top = jnp.max(score_values, axis=0, keepdims=True)
        raised = jnp.exp(score_values - top)
        total = jnp.sum(raised, axis=0, keepdims=True)
        weights = (raised * (1.0 / total)).astype(low)
        result = matmul_left(weights, values)
        attended[pl.ds(row, BLK), :] = merge_heads(result, lanes, head_count).astype(low)
        log_total[step] = top + jnp.log(total)

    def body(index, carry):
        for part in range(unroll):
            one(index * unroll + part)
        return carry

    lax.fori_loop(0, total_blocks // unroll, body, 0)


def attend_back_kernel(
    block_count,
    head_count,
    scale,
    unroll,
    lens,
    owners,
    offsets,
    globals_,
    qkv,
    log_total,
    grad_attended,
    grad_qkv,
    key_sum,
    value_sum,
):
    total_blocks = qkv.shape[0] // BLK
    width = qkv.shape[1] // 3
    lanes = lax.broadcasted_iota(jnp.int32, (BLK, width), 1) // (width // head_count)
    inner_rows = lax.broadcasted_iota(jnp.int32, (BLK, head_count * BLK), 0)
    key_sum[...] = jnp.zeros_like(key_sum)
    value_sum[...] = jnp.zeros_like(value_sum)

    def one(step):
        starts, limits = key_list(step, block_count, total_blocks, lens, owners, offsets, globals_)
        row = pl.multiple_of(step * BLK, BLK)
        queries = qkv[pl.ds(row, BLK), 0:width] * jnp.asarray(scale, low)
        query_rows = stack_heads(queries, lanes, head_count)
        grad_rows = stack_heads(grad_attended[pl.ds(row, BLK), :], lanes, head_count)
        keys = jnp.concatenate([qkv[pl.ds(s, BLK), width : 2 * width] for s in starts], axis=0)
        values = jnp.concatenate([qkv[pl.ds(s, BLK), 2 * width :] for s in starts], axis=0)
        score_values = masked_scores(keys, query_rows, limits, inner_rows)
        probs = jnp.exp(score_values - log_total[step])
        grad_probs = matmul_right(values, grad_rows)
        correction = jnp.sum(probs * grad_probs, axis=0, keepdims=True)
        grad_scores = (probs * (grad_probs - correction)).astype(low)
        grad_keys = matmul(grad_scores, query_rows)
        grad_values = matmul(probs.astype(low), grad_rows)
        grad_queries = merge_heads(matmul_left(grad_scores, keys), lanes, head_count) * scale
        grad_qkv[pl.ds(row, BLK), 0:width] = grad_queries.astype(low)
        for j, s in enumerate(starts):
            key_sum[pl.ds(s, BLK), :] += grad_keys[j * BLK : (j + 1) * BLK]
            value_sum[pl.ds(s, BLK), :] += grad_values[j * BLK : (j + 1) * BLK]

    def body(index, carry):
        for part in range(unroll):
            one(index * unroll + part)
        return carry

    lax.fori_loop(0, total_blocks // unroll, body, 0)
    grad_qkv[:, width : 2 * width] = key_sum[...].astype(low)
    grad_qkv[:, 2 * width :] = value_sum[...].astype(low)


smem = pl.BlockSpec(memory_space=pltpu.SMEM)
vmem = pl.BlockSpec(memory_space=pltpu.VMEM)


def attend(tables, qkv, block_count, head_count, scale):
    rows, width = qkv.shape[0], qkv.shape[1] // 3
    total_blocks = rows // BLK
    return pl.pallas_call(
        functools.partial(attend_kernel, block_count, head_count, scale, 3),
        out_shape=(
            jax.ShapeDtypeStruct((rows, width), low),
            jax.ShapeDtypeStruct((total_blocks, 1, head_count * BLK), full),
        ),
        in_specs=[smem] * 4 + [vmem],
        out_specs=(vmem, vmem),
        compiler_params=pltpu.CompilerParams(vmem_limit_bytes=40 * 2**20),
        cost_estimate=pl.CostEstimate(
            flops=total_blocks * 4 * 128 * 128 * 512, bytes_accessed=rows * width * 8, transcendentals=0
        ),
        name="attend",
    )(*tables, qkv)


def attend_back(tables, qkv, log_total, grad_attended, block_count, head_count, scale):
    rows, width = qkv.shape[0], qkv.shape[1] // 3
    total_blocks = rows // BLK
    return pl.pallas_call(
        functools.partial(attend_back_kernel, block_count, head_count, scale, 2),
        out_shape=jax.ShapeDtypeStruct((rows, 3 * width), low),
        in_specs=[smem] * 4 + [vmem] * 3,
        out_specs=vmem,
        scratch_shapes=[pltpu.VMEM((rows, width), full)] * 2,
        compiler_params=pltpu.CompilerParams(vmem_limit_bytes=40 * 2**20),
        cost_estimate=pl.CostEstimate(
            flops=total_blocks * 10 * 128 * 128 * 512, bytes_accessed=rows * width * 16, transcendentals=0
        ),
        name="attend_back",
    )(*tables, qkv, log_total, grad_attended)


def swap(blocks, axes):
    return lax.all_to_all(blocks, axes, split_axis=0, concat_axis=0, tiled=True)


def gather_rows(rows):
    return lax.all_gather(rows, "seq", axis=0, tiled=True)


def shards(
    inputs,
    cotangent,
    lengths,
    rand_owners,
    rand_offsets,
    global_ids,
    ln1_gain,
    ln1_shift,
    w_query,
    w_key,
    w_value,
    w_out,
    ln2_gain,
    ln2_shift,
    w_in,
    b_in,
    w_back,
    b_back,
):
    seq_count = lax.axis_size("seq")
    batch_count = lax.axis_size("batch")
    device_count = seq_count * batch_count
    seq_index = lax.axis_index("seq")
    token_count = inputs.shape[1]
    model_width = inputs.shape[2]
    ff_width = w_in.shape[1]
    block_count = token_count // BLK
    head_dim = model_width // HEADS
    scale = head_dim ** (-0.5)
    total_tokens = seq_count * token_count
    head_groups = min(HEADS, seq_count)
    copies = seq_count // head_groups
    head_count = HEADS // head_groups
    width = head_count * head_dim
    tables = (lengths, rand_owners, rand_offsets, global_ids)

    def to_heads(*parts):
        split = [p.reshape(token_count, head_groups, width).transpose(1, 0, 2) for p in parts]
        joined = jnp.concatenate(split, axis=2)
        if copies > 1:
            joined = jnp.repeat(joined, copies, axis=0)
        received = swap(joined, "seq")
        return received.reshape(total_tokens, len(parts) * width)

    def to_tokens(rows, count):
        received = swap(rows.reshape(seq_count, token_count, count * width), "seq")
        received = received[::copies]
        return [
            received[:, :, i * width : (i + 1) * width].transpose(1, 0, 2).reshape(token_count, model_width)
            for i in range(count)
        ]

    gain_one = ln1_gain.astype(full)
    gain_two = ln2_gain.astype(full)
    grad_out = cotangent[0]
    grad_out_all = gather_rows(grad_out)
    residual_in = inputs[0].astype(full)
    normed, scaled_one, inverse_one = normalize(residual_in, gain_one, ln1_shift.astype(full))
    normed_low = normed.astype(low)
    normed_all = gather_rows(normed_low)
    qkv = to_heads(
        matmul(normed_low, w_query).astype(low),
        matmul(normed_low, w_key).astype(low),
        matmul(normed_low, w_value).astype(low),
    )
    attended_all, log_total = attend(tables, qkv, block_count, head_count, scale)
    (attended,) = to_tokens(attended_all, 1)
    middle = residual_in + matmul(attended, w_out)
    normed_two, scaled_two, inverse_two = normalize(middle, gain_two, ln2_shift.astype(full))
    normed_two_low = normed_two.astype(low)
    normed_two_all = gather_rows(normed_two_low)
    inner = matmul(normed_two_low, w_in) + b_in.astype(full)
    gelu = functools.partial(jax.nn.gelu, approximate=False)
    activated, gelu_pull = jax.vjp(gelu, inner)
    activated = activated.astype(low)
    output = (middle + matmul(activated, w_back) + b_back.astype(full)).astype(low)

    def to_columns(rows):
        columns = rows.shape[1] // seq_count
        split = rows.reshape(token_count, seq_count, columns).transpose(1, 0, 2)
        return swap(split, "seq").reshape(total_tokens, columns)

    activated_all = to_columns(activated)
    grad_w_back = matmul_left(activated_all, grad_out_all).astype(low)
    grad_out_full = grad_out.astype(full)
    grad_b_back = jnp.sum(grad_out_full, axis=0)
    grad_inner = gelu_pull(matmul_right(grad_out, w_back))[0].astype(low)
    grad_inner_all = to_columns(grad_inner)
    grad_w_in = matmul_left(normed_two_all, grad_inner_all).astype(low)
    grad_b_in = jnp.sum(grad_inner.astype(full), axis=0)
    grad_normed_two = matmul_right(grad_inner, w_in)
    grad_ln2_gain = jnp.sum(grad_normed_two * scaled_two, axis=0)
    grad_ln2_shift = jnp.sum(grad_normed_two, axis=0)
    grad_middle = grad_out_full + normalize_back(grad_normed_two, scaled_two, inverse_two, gain_two)
    grad_middle_low = grad_middle.astype(low)
    grad_attended = matmul_right(grad_middle_low, w_out).astype(low)
    grad_middle_all = gather_rows(grad_middle_low)
    out_rows = width // copies
    own_attended = lax.dynamic_slice_in_dim(attended_all, seq_index % copies * out_rows, out_rows, axis=1)
    grad_w_out = matmul_left(own_attended, grad_middle_all).astype(low)
    grad_qkv = attend_back(
        tables, qkv, log_total, to_heads(grad_attended), block_count, head_count, scale
    )
    grad_queries, grad_keys, grad_values = to_tokens(grad_qkv, 3)
    grad_w_qkv = matmul_left(normed_all, grad_qkv).astype(low)
    grad_normed = (
        matmul_right(grad_queries, w_query)
        + matmul_right(grad_keys, w_key)
        + matmul_right(grad_values, w_value)
    )
    grad_ln1_gain = jnp.sum(grad_normed * scaled_one, axis=0)
    grad_ln1_shift = jnp.sum(grad_normed, axis=0)
    input_grad = (
        grad_middle + normalize_back(grad_normed, scaled_one, inverse_one, gain_one)
    ).astype(low)

    both = ("seq", "batch")
    slim = model_width // device_count

    def rows_of(columns, count):
        received = swap(columns.reshape(device_count, slim, columns.shape[1]), both)
        received = received.reshape(seq_count, batch_count, slim, columns.shape[1])
        summed = jnp.sum(received[::count].astype(full), axis=1)
        return summed.transpose(1, 0, 2)

    in_rows = rows_of(grad_w_in, 1).reshape(slim, ff_width)
    qkv_rows = rows_of(grad_w_qkv, copies)
    qkv_rows = [
        qkv_rows[:, :, i * width : (i + 1) * width].reshape(slim, model_width) for i in range(3)
    ]
    back_out = lax.psum_scatter(
        jnp.concatenate(
            [
                grad_w_back.reshape(batch_count, -1, model_width),
                grad_w_out.reshape(batch_count, -1, model_width),
            ],
            axis=1,
        ),
        "batch",
        scatter_dimension=0,
        tiled=False,
    ).astype(full)
    back_rows = ff_width // device_count
    small = [grad_ln1_gain, grad_ln1_shift, grad_ln2_gain, grad_ln2_shift, grad_b_back, grad_b_in]
    packed = jnp.concatenate([v.reshape(device_count, -1) for v in small], axis=1)
    packed = jnp.sum(swap(packed, both), axis=0)
    cuts, at = [], 0
    for v in small:
        size = v.shape[0] // device_count
        cuts.append(packed[at : at + size])
        at += size
    return (
        output[None],
        input_grad[None],
        cuts[0],
        cuts[1],
        qkv_rows[0],
        qkv_rows[1],
        qkv_rows[2],
        back_out[back_rows:],
        cuts[2],
        cuts[3],
        in_rows,
        cuts[5],
        back_out[:back_rows],
        cuts[4],
    )


def solution(mesh):
    rows = P("batch", "seq", None)
    table = P("batch", None, None)
    thin = P(("seq", "batch"))
    wide = P(("seq", "batch"), None)
    return jax.shard_map(
        shards,
        mesh=mesh,
        in_specs=(rows, rows, P("batch", None), table, table, table) + (P(),) * 12,
        out_specs=(rows, rows, thin, thin, wide, wide, wide, wide, thin, thin, wide, thin, wide, thin),
        check_vma=False,
    )
```

time: 1670 us -> 303 us (0.18)
  waiting for transfers between devices: 1250 us -> 129 us
  local copies, waits for them, and re-layouts: 135 us -> 15.3 us
  blocking collectives: 61.4 us -> 0 us
  matrix products: 120 us -> 63.6 us
  other arithmetic: 58.3 us -> 15.8 us
  starting transfers between devices: 19.5 us -> 41.3 us
  Pallas kernels: 0 us -> 21.2 us
    reduce_scatter x6 -> x1, waiting for transfers between devices: 1170 us -> 0.01 us  [shards(): lax.psum_scatter(jnp.concatenate([grad_w_back.reshape(batch_count, -1, mo...]
    all_to_all x2 -> x9, waiting for transfers between devices: 24.1 us -> 128 us  [swap(): return lax.all_to_all(blocks, axes, split_axis=0, concat_axis=0, tiled=True)]
    unnamed x1 -> x0, blocking collectives: 61.4 us -> none
    psum x2 -> x0, waiting for transfers between devices: 57.9 us -> none  [the longest x1 57.9 us: shards(): lax.psum(packed_terms.astype(jnp.bfloat16), 'seq').astype(jnp.float32)]
    concatenate x7 -> x1, local copies, waits for them, and re-layouts: 42.5 us -> 0.09 us  [shards(): jnp.concatenate([v.reshape(device_count, -1) for v in small], axis=1)]
    dot_general x17 -> x6, matrix products: 66.9 us -> 24.5 us  [matmul(): return jnp.dot(left, right, preferred_element_type=full)]
    all_to_all x2 -> x9, starting transfers between devices: 9.76 us -> 40.7 us  [swap(): return lax.all_to_all(blocks, axes, split_axis=0, concat_axis=0, tiled=True)]
    convert_element_type x8 -> x0, local copies, waits for them, and re-layouts: 22.8 us -> none  [the longest x1 8.45 us: shards(): slot_grads.reshape(seq_count, slot_count, BLK, double_width)]
  transfers between devices with their start and end apart: 14 -> 14, of which waited for: 7 -> 9; matrix products, arithmetic and copies ran while one was open for 9% -> 28% of each run, Pallas kernels for 0% -> 7%
where the time goes in v1:
time: 303 us; the launch traced here: 302 us
  waiting for transfers between devices  129 us (43%)
  matrix products  63.6 us (21%)
  starting transfers between devices  41.3 us (14%)
  Pallas kernels  21.2 us (7%)
  other arithmetic  15.8 us (5%)
  local copies, waits for them, and re-layouts  15.3 us (5%)
  between operations  15 us (5%)
    all_to_all x9, waiting for transfers between devices, swap(): return lax.all_to_all(blocks, axes, split_axis=0, concat_axis=0, tiled=True)  128 us
    all_to_all x9, starting transfers between devices, swap(): return lax.all_to_all(blocks, axes, split_axis=0, concat_axis=0, tiled=True)  40.7 us
    dot_general x6, matrix products, matmul(): return jnp.dot(left, right, preferred_element_type=full)  24.5 us
    dot_general x6, matrix products, matmul_right(): lax.dot_general(left, right, (((1,), (1,)), ((), ())), preferred_element_...  22.5 us
    dot_general x4, matrix products, matmul_left(): lax.dot_general(left, right, (((0,), (0,)), ((), ())), preferred_element_...  16.6 us
    pallas_call x1, Pallas kernels, attend_back(): pl.pallas_call(functools.partial(attend_back_kernel, block_count, head_co...  11.2 us
    pallas_call x1, Pallas kernels, attend(): pl.pallas_call(functools.partial(attend_kernel, block_count, head_count,...  10 us
  transfers between devices with their start and end apart: 14, of which 9 were waited for; matrix products, arithmetic and copies ran while one was open for 28% of the time, Pallas kernels for 7%

profile of v1, /device:TPU:0, one launch (start us, length us, event | category | flops | bytes accessed | tf_op | source)
XLA Modules:
  0.0 301.6 jit_solution(4767935011272981606)
XLA Ops:
  18.3 5.3 %all-to-all-start = ((bf16[8,192,384]{2,1,0:T(8,128)(2,1)}), bf16[8,192,384]{2,1,0:T(8,128)(2,1)S(1)}, u32[]{:S(2)}, u32[]{:S(2)}) async-start(bf16[8,192,384]{2,1,0:T(8,128)(2,1)} %pad_maximum_fusion.1), calls=%async_computation | async-start | bytes 2359296 | tf_op jit(solution)/shard_map/all_to_all | solution.py:212
  24.5 19.4 %all-to-all-done = bf16[8,192,384]{2,1,0:T(8,128)(2,1)S(1)} async-done(((bf16[8,192,384]{2,1,0:T(8,128)(2,1)}), bf16[8,192,384]{2,1,0:T(8,128)(2,1)S(1)}, u32[]{:S(2)}, u32[]{:S(2)}) %all-to-all-start) | async-done | bytes 1179680 | tf_op jit(solution)/shard_map/all_to_all | solution.py:212
  43.9 10.0 %attend.1 = (bf16[1536,128]{1,0:T(8,128)(2,1)}, f32[24,1,128]{2,1,0:T(1,128)S(1)}) custom-call(s32[1,1]{1,0:T(1,128)S(6)} %copy.134.lens, s32[1,24,3]{2,1,0:T(8,128)S(1)} %copy.69.owners, s32[1,24,3]{2,1,0:T(8,128)S(1)} %copy.70.offsets, s32[1,1,2]{2,1,0:T(1,128)S(1)} %copy-done.3, bf16[1536,384]{1,0:T(8,128)(2,1)S(1)} %bitcast.195), custom_call_target="tpu_custom_call" | custom-call | flops 805306368 | bytes 1572864 | tf_op jit(solution)/shard_map/attend/pallas_call | solution.py:178
  54.0 4.1 %all-to-all-start.1 = ((bf16[8,192,128]{2,1,0:T(8,128)(2,1)}), bf16[8,192,128]{2,1,0:T(8,128)(2,1)}, u32[]{:S(2)}, u32[]{:S(2)}) async-start(bf16[8,192,128]{2,1,0:T(8,128)(2,1)} %bitcast.5), calls=%async_computation.1 | async-start | bytes 786432 | tf_op jit(solution)/shard_map/all_to_all | solution.py:212
  59.1 7.3 %all-to-all-done.1 = bf16[8,192,128]{2,1,0:T(8,128)(2,1)} async-done(((bf16[8,192,128]{2,1,0:T(8,128)(2,1)}), bf16[8,192,128]{2,1,0:T(8,128)(2,1)}, u32[]{:S(2)}, u32[]{:S(2)}) %all-to-all-start.1) | async-done | bytes 393248 | tf_op jit(solution)/shard_map/all_to_all | solution.py:212
  70.7 11.9 %multiply_convert_fusion = (bf16[192,4096]{1,0:T(8,128)(2,1)}, f32[192,4096]{1,0:T(8,128)S(1)}, f32[192,4096]{1,0:T(8,128)S(1)}) fusion(f32[4096]{0:T(1024)S(1)} %convert_element_type.102, bf16[192,1024]{1,0:T(8,128)(2,1)} %add_convert_fusion.1, bf16[1024,4096]{1,0:T(8,128)(2,1)} %param.32), kind=kOutput, calls=%fused_computation.7 | convolution fusion | flops 1662517248 | bytes 16662528 | tf_op jit(solution)/shard_map/dot_general | solution.py:21
  82.6 7.4 %convert_reduce_fusion = (f32[4096]{0:T(1024)S(1)}, bf16[192,4096]{1,0:T(8,128)(2,1)S(1)}) fusion(f32[192,4096]{1,0:T(8,128)S(1)} %get-tuple-element.29, f32[192,4096]{1,0:T(8,128)S(1)} %get-tuple-element.44, bf16[4096,1024]{1,0:T(8,128)(2,1)} %param.34, bf16[1,192,1024]{2,1,0:T(8,128)(2,1)S(1)} %copy-done.14), kind=kOutput, calls=%fused_computation.5 | convolution fusion | flops 1623191552 | bytes 16662528 | tf_op jit(solution)/shard_map/dot_general | solution.py:29
  90.0 7.2 %multiply_reduce_fusion = (f32[1024]{0:T(1024)S(1)}, f32[192]{0:T(256)S(1)}, f32[192]{0:T(256)S(1)}, f32[1024]{0:T(1024)S(1)}, f32[192,1024]{1,0:T(8,128)S(1)}) fusion(f32[192,1024]{1,0:T(8,128)S(1)} %copy-done.5, f32[192]{0:T(256)S(1)} %add_rsqrt_fusion, f32[192]{0:T(256)S(1)} %broadcast_multiply_fusion.4, f32[1024]{0:T(1024)S(1)} %convert_element_type.99, ...), kind=kOutput, calls=%fused_computation.66 | convolution fusion | flops 1612379648 | bytes 11549696 | tf_op jit(solution)/shard_map/dot_general | solution.py:29
  102.1 4.1 %all-to-all-start.2 = ((bf16[8,192,128]{2,1,0:T(8,128)(2,1)}), bf16[8,192,128]{2,1,0:T(8,128)(2,1)}, u32[]{:S(2)}, u32[]{:S(2)}) async-start(bf16[8,192,128]{2,1,0:T(8,128)(2,1)} %bitcast.203), calls=%async_computation.2 | async-start | bytes 786432 | tf_op jit(solution)/shard_map/all_to_all | solution.py:212
  106.8 11.5 %all-to-all-done.2 = bf16[8,192,128]{2,1,0:T(8,128)(2,1)} async-done(((bf16[8,192,128]{2,1,0:T(8,128)(2,1)}), bf16[8,192,128]{2,1,0:T(8,128)(2,1)}, u32[]{:S(2)}, u32[]{:S(2)}) %all-to-all-start.2) | async-done | bytes 393248 | tf_op jit(solution)/shard_map/all_to_all | solution.py:212
  118.3 11.2 %attend_back.1 = bf16[1536,384]{1,0:T(8,128)(2,1)S(1)} custom-call(s32[1,1]{1,0:T(1,128)S(6)} %copy.134.lens, s32[1,24,3]{2,1,0:T(8,128)S(1)} %copy.69.owners, s32[1,24,3]{2,1,0:T(8,128)S(1)} %copy.70.offsets, s32[1,1,2]{2,1,0:T(1,128)S(1)} %copy-done.3, bf16[1536,384]{1,0:T(8,128)(2,1)S(1)} %bitcast.196, f32[24,1,128]{2,1,0:T(1,128)S(1)} %get-tuple-element.17.log_total, ...), custom_call_target="tpu_custom_call" | custom-call | flops 2013265920 | bytes 3145728 | tf_op jit(solution)/shard_map/attend_back/pallas_call | solution.py:197
  136.8 16.5 %all-to-all-done.3 = bf16[8,192,384]{2,1,0:T(8,128)(2,1)S(1)} async-done(((bf16[8,192,384]{2,1,0:T(8,128)(2,1)}), bf16[8,192,384]{2,1,0:T(8,128)(2,1)S(1)}, u32[]{:S(2)}, u32[]{:S(2)}) %all-to-all-start.3) | async-done | bytes 1179680 | tf_op jit(solution)/shard_map/all_to_all | solution.py:212
  153.3 4.3 %all-to-all-start.6 = ((bf16[8,192,512]{2,1,0:T(8,128)(2,1)}), bf16[8,192,512]{2,1,0:T(8,128)(2,1)}, u32[]{:S(2)}, u32[]{:S(2)}) async-start(bf16[8,192,512]{2,1,0:T(8,128)(2,1)} %bitcast.199), calls=%async_computation.6 | async-start | bytes 3145728 | tf_op jit(solution)/shard_map/all_to_all | solution.py:212
  160.3 26.7 %all-to-all-done.6 = bf16[8,192,512]{2,1,0:T(8,128)(2,1)} async-done(((bf16[8,192,512]{2,1,0:T(8,128)(2,1)}), bf16[8,192,512]{2,1,0:T(8,128)(2,1)}, u32[]{:S(2)}, u32[]{:S(2)}) %all-to-all-start.6) | async-done | bytes 1572896 | tf_op jit(solution)/shard_map/all_to_all | solution.py:212
  187.0 4.3 %all-to-all-start.7 = ((bf16[8,192,512]{2,1,0:T(8,128)(2,1)}), bf16[8,192,512]{2,1,0:T(8,128)(2,1)}, u32[]{:S(2)}, u32[]{:S(2)}) async-start(bf16[8,192,512]{2,1,0:T(8,128)(2,1)} %bitcast.198), calls=%async_computation.8 | async-start | bytes 3145728 | tf_op jit(solution)/shard_map/all_to_all | solution.py:212
  198.1 14.3 %all-to-all-done.7 = bf16[8,192,512]{2,1,0:T(8,128)(2,1)} async-done(((bf16[8,192,512]{2,1,0:T(8,128)(2,1)}), bf16[8,192,512]{2,1,0:T(8,128)(2,1)}, u32[]{:S(2)}, u32[]{:S(2)}) %all-to-all-start.7) | async-done | bytes 1572896 | tf_op jit(solution)/shard_map/all_to_all | solution.py:212
  212.4 3.7 %all-to-all-start.4 = ((f32[32,1,288]{2,1,0:T(1,128)}), f32[32,1,288]{2,1,0:T(1,128)S(1)}, u32[]{:S(2)}, u32[]{:S(2)}) async-start(f32[32,1,288]{2,1,0:T(1,128)} %all_to_all.34), calls=%async_computation.4 | async-start | bytes 98304 | tf_op jit(solution)/shard_map/all_to_all | solution.py:212
  216.2 4.6 %convolution_convert_fusion.1 = bf16[1024,384]{1,0:T(8,128)(2,1)} fusion(bf16[1536,1024]{1,0:T(8,128)(2,1)} %all-gather.6.cloned.1.call-done, bf16[1536,384]{1,0:T(8,128)(2,1)S(1)} %copy-done.2), kind=kOutput, calls=%fused_computation.27 | convolution fusion | flops 1208352768 | bytes 5111808 | tf_op jit(solution)/shard_map/dot_general | solution.py:25
  227.0 4.2 %fusion.8 = bf16[512,1024]{1,0:T(8,128)(2,1)S(1)} fusion(bf16[1536,512]{1,0:T(8,128)(2,1)} %bitcast.21, bf16[1,1536,1024]{2,1,0:T(8,128)(2,1)} %all-gather.12.cloned.1.call-done), kind=kOutput, calls=%fused_computation.25 | convolution fusion | flops 1611137024 | bytes 5767168 | tf_op jit(solution)/shard_map/dot_general | solution.py:25
  235.1 5.2 %convolution_convert_fusion = bf16[1024,512]{1,0:T(8,128)(2,1)} fusion(bf16[1536,1024]{1,0:T(8,128)(2,1)} %all-gather.10.cloned.1.call-done, bf16[1536,512]{1,0:T(8,128)(2,1)} %bitcast.27), kind=kOutput, calls=%fused_computation.26 | convolution fusion | flops 1611137024 | bytes 5767168 | tf_op jit(solution)/shard_map/dot_general | solution.py:25
  240.3 8.9 %all-to-all-done.5 = bf16[32,32,384]{2,1,0:T(8,128)(2,1)} async-done(((bf16[32,32,384]{2,1,0:T(8,128)(2,1)}), bf16[32,32,384]{2,1,0:T(8,128)(2,1)}, u32[]{:S(2)}, u32[]{:S(2)}) %all-to-all-start.5) | async-done | bytes 786464 | tf_op jit(solution)/shard_map/all_to_all | solution.py:212
  249.2 8.0 %all-to-all-start.8 = ((bf16[32,32,512]{2,1,0:T(8,128)(2,1)}), bf16[32,32,512]{2,1,0:T(8,128)(2,1)}, u32[]{:S(2)}, u32[]{:S(2)}) async-start(bf16[32,32,512]{2,1,0:T(8,128)(2,1)} %bitcast.206), calls=%async_computation.9 | async-start | bytes 2097152 | tf_op jit(solution)/shard_map/all_to_all | solution.py:212
  257.3 6.6 %fusion.17 = bf16[1,192,1024]{2,1,0:T(8,128)(2,1)} fusion(f32[192,1024]{1,0:T(8,128)S(1)} %copy-done.6, bf16[192,4096]{1,0:T(8,128)(2,1)} %get-tuple-element.28, bf16[4096,1024]{1,0:T(8,128)(2,1)} %param.34, f32[1024]{0:T(1024)S(1)} %convert_element_type.104), kind=kOutput, calls=%fused_computation.44 | convolution fusion | flops 1611202560 | bytes 11145216 | tf_op jit(solution)/shard_map/dot_general | solution.py:21
  269.5 20.8 %all-to-all-done.8 = bf16[32,32,512]{2,1,0:T(8,128)(2,1)} async-done(((bf16[32,32,512]{2,1,0:T(8,128)(2,1)}), bf16[32,32,512]{2,1,0:T(8,128)(2,1)}, u32[]{:S(2)}, u32[]{:S(2)}) %all-to-all-start.8) | async-done | bytes 1048608 | tf_op jit(solution)/shard_map/all_to_all | solution.py:212
  (122 shorter events, 59.1 us)
Async XLA Ops:
  7.2 8.5 %copy-start = (bf16[1024,1024]{1,0:T(8,128)(2,1)S(1)}, bf16[1024,1024]{1,0:T(8,128)(2,1)}, u32[]{:S(2)}) copy-start(bf16[1024,1024]{1,0:T(8,128)(2,1)} %param.28) | copy-start | bytes 6291460
  7.2 208.9 %all-gather.6.cloned.1.call-start = ((), (), s32[]{:S(2)}) async-start(), calls=%async_computation.10 | async-start | bytes 3538944 | tf_op jit(solution)/shard_map/all_gather | solution.py:216
  16.9 7.5 %copy-start.21 = (s32[1,24,3]{1,0,2:T(1,128)S(1)}, s32[1,24,3]{1,0,2:T(1,128)}, u32[]{:S(2)}) copy-start(s32[1,24,3]{1,0,2:T(1,128)} %param.22) | copy-start | bytes 868
  16.9 27.0 %copy-start.3 = (s32[1,1,2]{2,1,0:T(1,128)S(1)}, s32[1,1,2]{2,1,0:T(1,128)}, u32[]{:S(2)}) copy-start(s32[1,1,2]{2,1,0:T(1,128)} %globals_.3) | copy-start | bytes 28
  18.3 40.7 %copy-start.16 = (bf16[4096]{0:T(1024)(128)(2,1)S(1)}, bf16[4096]{0:T(1024)(128)(2,1)}, u32[]{:S(2)}) copy-start(bf16[4096]{0:T(1024)(128)(2,1)} %param.33) | copy-start | bytes 24580
  18.3 40.7 %copy-start.17 = (bf16[1024]{0:T(1024)(128)(2,1)S(1)}, bf16[1024]{0:T(1024)(128)(2,1)}, u32[]{:S(2)}) copy-start(bf16[1024]{0:T(1024)(128)(2,1)} %param.31) | copy-start | bytes 6148
  18.3 40.8 %copy-start.18 = (bf16[1024]{0:T(1024)(128)(2,1)S(1)}, bf16[1024]{0:T(1024)(128)(2,1)}, u32[]{:S(2)}) copy-start(bf16[1024]{0:T(1024)(128)(2,1)} %param.30) | copy-start | bytes 6148
  18.3 25.6 %all-to-all-start = ((bf16[8,192,384]{2,1,0:T(8,128)(2,1)}), bf16[8,192,384]{2,1,0:T(8,128)(2,1)S(1)}, u32[]{:S(2)}, u32[]{:S(2)}) async-start(bf16[8,192,384]{2,1,0:T(8,128)(2,1)} %pad_maximum_fusion.1), calls=%async_computation | async-start | bytes 2359296 | tf_op jit(solution)/shard_map/all_to_all | solution.py:212
  54.0 12.5 %all-to-all-start.1 = ((bf16[8,192,128]{2,1,0:T(8,128)(2,1)}), bf16[8,192,128]{2,1,0:T(8,128)(2,1)}, u32[]{:S(2)}, u32[]{:S(2)}) async-start(bf16[8,192,128]{2,1,0:T(8,128)(2,1)} %bitcast.5), calls=%async_computation.1 | async-start | bytes 786432 | tf_op jit(solution)/shard_map/all_to_all | solution.py:212
  58.1 168.9 %all-gather.12.cloned.1.call-start = ((), (), s32[]{:S(2)}) async-start(), calls=%async_computation.14 | async-start | bytes 3538944 | tf_op jit(solution)/shard_map/all_gather | solution.py:216
  58.8 172.3 %all-gather.8.cloned.1.call-start = ((), (), s32[]{:S(2)}) async-start(), calls=%async_computation.11 | async-start | bytes 3538944 | tf_op jit(solution)/shard_map/all_gather | solution.py:216
  70.7 11.9 %copy-start.14 = (bf16[1,192,1024]{2,1,0:T(8,128)(2,1)S(1)}, bf16[1,192,1024]{2,1,0:T(8,128)(2,1)}, u32[]{:S(2)}) copy-start(bf16[1,192,1024]{2,1,0:T(8,128)(2,1)} %param.19) | copy-start | bytes 1179652
  102.1 16.2 %all-to-all-start.2 = ((bf16[8,192,128]{2,1,0:T(8,128)(2,1)}), bf16[8,192,128]{2,1,0:T(8,128)(2,1)}, u32[]{:S(2)}, u32[]{:S(2)}) async-start(bf16[8,192,128]{2,1,0:T(8,128)(2,1)} %bitcast.203), calls=%async_computation.2 | async-start | bytes 786432 | tf_op jit(solution)/shard_map/all_to_all | solution.py:212
  106.2 128.8 %all-gather.10.cloned.1.call-start = ((), (), s32[]{:S(2)}) async-start(), calls=%async_computation.13 | async-start | bytes 3538944 | tf_op jit(solution)/shard_map/all_gather | solution.py:216
  130.5 22.8 %all-to-all-start.3 = ((bf16[8,192,384]{2,1,0:T(8,128)(2,1)}), bf16[8,192,384]{2,1,0:T(8,128)(2,1)S(1)}, u32[]{:S(2)}, u32[]{:S(2)}) async-start(bf16[8,192,384]{2,1,0:T(8,128)(2,1)} %bitcast.197), calls=%async_computation.3 | async-start | bytes 2359296 | tf_op jit(solution)/shard_map/all_to_all | solution.py:212
  153.3 33.7 %all-to-all-start.6 = ((bf16[8,192,512]{2,1,0:T(8,128)(2,1)}), bf16[8,192,512]{2,1,0:T(8,128)(2,1)}, u32[]{:S(2)}, u32[]{:S(2)}) async-start(bf16[8,192,512]{2,1,0:T(8,128)(2,1)} %bitcast.199), calls=%async_computation.6 | async-start | bytes 3145728 | tf_op jit(solution)/shard_map/all_to_all | solution.py:212
  187.0 25.3 %all-to-all-start.7 = ((bf16[8,192,512]{2,1,0:T(8,128)(2,1)}), bf16[8,192,512]{2,1,0:T(8,128)(2,1)}, u32[]{:S(2)}, u32[]{:S(2)}) async-start(bf16[8,192,512]{2,1,0:T(8,128)(2,1)} %bitcast.198), calls=%async_computation.8 | async-start | bytes 3145728 | tf_op jit(solution)/shard_map/all_to_all | solution.py:212
  195.2 20.9 %copy-start.2 = (bf16[1536,384]{1,0:T(8,128)(2,1)S(1)}, bf16[1536,384]{1,0:T(8,128)(2,1)}, u32[]{:S(2)}) copy-start(bf16[1536,384]{1,0:T(8,128)(2,1)} %copy-done.1) | copy-start | bytes 3538948
  212.4 11.1 %all-to-all-start.4 = ((f32[32,1,288]{2,1,0:T(1,128)}), f32[32,1,288]{2,1,0:T(1,128)S(1)}, u32[]{:S(2)}, u32[]{:S(2)}) async-start(f32[32,1,288]{2,1,0:T(1,128)} %all_to_all.34), calls=%async_computation.4 | async-start | bytes 98304 | tf_op jit(solution)/shard_map/all_to_all | solution.py:212
  216.1 10.8 %copy-start.19 = (bf16[1024]{0:T(1024)(128)(2,1)S(1)}, bf16[1024]{0:T(1024)(128)(2,1)}, u32[]{:S(2)}) copy-start(bf16[1024]{0:T(1024)(128)(2,1)} %param.35) | copy-start | bytes 6148
  223.5 25.7 %all-to-all-start.5 = ((bf16[32,32,384]{2,1,0:T(8,128)(2,1)}), bf16[32,32,384]{2,1,0:T(8,128)(2,1)}, u32[]{:S(2)}, u32[]{:S(2)}) async-start(bf16[32,32,384]{2,1,0:T(8,128)(2,1)} %bitcast.209), calls=%async_computation.5 | async-start | bytes 1572864 | tf_op jit(solution)/shard_map/all_to_all | solution.py:212
  226.9 65.7 %reduce-scatter.2.cloned.1.call-start = ((), (), s32[]{:S(2)}) async-start(), calls=%async_computation.12 | async-start | bytes 1638400 | tf_op jit(solution)/shard_map/reduce_scatter | solution.py:350
  235.0 22.2 %copy-start.6 = (f32[192,1024]{1,0:T(8,128)S(1)}, f32[192,1024]{1,0:T(8,128)}, u32[]{:S(2)}) copy-start(f32[192,1024]{1,0:T(8,128)} %copy-done.4) | copy-start | bytes 2359300
  249.2 41.1 %all-to-all-start.8 = ((bf16[32,32,512]{2,1,0:T(8,128)(2,1)}), bf16[32,32,512]{2,1,0:T(8,128)(2,1)}, u32[]{:S(2)}, u32[]{:S(2)}) async-start(bf16[32,32,512]{2,1,0:T(8,128)(2,1)} %bitcast.206), calls=%async_computation.9 | async-start | bytes 2097152 | tf_op jit(solution)/shard_map/all_to_all | solution.py:212
  (12 other events, 55.7 us)
Sparse Core Ops, SparseCore 0:
  13.3 45.3 all-gather.5
  60.8 33.6 all-gather.11
  98.8 36.5 all-gather.7
  137.7 45.7 all-gather.9
  235.1 40.2 reduce-scatter.1

commit v2 on v1

--- a/solution.py
+++ b/solution.py
@@ -27,15 +27,6 @@
 
 def matmul_right(left, right):
     return lax.dot_general(left, right, (((1,), (1,)), ((), ())), preferred_element_type=full)
-
-
-def normalize(values, ln_gain, ln_shift):
-    average = jnp.mean(values, axis=-1, keepdims=True)
-    centered = values - average
-    variance = jnp.mean(centered * centered, axis=-1, keepdims=True)
-    inverse = lax.rsqrt(variance + norm_eps)
-    scaled = centered * inverse
-    return (scaled * ln_gain + ln_shift, scaled, inverse)
 
 
 def normalize_back(grad_normed, scaled, inverse, ln_gain):
@@ -208,12 +199,401 @@
     )(*tables, qkv, log_total, grad_attended)
 
 
+def row_stats(values):
+    average = jnp.mean(values, axis=-1, keepdims=True)
+    centered = values - average
+    variance = jnp.mean(centered * centered, axis=-1, keepdims=True)
+    inverse = lax.rsqrt(variance + norm_eps)
+    return centered * inverse, inverse
+
+
+def project_kernel(width, inputs, grad_out, gain, shift, w_query, w_key, w_value, sent, kept):
+    model = inputs.shape[1]
+
+    @pl.when(pl.program_id(0) == 0)
+    def _():
+        scaled, _ = row_stats(inputs[...].astype(full))
+        normed = scaled * gain[...].astype(full) + shift[...].astype(full)
+        kept[:, :model] = normed.astype(low)
+        kept[:, model:] = grad_out[...]
+
+    rows = kept[:, :model]
+    for part, weight in enumerate((w_query, w_key, w_value)):
+        result = matmul(rows, weight[...]).astype(low)
+        for i in range(sent.shape[0]):
+            sent[i, :, part * width : (part + 1) * width] = result[:, i * width : (i + 1) * width]
+
+
+def project(inputs, grad_out, gain, shift, w_query, w_key, w_value, groups, width):
+    tokens, model = inputs.shape
+    columns = 256
+    per_step = columns // width
+    weight = pl.BlockSpec((model, columns), lambda j: (0, j))
+    row = pl.BlockSpec((1, model), lambda j: (0, 0))
+    whole = pl.BlockSpec((tokens, model), lambda j: (0, 0))
+    return pl.pallas_call(
+        functools.partial(project_kernel, width),
+        grid=(model // columns,),
+        out_shape=(
+            jax.ShapeDtypeStruct((groups, tokens, 3 * width), low),
+            jax.ShapeDtypeStruct((tokens, 2 * model), low),
+        ),
+        in_specs=[whole, whole, row, row, weight, weight, weight],
+        out_specs=(
+            pl.BlockSpec((per_step, tokens, 3 * width), lambda j: (j, 0, 0)),
+            pl.BlockSpec((tokens, 2 * model), lambda j: (0, 0)),
+        ),
+        compiler_params=pltpu.CompilerParams(vmem_limit_bytes=58 * 2**20),
+        cost_estimate=pl.CostEstimate(
+            flops=6 * tokens * model * model, bytes_accessed=6 * model * model, transcendentals=0
+        ),
+        name="project",
+    )(inputs, grad_out, gain, shift, w_query, w_key, w_value)
+
+
+def project_back_kernel(
+    width, inputs, gain, grad_middle, received, w_query, w_key, w_value, input_grad, gain_grads, total
+):
+    step = pl.program_id(0)
+
+    @pl.when(step == 0)
+    def _():
+        total[...] = jnp.zeros_like(total)
+
+    result = total[...]
+    for part, weight in enumerate((w_query, w_key, w_value)):
+        pieces = [
+            received[i, :, part * width : (part + 1) * width] for i in range(received.shape[0])
+        ]
+        result += matmul_right(jnp.concatenate(pieces, axis=1), weight[...])
+    total[...] = result
+
+    @pl.when(step == pl.num_programs(0) - 1)
+    def _():
+        grad_normed = total[...]
+        scaled, inverse = row_stats(inputs[...].astype(full))
+        back = normalize_back(grad_normed, scaled, inverse, gain[...].astype(full))
+        input_grad[...] = (grad_middle[...] + back).astype(low)
+        gain_grads[0:1, :] = jnp.sum(grad_normed * scaled, axis=0, keepdims=True)
+        gain_grads[1:2, :] = jnp.sum(grad_normed, axis=0, keepdims=True)
+
+
+def project_back(inputs, gain, grad_middle, received, w_query, w_key, w_value):
+    tokens, model = inputs.shape
+    columns = 256
+    width = received.shape[2] // 3
+    per_step = columns // width
+    weight = pl.BlockSpec((model, columns), lambda j: (0, j))
+    row = pl.BlockSpec((1, model), lambda j: (0, 0))
+    whole = pl.BlockSpec((tokens, model), lambda j: (0, 0))
+    return pl.pallas_call(
+        functools.partial(project_back_kernel, width),
+        grid=(model // columns,),
+        out_shape=(
+            jax.ShapeDtypeStruct((tokens, model), low),
+            jax.ShapeDtypeStruct((2, model), full),
+        ),
+        in_specs=[
+            whole,
+            row,
+            whole,
+            pl.BlockSpec((per_step, tokens, 3 * width), lambda j: (j, 0, 0)),
+            weight,
+            weight,
+            weight,
+        ],
+        out_specs=(whole, pl.BlockSpec((2, model), lambda j: (0, 0))),
+        scratch_shapes=[pltpu.VMEM((tokens, model), full)],
+        compiler_params=pltpu.CompilerParams(vmem_limit_bytes=58 * 2**20),
+        cost_estimate=pl.CostEstimate(
+            flops=6 * tokens * model * model, bytes_accessed=6 * model * model, transcendentals=0
+        ),
+        name="project_back",
+    )(inputs, gain, grad_middle, received, w_query, w_key, w_value)
+
+
+def middle_kernel(received, inputs, w_out, gain, shift, middle, normed, attended):
+    attended[...] = jnp.concatenate([received[i] for i in range(received.shape[0])], axis=1)
+    rows = inputs[...].astype(full) + matmul(attended[...], w_out[...])
+    middle[...] = rows
+    unit, _ = row_stats(rows)
+    normed[...] = (unit * gain[...].astype(full) + shift[...].astype(full)).astype(low)
+
+
+def attend_out(received, inputs, w_out, gain, shift):
+    tokens, model = inputs.shape
+    return pl.pallas_call(
+        middle_kernel,
+        out_shape=(
+            jax.ShapeDtypeStruct((tokens, model), full),
+            jax.ShapeDtypeStruct((tokens, model), low),
+            jax.ShapeDtypeStruct((tokens, model), low),
+        ),
+        in_specs=[vmem] * 5,
+        out_specs=(vmem, vmem, vmem),
+        compiler_params=pltpu.CompilerParams(vmem_limit_bytes=24 * 2**20),
+        cost_estimate=pl.CostEstimate(
+            flops=2 * tokens * model * model, bytes_accessed=2 * model * model, transcendentals=0
+        ),
+        name="attend_out",
+    )(received, inputs, w_out, gain, shift)
+
+
+def hidden(normed, grad_out, w_in, b_in, w_back):
+    inner = matmul(normed, w_in) + b_in.astype(full)
+    share = 0.5 * (1.0 + lax.erf(inner * 0.7071067811865476))
+    density = jnp.exp(inner * inner * -0.5) * 0.3989422804014327
+    grad_active = matmul_right(grad_out, w_back)
+    grads = (grad_active * (share + inner * density)).astype(low)
+    return (inner * share).astype(low), grads
+
+
+def feed_kernel(
+    normed,
+    middle,
+    grad_out,
+    w_out,
+    gain,
+    b_back,
+    w_in,
+    b_in,
+    w_back,
+    output,
+    grad_middle,
+    grad_middle_low,
+    grad_attended,
+    gain_grads,
+    b_in_grad,
+    out_total,
+    grad_total,
+):
+    step = pl.program_id(0)
+    groups, _, width = grad_attended.shape
+
+    @pl.when(step == 0)
+    def _():
+        out_total[...] = middle[...] + b_back[...].astype(full)
+        grad_total[...] = jnp.zeros_like(grad_total)
+
+    active, grads = hidden(normed[...], grad_out[...], w_in[...], b_in[...], w_back[...])
+    b_in_grad[...] = jnp.sum(grads.astype(full), axis=0, keepdims=True)
+    out_total[...] += matmul(active, w_back[...])
+    grad_total[...] += matmul_right(grads, w_in[...])
+
+    @pl.when(step == pl.num_programs(0) - 1)
+    def _():
+        output[...] = out_total[...].astype(low)
+        grad_normed = grad_total[...]
+        unit, rate = row_stats(middle[...])
+        grad_full = grad_out[...].astype(full)
+        back = normalize_back(grad_normed, unit, rate, gain[...].astype(full))
+        grads_middle = grad_full + back
+        grad_middle[...] = grads_middle
+        grads_low = grads_middle.astype(low)
+        grad_middle_low[...] = grads_low
+        result = matmul_right(grads_low, w_out[...]).astype(low)
+        for i in range(groups):
+            grad_attended[i] = result[:, i * width : (i + 1) * width]
+        gain_grads[0:1, :] = jnp.sum(grad_normed * unit, axis=0, keepdims=True)
+        gain_grads[1:2, :] = jnp.sum(grad_normed, axis=0, keepdims=True)
+        gain_grads[2:3, :] = jnp.sum(grad_full, axis=0, keepdims=True)
+
+
+def feed(normed, middle, grad_out, w_out, gain, b_back, w_in, b_in, w_back, groups, width):
+    tokens, model = normed.shape
+    ff = w_in.shape[1]
+    columns = 512
+    row = pl.BlockSpec((1, model), lambda j: (0, 0))
+    whole = pl.BlockSpec((tokens, model), lambda j: (0, 0))
+    heads = pl.BlockSpec((groups, tokens, width), lambda j: (0, 0, 0))
+    return pl.pallas_call(
+        feed_kernel,
+        grid=(ff // columns,),
+        out_shape=(
+            jax.ShapeDtypeStruct((tokens, model), low),
+            jax.ShapeDtypeStruct((tokens, model), full),
+            jax.ShapeDtypeStruct((tokens, model), low),
+            jax.ShapeDtypeStruct((groups, tokens, width), low),
+            jax.ShapeDtypeStruct((3, model), full),
+            jax.ShapeDtypeStruct((1, ff), full),
+        ),
+        in_specs=[
+            whole,
+            whole,
+            whole,
+            pl.BlockSpec((model, model), lambda j: (0, 0), pipeline_mode=pl.Buffered(1)),
+            row,
+            row,
+            pl.BlockSpec((model, columns), lambda j: (0, j)),
+            pl.BlockSpec((1, columns), lambda j: (0, j)),
+            pl.BlockSpec((columns, model), lambda j: (j, 0)),
+        ],
+        out_specs=(
+            whole,
+            whole,
+            whole,
+            heads,
+            pl.BlockSpec((3, model), lambda j: (0, 0)),
+            pl.BlockSpec((1, columns), lambda j: (0, j)),
+        ),
+        scratch_shapes=[pltpu.VMEM((tokens, model), full)] * 2,
+        compiler_params=pltpu.CompilerParams(vmem_limit_bytes=48 * 2**20),
+        cost_estimate=pl.CostEstimate(
+            flops=8 * tokens * model * ff, bytes_accessed=4 * model * ff, transcendentals=0
+        ),
+        name="feed",
+    )(normed, middle, grad_out, w_out, gain, b_back, w_in, b_in, w_back)
+
+
+def pick_blocks(index, total, sent, own, other):
+    def block(distance):
+        return total[:, pl.ds(index ^ distance, 1)][:, 0].astype(low)
+
+    sent[0] = block(1)
+    sent[1] = block(3)
+    own[...] = block(0)
+    other[...] = block(2)
+
+
+def picked_shapes(outer, rows, columns):
+    shape = (outer, rows, columns)
+    return [jax.ShapeDtypeStruct((2,) + shape, low)] + [jax.ShapeDtypeStruct(shape, low)] * 2
+
+
+def picked_specs(outer, rows, columns):
+    whole = pl.BlockSpec((outer, rows, columns), lambda j, places: (0, 0, 0))
+    return [pl.BlockSpec((2, outer, rows, columns), lambda j, places: (0, 0, 0, 0)), whole, whole]
+
+
+def product_kernel(places, left, right, sent, own, other, total):
+    step = pl.program_id(0)
+
+    @pl.when(step == 0)
+    def _():
+        total[...] = jnp.zeros_like(total)
+
+    total[...] += matmul_left(left[...], right[...]).reshape(total.shape)
+
+    @pl.when(step == pl.num_programs(0) - 1)
+    def _():
+        pick_blocks(places[1], total, sent, own, other)
+
+
+def product(places, left, left_columns, right, outer, name):
+    tokens, columns = right.shape
+    chunk = min(512, tokens)
+    rows = left_columns // (4 * outer)
+    return pl.pallas_call(
+        product_kernel,
+        grid_spec=pltpu.PrefetchScalarGridSpec(
+            num_scalar_prefetch=1,
+            grid=(tokens // chunk,),
+            in_specs=[
+                pl.BlockSpec((chunk, left_columns), lambda j, places: (j, 0)),
+                pl.BlockSpec((chunk, columns), lambda j, places: (j, 0)),
+            ],
+            out_specs=picked_specs(outer, rows, columns),
+            scratch_shapes=[pltpu.VMEM((outer, 4, rows, columns), full)],
+        ),
+        out_shape=picked_shapes(outer, rows, columns),
+        compiler_params=pltpu.CompilerParams(vmem_limit_bytes=40 * 2**20),
+        cost_estimate=pl.CostEstimate(
+            flops=2 * tokens * left_columns * columns,
+            bytes_accessed=2 * tokens * (left_columns + columns),
+            transcendentals=0,
+        ),
+        name=name,
+    )(places, left, right)
+
+
+def feed_products_kernel(
+    places,
+    normed,
+    grad_out,
+    w_in,
+    b_in,
+    w_back,
+    in_sent,
+    in_own,
+    in_other,
+    back_sent,
+    back_own,
+    back_other,
+    in_total,
+    back_total,
+):
+    step = pl.program_id(0)
+
+    @pl.when(step == 0)
+    def _():
+        in_total[...] = jnp.zeros_like(in_total)
+        back_total[...] = jnp.zeros_like(back_total)
+
+    active, grads = hidden(normed[...], grad_out[...], w_in[...], b_in[...], w_back[...])
+    in_total[...] += matmul_left(normed[...], grads).reshape(in_total.shape)
+    back_total[...] += matmul_left(active, grad_out[...]).reshape(back_total.shape)
+
+    @pl.when(step == pl.num_programs(0) - 1)
+    def _():
+        pick_blocks(places[1], in_total, in_sent, in_own, in_other)
+        pick_blocks(places[1], back_total, back_sent, back_own, back_other)
+
+
+def feed_products(places, normed, kept, w_in, b_in, w_back, seq_count):
+    tokens, model = normed.shape
+    columns = w_in.shape[1] // seq_count
+    chunk = 512
+    slim = model // (4 * seq_count)
+    back_slim = columns // 4
+    return pl.pallas_call(
+        feed_products_kernel,
+        grid_spec=pltpu.PrefetchScalarGridSpec(
+            num_scalar_prefetch=1,
+            grid=(tokens // chunk,),
+            in_specs=[
+                pl.BlockSpec((chunk, model), lambda j, places: (j, 0)),
+                pl.BlockSpec((chunk, model), lambda j, places: (j, 1)),
+                pl.BlockSpec((model, columns), lambda j, places: (0, places[0])),
+                pl.BlockSpec((1, columns), lambda j, places: (0, places[0])),
+                pl.BlockSpec((columns, model), lambda j, places: (places[0], 0)),
+            ],
+            out_specs=picked_specs(seq_count, slim, columns) + picked_specs(1, back_slim, model),
+            scratch_shapes=[
+                pltpu.VMEM((seq_count, 4, slim, columns), full),
+                pltpu.VMEM((1, 4, back_slim, model), full),
+            ],
+        ),
+        out_shape=picked_shapes(seq_count, slim, columns) + picked_shapes(1, back_slim, model),
+        compiler_params=pltpu.CompilerParams(vmem_limit_bytes=48 * 2**20),
+        cost_estimate=pl.CostEstimate(
+            flops=8 * tokens * model * columns,
+            bytes_accessed=4 * tokens * model + 4 * model * columns,
+            transcendentals=0,
+        ),
+        name="feed_products",
+    )(places, normed, kept, w_in, b_in, w_back)
+
+
 def swap(blocks, axes):
     return lax.all_to_all(blocks, axes, split_axis=0, concat_axis=0, tiled=True)
 
 
-def gather_rows(rows):
-    return lax.all_gather(rows, "seq", axis=0, tiled=True)
+def gather_rows(rows, axis):
+    return lax.all_gather(rows, axis, axis=0, tiled=True)
+
+
+def trade(block, distance):
+    return lax.ppermute(block, "batch", [(i, i ^ distance) for i in range(4)])
+
+
+def first_sum(got, own, other):
+    own = own.astype(full) + got[0].astype(full)
+    other = (other.astype(full) + got[1].astype(full)).astype(low)
+    return own, other
+
+
+def together(*values):
+    return lax.optimization_barrier(values)
 
 
 def shards(
@@ -239,7 +619,6 @@
     seq_count = lax.axis_size("seq")
     batch_count = lax.axis_size("batch")
     device_count = seq_count * batch_count
-    seq_index = lax.axis_index("seq")
     token_count = inputs.shape[1]
     model_width = inputs.shape[2]
     ff_width = w_in.shape[1]
@@ -253,116 +632,89 @@
     width = head_count * head_dim
     tables = (lengths, rand_owners, rand_offsets, global_ids)
 
-    def to_heads(*parts):
-        split = [p.reshape(token_count, head_groups, width).transpose(1, 0, 2) for p in parts]
-        joined = jnp.concatenate(split, axis=2)
+    def to_heads(sent):
         if copies > 1:
-            joined = jnp.repeat(joined, copies, axis=0)
-        received = swap(joined, "seq")
-        return received.reshape(total_tokens, len(parts) * width)
-
-    def to_tokens(rows, count):
-        received = swap(rows.reshape(seq_count, token_count, count * width), "seq")
-        received = received[::copies]
-        return [
-            received[:, :, i * width : (i + 1) * width].transpose(1, 0, 2).reshape(token_count, model_width)
-            for i in range(count)
-        ]
-
-    gain_one = ln1_gain.astype(full)
-    gain_two = ln2_gain.astype(full)
-    grad_out = cotangent[0]
-    grad_out_all = gather_rows(grad_out)
-    residual_in = inputs[0].astype(full)
-    normed, scaled_one, inverse_one = normalize(residual_in, gain_one, ln1_shift.astype(full))
-    normed_low = normed.astype(low)
-    normed_all = gather_rows(normed_low)
-    qkv = to_heads(
-        matmul(normed_low, w_query).astype(low),
-        matmul(normed_low, w_key).astype(low),
-        matmul(normed_low, w_value).astype(low),
+            sent = jnp.repeat(sent, copies, axis=0)
+        return swap(sent, "seq").reshape(total_tokens, -1)
+
+    def to_tokens(rows):
+        return swap(rows.reshape(seq_count, token_count, -1), "seq")[::copies]
+
+    def one_row(vector):
+        return vector.reshape(1, -1)
+
+    rows_in, grad_out = inputs[0], cotangent[0]
+    gain_one, gain_two = one_row(ln1_gain), one_row(ln2_gain)
+    places = jnp.stack([lax.axis_index("seq"), lax.axis_index("batch")]).astype(jnp.int32)
+    sent, kept = project(
+        rows_in, grad_out, gain_one, one_row(ln1_shift), w_query, w_key, w_value, head_groups, width
     )
+    qkv, kept = together(to_heads(sent), kept)
+    kept_all = gather_rows(kept, "seq")
     attended_all, log_total = attend(tables, qkv, block_count, head_count, scale)
-    (attended,) = to_tokens(attended_all, 1)
-    middle = residual_in + matmul(attended, w_out)
-    normed_two, scaled_two, inverse_two = normalize(middle, gain_two, ln2_shift.astype(full))
-    normed_two_low = normed_two.astype(low)
-    normed_two_all = gather_rows(normed_two_low)
-    inner = matmul(normed_two_low, w_in) + b_in.astype(full)
-    gelu = functools.partial(jax.nn.gelu, approximate=False)
-    activated, gelu_pull = jax.vjp(gelu, inner)
-    activated = activated.astype(low)
-    output = (middle + matmul(activated, w_back) + b_back.astype(full)).astype(low)
-
-    def to_columns(rows):
-        columns = rows.shape[1] // seq_count
-        split = rows.reshape(token_count, seq_count, columns).transpose(1, 0, 2)
-        return swap(split, "seq").reshape(total_tokens, columns)
-
-    activated_all = to_columns(activated)
-    grad_w_back = matmul_left(activated_all, grad_out_all).astype(low)
-    grad_out_full = grad_out.astype(full)
-    grad_b_back = jnp.sum(grad_out_full, axis=0)
-    grad_inner = gelu_pull(matmul_right(grad_out, w_back))[0].astype(low)
-    grad_inner_all = to_columns(grad_inner)
-    grad_w_in = matmul_left(normed_two_all, grad_inner_all).astype(low)
-    grad_b_in = jnp.sum(grad_inner.astype(full), axis=0)
-    grad_normed_two = matmul_right(grad_inner, w_in)
-    grad_ln2_gain = jnp.sum(grad_normed_two * scaled_two, axis=0)
-    grad_ln2_shift = jnp.sum(grad_normed_two, axis=0)
-    grad_middle = grad_out_full + normalize_back(grad_normed_two, scaled_two, inverse_two, gain_two)
-    grad_middle_low = grad_middle.astype(low)
-    grad_attended = matmul_right(grad_middle_low, w_out).astype(low)
-    grad_middle_all = gather_rows(grad_middle_low)
-    out_rows = width // copies
-    own_attended = lax.dynamic_slice_in_dim(attended_all, seq_index % copies * out_rows, out_rows, axis=1)
-    grad_w_out = matmul_left(own_attended, grad_middle_all).astype(low)
-    grad_qkv = attend_back(
-        tables, qkv, log_total, to_heads(grad_attended), block_count, head_count, scale
+    middle, normed_two, attended = attend_out(
+        to_tokens(attended_all), rows_in, w_out, gain_two, one_row(ln2_shift)
     )
-    grad_queries, grad_keys, grad_values = to_tokens(grad_qkv, 3)
-    grad_w_qkv = matmul_left(normed_all, grad_qkv).astype(low)
-    grad_normed = (
-        matmul_right(grad_queries, w_query)
-        + matmul_right(grad_keys, w_key)
-        + matmul_right(grad_values, w_value)
+    normed_two_all = gather_rows(normed_two, "seq")
+    output, grad_middle, grad_middle_low, grad_attended, gain_two_grads, grad_b_in = feed(
+        normed_two,
+        middle,
+        grad_out,
+        w_out,
+        gain_two,
+        one_row(b_back),
+        w_in,
+        one_row(b_in),
+        w_back,
+        head_groups,
+        width,
     )
-    grad_ln1_gain = jnp.sum(grad_normed * scaled_one, axis=0)
-    grad_ln1_shift = jnp.sum(grad_normed, axis=0)
-    input_grad = (
-        grad_middle + normalize_back(grad_normed, scaled_one, inverse_one, gain_one)
-    ).astype(low)
-
-    both = ("seq", "batch")
+    out_blocks = product(places, attended, model_width, grad_middle_low, seq_count, "out_product")
+    grad_rows, out_blocks = together(to_heads(grad_attended), out_blocks)
+    out_got = trade(out_blocks[0], 1)
+    grad_qkv = attend_back(tables, qkv, log_total, grad_rows, block_count, head_count, scale)
+    out_own, out_other = first_sum(out_got, *out_blocks[1:])
+    out_last = trade(out_other, 2)
+    grad_qkv_near = to_tokens(grad_qkv)
+
     slim = model_width // device_count
-
-    def rows_of(columns, count):
-        received = swap(columns.reshape(device_count, slim, columns.shape[1]), both)
-        received = received.reshape(seq_count, batch_count, slim, columns.shape[1])
-        summed = jnp.sum(received[::count].astype(full), axis=1)
-        return summed.transpose(1, 0, 2)
-
-    in_rows = rows_of(grad_w_in, 1).reshape(slim, ff_width)
-    qkv_rows = rows_of(grad_w_qkv, copies)
+    inner_columns = ff_width // seq_count
+    qkv_blocks = product(places, kept_all, model_width, grad_qkv, seq_count, "qkv_product")
+    qkv_got = trade(qkv_blocks[0], 1)
+    in_sent, in_own, in_other, back_sent, back_own, back_other = feed_products(
+        places, normed_two_all, kept_all, w_in, one_row(b_in), w_back, seq_count
+    )
+    qkv_got, grad_qkv_near, in_sent, back_sent, out_last = together(
+        qkv_got, grad_qkv_near, in_sent, back_sent, out_last
+    )
+    qkv_own, qkv_other = first_sum(qkv_got, *qkv_blocks[1:])
+    qkv_last = trade(qkv_other, 2)
+    in_got = trade(in_sent, 1)
+    back_got = trade(back_sent, 1)
+    input_grad, gain_one_grads = project_back(
+        rows_in, gain_one, grad_middle, grad_qkv_near, w_query, w_key, w_value
+    )
+    in_got, back_got, qkv_last, gain_one_grads = together(in_got, back_got, qkv_last, gain_one_grads)
+    in_own, in_other = first_sum(in_got, in_own, in_other)
+    in_last = trade(in_other, 2)
+    back_own, back_other = first_sum(back_got, back_own, back_other)
+    back_rows = (back_own + trade(back_other, 2).astype(full))[0]
+
+    mixed = [
+        (own + last.astype(full)).astype(low)
+        for own, last in ((in_own, in_last), (qkv_own, qkv_last), (out_own, out_last))
+    ]
+    mixed = swap(jnp.concatenate(mixed, axis=2), "seq")
+    at = inner_columns + 3 * width
+    in_rows = mixed[:, :, :inner_columns].transpose(1, 0, 2).reshape(slim, ff_width).astype(full)
+    qkv_rows = mixed[::copies, :, inner_columns:at].transpose(1, 0, 2).astype(full)
     qkv_rows = [
         qkv_rows[:, :, i * width : (i + 1) * width].reshape(slim, model_width) for i in range(3)
     ]
-    back_out = lax.psum_scatter(
-        jnp.concatenate(
-            [
-                grad_w_back.reshape(batch_count, -1, model_width),
-                grad_w_out.reshape(batch_count, -1, model_width),
-            ],
-            axis=1,
-        ),
-        "batch",
-        scatter_dimension=0,
-        tiled=False,
-    ).astype(full)
-    back_rows = ff_width // device_count
-    small = [grad_ln1_gain, grad_ln1_shift, grad_ln2_gain, grad_ln2_shift, grad_b_back, grad_b_in]
+    out_rows = jnp.sum(mixed[:, :, at:].astype(full), axis=0)
+    small = [gain_one_grads[0], gain_one_grads[1], *gain_two_grads, grad_b_in[0]]
     packed = jnp.concatenate([v.reshape(device_count, -1) for v in small], axis=1)
-    packed = jnp.sum(swap(packed, both), axis=0)
+    packed = jnp.sum(swap(packed, ("seq", "batch")), axis=0)
     cuts, at = [], 0
     for v in small:
         size = v.shape[0] // device_count
@@ -376,12 +728,12 @@
         qkv_rows[0],
         qkv_rows[1],
         qkv_rows[2],
-        back_out[back_rows:],
+        out_rows,
         cuts[2],
         cuts[3],
         in_rows,
         cuts[5],
-        back_out[:back_rows],
+        back_rows,
         cuts[4],
     )
 

time: 303 us -> 226 us (0.75)
  waiting for transfers between devices: 129 us -> 51.7 us
  matrix products: 63.6 us -> 0 us
  Pallas kernels: 21.2 us -> 68.9 us
  blocking collectives: 0 us -> 22.2 us
  starting transfers between devices: 41.3 us -> 33.8 us
  local copies, waits for them, and re-layouts: 15.3 us -> 21.5 us
  other arithmetic: 15.8 us -> 11.5 us
    all_to_all x9 -> x5, waiting for transfers between devices: 128 us -> 15.6 us  [swap(): return lax.all_to_all(blocks, axes, split_axis=0, concat_axis=0, tiled=True)]
    dot_general x16 -> x0, matrix products: 63.6 us -> none  [the longest x6 24.5 us: matmul(): return jnp.dot(left, right, preferred_element_type=full)]
    pallas_call x0 -> x7, Pallas kernels: none -> 46.8 us  [the longest x1 15.4 us: feed(): pl.pallas_call(feed_kernel, grid=(ff // columns,), out_shape=(jax.ShapeDt...]
    ppermute x0 -> x8, waiting for transfers between devices: none -> 36.1 us  [trade(): return lax.ppermute(block, 'batch', [(i, i ^ distance) for i in range(4)])]
    all_to_all x0 -> x1, blocking collectives: none -> 22.2 us  [swap(): return lax.all_to_all(blocks, axes, split_axis=0, concat_axis=0, tiled=True)]
    all_to_all x9 -> x5, starting transfers between devices: 40.7 us -> 22 us  [swap(): return lax.all_to_all(blocks, axes, split_axis=0, concat_axis=0, tiled=True)]
    unnamed x48 -> x57, local copies, waits for them, and re-layouts: 2.17 us -> 14.3 us
    ppermute x0 -> x8, starting transfers between devices: none -> 11.6 us  [trade(): return lax.ppermute(block, 'batch', [(i, i ^ distance) for i in range(4)])]
  transfers between devices with their start and end apart: 14 -> 15, of which waited for: 9 -> 9; matrix products, arithmetic and copies ran while one was open for 28% -> 5% of each run, Pallas kernels for 7% -> 28%
where the time goes in v2:
time: 226 us; the launch traced here: 225 us
  Pallas kernels  68.9 us (30%)
  waiting for transfers between devices  51.7 us (23%)
  starting transfers between devices  33.8 us (15%)
  blocking collectives  22.2 us (10%)
  local copies, waits for them, and re-layouts  21.5 us (10%)
  between operations  15.2 us (7%)
  other arithmetic  11.5 us (5%)
    ppermute x8, waiting for transfers between devices, trade(): return lax.ppermute(block, 'batch', [(i, i ^ distance) for i in range(4)])  36.1 us
    all_to_all x1, blocking collectives, swap(): return lax.all_to_all(blocks, axes, split_axis=0, concat_axis=0, tiled=True)  22.2 us
    all_to_all x5, starting transfers between devices, swap(): return lax.all_to_all(blocks, axes, split_axis=0, concat_axis=0, tiled=True)  22 us
    all_to_all x5, waiting for transfers between devices, swap(): return lax.all_to_all(blocks, axes, split_axis=0, concat_axis=0, tiled=True)  15.6 us
    pallas_call x1, Pallas kernels, feed(): pl.pallas_call(feed_kernel, grid=(ff // columns,), out_shape=(jax.ShapeDt...  15.4 us
    unnamed x57, local copies, waits for them, and re-layouts  14.3 us
    pallas_call x1, Pallas kernels, attend_back(): pl.pallas_call(functools.partial(attend_back_kernel, block_count, head_co...  12.1 us
    ppermute x8, starting transfers between devices, trade(): return lax.ppermute(block, 'batch', [(i, i ^ distance) for i in range(4)])  11.6 us
  transfers between devices with their start and end apart: 15, of which 9 were waited for; matrix products, arithmetic and copies ran while one was open for 5% of the time, Pallas kernels for 28%

profile of v2, /device:TPU:0, one launch (start us, length us, event | category | flops | bytes accessed | tf_op | source)
XLA Modules:
  0.0 224.7 jit_solution(17466815096004241606)
XLA Ops:
  9.8 6.0 %project.1 = (bf16[8,192,384]{2,1,0:T(8,128)(2,1)}, bf16[192,2048]{1,0:T(8,128)(2,1)}) custom-call(bf16[192,1024]{1,0:T(8,128)(2,1)} %bitcast.60, bf16[192,1024]{1,0:T(8,128)(2,1)} %bitcast.66, bf16[1,1024]{1,0:T(2,128)(2,1)} %reshape.113.gain, bf16[1,1024]{1,0:T(2,128)(2,1)} %reshape.114.shift, bf16[1024,1024]{1,0:T(8,128)(2,1)} %w_query.3, ...), custom_call_target="tpu_custom_call" | custom-call | flops 1207959552 | bytes 6291456 | tf_op jit(solution)/shard_map/project/pallas_call | solution.py:234
  15.8 22.2 %all_to_all.34 = bf16[8,192,384]{2,1,0:T(8,128)(2,1)} all-to-all(bf16[8,192,384]{2,1,0:T(8,128)(2,1)} %get-tuple-element.56), channel_id=1, replica_groups=mesh['seq'=8,'batch'=4] {'seq'}, dimensions={0} | all-to-all | bytes 2359296 | tf_op jit(solution)/shard_map/all_to_all | solution.py:578
  40.3 10.0 %attend.1 = (bf16[1536,128]{1,0:T(8,128)(2,1)}, f32[24,1,128]{2,1,0:T(1,128)S(1)}) custom-call(s32[1,1]{1,0:T(1,128)S(6)} %copy.60.lens, s32[1,24,3]{2,1,0:T(8,128)S(1)} %copy.44.owners, s32[1,24,3]{2,1,0:T(8,128)S(1)} %copy.45.offsets, s32[1,1,2]{2,1,0:T(1,128)S(1)} %copy-done.14, bf16[1536,384]{1,0:T(8,128)(2,1)S(1)} %bitcast.63), custom_call_target="tpu_custom_call" | custom-call | flops 805306368 | bytes 1572864 | tf_op jit(solution)/shard_map/attend/pallas_call | solution.py:169
  50.3 3.6 %all-to-all-start.1 = ((bf16[8,192,128]{2,1,0:T(8,128)(2,1)}), bf16[8,192,128]{2,1,0:T(8,128)(2,1)S(1)}, u32[]{:S(2)}, u32[]{:S(2)}) async-start(bf16[8,192,128]{2,1,0:T(8,128)(2,1)} %bitcast.3), calls=%async_computation.1 | async-start | bytes 786432 | tf_op jit(solution)/shard_map/all_to_all | solution.py:578
  54.0 8.2 %all-to-all-done.1.received = bf16[8,192,128]{2,1,0:T(8,128)(2,1)S(1)} async-done(((bf16[8,192,128]{2,1,0:T(8,128)(2,1)}), bf16[8,192,128]{2,1,0:T(8,128)(2,1)S(1)}, u32[]{:S(2)}, u32[]{:S(2)}) %all-to-all-start.1) | async-done | bytes 393248 | tf_op jit(solution)/shard_map/all_to_all | solution.py:578
  66.6 15.4 %feed.1 = (bf16[192,1024]{1,0:T(8,128)(2,1)}, f32[192,1024]{1,0:T(8,128)S(1)}, bf16[192,1024]{1,0:T(8,128)(2,1)S(1)}, bf16[8,192,128]{2,1,0:T(8,128)(2,1)}, f32[...) custom-call(bf16[192,1024]{1,0:T(8,128)(2,1)} %get-tuple-element.60.normed, f32[192,1024]{1,0:T(8,128)S(1)} %copy-done.10, ...), custom_call_target="tpu_custom_call" | custom-call | flops 6442450944 | bytes 16777216 | tf_op jit(solution)/shard_map/feed/pallas_call | solution.py:409
  83.7 3.6 %all-to-all-start.2 = ((bf16[8,192,128]{2,1,0:T(8,128)(2,1)}), bf16[8,192,128]{2,1,0:T(8,128)(2,1)S(1)}, u32[]{:S(2)}, u32[]{:S(2)}) async-start(bf16[8,192,128]{2,1,0:T(8,128)(2,1)} %get-tuple-element.66), calls=%async_computation.2 | async-start | bytes 786432 | tf_op jit(solution)/shard_map/all_to_all | solution.py:578
  91.8 3.7 %all-to-all-done.2 = bf16[8,192,128]{2,1,0:T(8,128)(2,1)S(1)} async-done(((bf16[8,192,128]{2,1,0:T(8,128)(2,1)}), bf16[8,192,128]{2,1,0:T(8,128)(2,1)S(1)}, u32[]{:S(2)}, u32[]{:S(2)}) %all-to-all-start.2) | async-done | bytes 393248 | tf_op jit(solution)/shard_map/all_to_all | solution.py:578
  97.5 12.1 %attend_back.1.right = bf16[1536,384]{1,0:T(8,128)(2,1)} custom-call(s32[1,1]{1,0:T(1,128)S(6)} %copy.60.lens, s32[1,24,3]{2,1,0:T(8,128)S(1)} %copy.44.owners, s32[1,24,3]{2,1,0:T(8,128)S(1)} %copy.45.offsets, s32[1,1,2]{2,1,0:T(1,128)S(1)} %copy-done.14, bf16[1536,384]{1,0:T(8,128)(2,1)S(1)} %bitcast.64, f32[24,1,128]{2,1,0:T(1,128)S(1)} %get-tuple-element.65.log_total, ...), custom_call_target="tpu_custom_call" | custom-call | flops 2013265920 | bytes 3145728 | tf_op jit(solution)/shard_map/attend_back/pallas_call | solution.py:188
  109.6 4.4 %all-to-all-start.3 = ((bf16[8,192,384]{2,1,0:T(8,128)(2,1)}), bf16[8,192,384]{2,1,0:T(8,128)(2,1)}, u32[]{:S(2)}, u32[]{:S(2)}) async-start(bf16[8,192,384]{2,1,0:T(8,128)(2,1)} %bitcast.8), calls=%async_computation.3 | async-start | bytes 2359296 | tf_op jit(solution)/shard_map/all_to_all | solution.py:578
  114.3 5.0 %collective-permute-done.1 = bf16[2,8,32,1024]{3,2,1,0:T(8,128)(2,1)} collective-permute-done((bf16[2,8,32,1024]{3,2,1,0:T(8,128)(2,1)}, bf16[2,8,32,1024]{3,2,1,0:T(8,128)(2,1)}, u32[]{:S(2)}, u32[]{:S(2)}) %collective-permute-start.1) | collective-permute-done | bytes 1048608 | tf_op jit(solution)/shard_map/ppermute | solution.py:586
  121.3 2.8 %collective-permute-start.2 = (bf16[8,32,1024]{2,1,0:T(8,128)(2,1)}, bf16[8,32,1024]{2,1,0:T(8,128)(2,1)}, u32[]{:S(2)}, u32[]{:S(2)}) collective-permute-start(bf16[8,32,1024]{2,1,0:T(8,128)(2,1)} %fusion.2), channel_id=1, source_target_pairs={{0,2},{1,3},{2,0},{3,1},{4,6},{5,7},{6,4},{7,5},{8,10},{9,11},{10,... | collective-permute-start | bytes 1572872 | tf_op jit(solution)/shard_map/ppermute | solution.py:586
  124.1 2.8 %copy-done = bf16[1536,2048]{1,0:T(8,128)(2,1)S(1)} copy-done((bf16[1536,2048]{1,0:T(8,128)(2,1)S(1)}, bf16[1536,2048]{1,0:T(8,128)(2,1)}, u32[]{:S(2)}) %copy-start) | copy-done | bytes 6291480
  126.9 4.4 %qkv_product.1 = (bf16[2,8,32,384]{3,2,1,0:T(8,128)(2,1)S(1)}, bf16[8,32,384]{2,1,0:T(8,128)(2,1)S(1)}, bf16[8,32,384]{2,1,0:T(8,128)(2,1)S(1)}) custom-call(s32[2]{0:T(128)S(1)} %pad_add_fusion.places, bf16[1536,2048]{1,0:T(8,128)(2,1)S(1)} %copy-done, bf16[1536,384]{1,0:T(8,128)(2,1)} %attend_back.1.right), custom_call_target="tpu_custom_call" | custom-call | flops 1207959552 | bytes 4325376 | tf_op jit(solution)/shard_map/qkv_product/pallas_call | solution.py:486
  134.8 10.8 %feed_products.1 = (bf16[2,8,32,512]{3,2,1,0:T(8,128)(2,1)S(1)}, bf16[8,32,512]{2,1,0:T(8,128)(2,1)S(1)}, bf16[8,32,512]{2,1,0:T(8,128)(2,1)S(1)}, bf16[2,1,128,...) custom-call(s32[2]{0:T(128)S(1)} %pad_add_fusion.places, ...), custom_call_target="tpu_custom_call" | custom-call | flops 6442450944 | bytes 8388608 | tf_op jit(solution)/shard_map/feed_products/pallas_call | solution.py:548
  146.4 3.2 %collective-permute-done = bf16[2,8,32,384]{3,2,1,0:T(8,128)(2,1)} collective-permute-done((bf16[2,8,32,384]{3,2,1,0:T(8,128)(2,1)S(1)}, bf16[2,8,32,384]{3,2,1,0:T(8,128)(2,1)}, u32[]{:S(2)}, u32[]{:S(2)}) %collective-permute-start) | collective-permute-done | bytes 393248 | tf_op jit(solution)/shard_map/ppermute | solution.py:586
  153.6 7.1 %project_back.1 = (bf16[192,1024]{1,0:T(8,128)(2,1)}, f32[2,1024]{1,0:T(2,128)}) custom-call(bf16[192,1024]{1,0:T(8,128)(2,1)} %bitcast.61, bf16[1,1024]{1,0:T(2,128)(2,1)} %reshape.113.gain, f32[192,1024]{1,0:T(8,128)} %copy-done.6, bf16[8,192,384]{2,1,0:T(8,128)(2,1)} %all-to-all-done.3.received, bf16[1024,1024]{1,0:T(8,128)(2,1)} %w_query.3, ...), custom_call_target="tpu_custom_call" | custom-call | flops 1207959552 | bytes 6291456 | tf_op jit(solution)/shard_map/project_back/pallas_call | solution.py:289
  160.7 2.3 %fusion.1 = bf16[8,32,1024]{2,1,0:T(8,128)(2,1)} fusion(bf16[8,32,1024]{2,1,0:T(8,128)(2,1)} %collective-permute-done.2, bf16[8,32,1024]{2,1,0:T(8,128)(2,1)S(1)} %get-tuple-element.93, bf16[2,8,32,1024]{3,2,1,0:T(8,128)(2,1)} %collective-permute-done.1), kind=kLoop, calls=%fused_computation.2 | loop fusion | flops 1572864 | bytes 2097152 | tf_op jit(solution)/shard_map/convert_element_type | solution.py:704
  163.0 11.8 %collective-permute-done.5 = bf16[8,32,384]{2,1,0:T(8,128)(2,1)S(1)} collective-permute-done((bf16[8,32,384]{2,1,0:T(8,128)(2,1)S(1)}, bf16[8,32,384]{2,1,0:T(8,128)(2,1)S(1)}, u32[]{:S(2)}, u32[]{:S(2)}) %collective-permute-start.5) | collective-permute-done | bytes 196640 | tf_op jit(solution)/shard_map/ppermute | solution.py:586
  174.9 2.2 collective-permute-done.4
  180.4 6.6 %all-to-all-start.4 = ((f32[32,1,288]{2,1,0:T(1,128)}), f32[32,1,288]{2,1,0:T(1,128)S(1)}, u32[]{:S(2)}, u32[]{:S(2)}) async-start(f32[32,1,288]{2,1,0:T(1,128)} %all_to_all.25), calls=%async_computation.4 | async-start | bytes 98304 | tf_op jit(solution)/shard_map/all_to_all | solution.py:578
  191.2 3.7 %all-to-all-done.4 = f32[32,1,288]{2,1,0:T(1,128)S(1)} async-done(((f32[32,1,288]{2,1,0:T(1,128)}), f32[32,1,288]{2,1,0:T(1,128)S(1)}, u32[]{:S(2)}, u32[]{:S(2)}) %all-to-all-start.4) | async-done | bytes 36896 | tf_op jit(solution)/shard_map/all_to_all | solution.py:578
  194.9 3.9 %all-to-all-start.5 = ((bf16[8,32,1920]{2,1,0:T(8,128)(2,1)}), bf16[8,32,1920]{2,1,0:T(8,128)(2,1)S(1)}, u32[]{:S(2)}, u32[]{:S(2)}) async-start(bf16[8,32,1920]{2,1,0:T(8,128)(2,1)} %pad_maximum_fusion), calls=%async_computation.5 | async-start | bytes 1966080 | tf_op jit(solution)/shard_map/all_to_all | solution.py:578
  201.1 12.8 %collective-permute-done.7 = bf16[1,128,1024]{2,1,0:T(8,128)(2,1)S(1)} collective-permute-done((bf16[1,128,1024]{2,1,0:T(8,128)(2,1)S(1)}, bf16[1,128,1024]{2,1,0:T(8,128)(2,1)S(1)}, u32[]{:S(2)}, u32[]{:S(2)}) %collective-permute-start.7) | collective-permute-done | bytes 262176 | tf_op jit(solution)/shard_map/ppermute | solution.py:586
  (109 shorter events, 41.0 us)
Async XLA Ops:
  7.2 116.9 %all-gather.3.cloned.1.call-start = ((), (), s32[]{:S(2)}) async-start(), calls=%async_computation.6 | async-start | bytes 7077888 | tf_op jit(solution)/shard_map/all_gather | solution.py:582
  15.8 23.1 %copy-start.25 = (s32[1,24,3]{1,0,2:T(1,128)S(1)}, s32[1,24,3]{1,0,2:T(1,128)}, u32[]{:S(2)}) copy-start(s32[1,24,3]{1,0,2:T(1,128)} %param.21) | copy-start | bytes 868
  15.8 23.1 %copy-start.26 = (s32[1,24,3]{1,0,2:T(1,128)S(1)}, s32[1,24,3]{1,0,2:T(1,128)}, u32[]{:S(2)}) copy-start(s32[1,24,3]{1,0,2:T(1,128)} %param.22) | copy-start | bytes 868
  15.8 23.2 %copy-start.14 = (s32[1,1,2]{2,1,0:T(1,128)S(1)}, s32[1,1,2]{2,1,0:T(1,128)}, u32[]{:S(2)}) copy-start(s32[1,1,2]{2,1,0:T(1,128)} %globals_.3) | copy-start | bytes 28
  38.0 16.0 %copy-start.22 = (bf16[1024]{0:T(1024)(128)(2,1)S(1)}, bf16[1024]{0:T(1024)(128)(2,1)}, u32[]{:S(2)}) copy-start(bf16[1024]{0:T(1024)(128)(2,1)} %param.30) | copy-start | bytes 6148
  38.0 16.0 %copy-start.23 = (bf16[1024]{0:T(1024)(128)(2,1)S(1)}, bf16[1024]{0:T(1024)(128)(2,1)}, u32[]{:S(2)}) copy-start(bf16[1024]{0:T(1024)(128)(2,1)} %param.31) | copy-start | bytes 6148
  38.0 24.2 %copy-start.1 = (bf16[1,192,1024]{2,1,0:T(8,128)(2,1)S(1)}, bf16[1,192,1024]{2,1,0:T(8,128)(2,1)}, u32[]{:S(2)}) copy-start(bf16[1,192,1024]{2,1,0:T(8,128)(2,1)} %param.18) | copy-start | bytes 1179652
  38.0 24.2 %copy-start.3 = (bf16[1024,1024]{1,0:T(8,128)(2,1)S(1)}, bf16[1024,1024]{1,0:T(8,128)(2,1)}, u32[]{:S(2)}) copy-start(bf16[1024,1024]{1,0:T(8,128)(2,1)} %w_out.3) | copy-start | bytes 6291460
  50.3 11.9 %all-to-all-start.1 = ((bf16[8,192,128]{2,1,0:T(8,128)(2,1)}), bf16[8,192,128]{2,1,0:T(8,128)(2,1)S(1)}, u32[]{:S(2)}, u32[]{:S(2)}) async-start(bf16[8,192,128]{2,1,0:T(8,128)(2,1)} %bitcast.3), calls=%async_computation.1 | async-start | bytes 786432 | tf_op jit(solution)/shard_map/all_to_all | solution.py:578
  53.9 79.0 %all-gather.5.cloned.1.call-start = ((), (), s32[]{:S(2)}) async-start(), calls=%async_computation.7 | async-start | bytes 3538944 | tf_op jit(solution)/shard_map/all_gather | solution.py:582
  83.7 11.9 %all-to-all-start.2 = ((bf16[8,192,128]{2,1,0:T(8,128)(2,1)}), bf16[8,192,128]{2,1,0:T(8,128)(2,1)S(1)}, u32[]{:S(2)}, u32[]{:S(2)}) async-start(bf16[8,192,128]{2,1,0:T(8,128)(2,1)} %get-tuple-element.66), calls=%async_computation.2 | async-start | bytes 786432 | tf_op jit(solution)/shard_map/all_to_all | solution.py:578
  95.6 23.7 %collective-permute-start.1 = (bf16[2,8,32,1024]{3,2,1,0:T(8,128)(2,1)}, bf16[2,8,32,1024]{3,2,1,0:T(8,128)(2,1)}, u32[]{:S(2)}, u32[]{:S(2)}) collective-permute-start(bf16[2,8,32,1024]{3,2,1,0:T(8,128)(2,1)} %copy-done.8), channel_id=1, source_target_pairs={{0,1},{1,0},{2,3},{3,2},{4,5},{5,4},{6,7},{7,6},{8,9},{9,8},{10,11... | collective-permute-start | bytes 3145736 | tf_op jit(solution)/shard_map/ppermute | solution.py:586
  109.6 36.8 %all-to-all-start.3 = ((bf16[8,192,384]{2,1,0:T(8,128)(2,1)}), bf16[8,192,384]{2,1,0:T(8,128)(2,1)}, u32[]{:S(2)}, u32[]{:S(2)}) async-start(bf16[8,192,384]{2,1,0:T(8,128)(2,1)} %bitcast.8), calls=%async_computation.3 | async-start | bytes 2359296 | tf_op jit(solution)/shard_map/all_to_all | solution.py:578
  121.3 25.1 %collective-permute-start.2 = (bf16[8,32,1024]{2,1,0:T(8,128)(2,1)}, bf16[8,32,1024]{2,1,0:T(8,128)(2,1)}, u32[]{:S(2)}, u32[]{:S(2)}) collective-permute-start(bf16[8,32,1024]{2,1,0:T(8,128)(2,1)} %fusion.2), channel_id=1, source_target_pairs={{0,2},{1,3},{2,0},{3,1},{4,6},{5,7},{6,4},{7,5},{8,10},{9,11},{10,... | collective-permute-start | bytes 1572872 | tf_op jit(solution)/shard_map/ppermute | solution.py:586
  131.3 18.3 %collective-permute-start = (bf16[2,8,32,384]{3,2,1,0:T(8,128)(2,1)S(1)}, bf16[2,8,32,384]{3,2,1,0:T(8,128)(2,1)}, u32[]{:S(2)}, u32[]{:S(2)}) collective-permute-start(bf16[2,8,32,384]{3,2,1,0:T(8,128)(2,1)S(1)} %get-tuple-element.73), channel_id=1, source_target_pairs={{0,1},{1,0},{2,3},{3,2},{4,5},{5,4},{6,7},{7,6},{8,9},{9,8},{10,11... | collective-permute-start | bytes 1179656 | tf_op jit(solution)/shard_map/ppermute | solution.py:586
  149.6 25.3 %collective-permute-start.3 = (bf16[2,8,32,512]{3,2,1,0:T(8,128)(2,1)}, bf16[2,8,32,512]{3,2,1,0:T(8,128)(2,1)}, u32[]{:S(2)}, u32[]{:S(2)}) collective-permute-start(bf16[2,8,32,512]{3,2,1,0:T(8,128)(2,1)} %copy-done.11), channel_id=1, source_target_pairs={{0,1},{1,0},{2,3},{3,2},{4,5},{5,4},{6,7},{7,6},{8,9},{9,8},{10,11... | collective-permute-start | bytes 1572872 | tf_op jit(solution)/shard_map/ppermute | solution.py:586
  149.6 27.5 %collective-permute-start.4 = (bf16[2,1,128,1024]{3,2,1,0:T(8,128)(2,1)S(1)}, bf16[2,1,128,1024]{3,2,1,0:T(8,128)(2,1)S(1)}, u32[]{:S(2)}, u32[]{:S(2)}) collective-permute-start(bf16[2,1,128,1024]{3,2,1,0:T(8,128)(2,1)S(1)} %get-tuple-element.81), channel_id=1, source_target_pairs={{0,1},{1,0},{2,3},{3,2},{4,5},{5,4},{6,7},{7,6},{8,9},{9,8},{10,11... | collective-permute-start | bytes 1572872 | tf_op jit(solution)/shard_map/ppermute | solution.py:586
  152.6 22.3 %collective-permute-start.5 = (bf16[8,32,384]{2,1,0:T(8,128)(2,1)S(1)}, bf16[8,32,384]{2,1,0:T(8,128)(2,1)S(1)}, u32[]{:S(2)}, u32[]{:S(2)}) collective-permute-start(bf16[8,32,384]{2,1,0:T(8,128)(2,1)S(1)} %fusion.11), channel_id=1, source_target_pairs={{0,2},{1,3},{2,0},{3,1},{4,6},{5,7},{6,4},{7,5},{8,10},{9,11},{10,... | collective-permute-start | bytes 589832 | tf_op jit(solution)/shard_map/ppermute | solution.py:586
  160.7 18.8 %copy-start.21 = (f32[2,1024]{1,0:T(2,128)S(1)}, f32[2,1024]{1,0:T(2,128)}, u32[]{:S(2)}) copy-start(f32[2,1024]{1,0:T(2,128)} %get-tuple-element.85) | copy-start | bytes 24580
  163.0 27.1 %copy-start.17 = (bf16[8,32,1024]{2,1,0:T(8,128)(2,1)S(1)}, bf16[8,32,1024]{2,1,0:T(8,128)(2,1)}, u32[]{:S(2)}) copy-start(bf16[8,32,1024]{2,1,0:T(8,128)(2,1)} %fusion.1) | copy-start | bytes 1572868
  178.2 10.8 %collective-permute-start.6 = (bf16[8,32,512]{2,1,0:T(8,128)(2,1)S(1)}, bf16[8,32,512]{2,1,0:T(8,128)(2,1)S(1)}, u32[]{:S(2)}, u32[]{:S(2)}) collective-permute-start(bf16[8,32,512]{2,1,0:T(8,128)(2,1)S(1)} %fusion.6), channel_id=1, source_target_pairs={{0,2},{1,3},{2,0},{3,1},{4,6},{5,7},{6,4},{7,5},{8,10},{9,11},{10,... | collective-permute-start | bytes 786440 | tf_op jit(solution)/shard_map/ppermute | solution.py:586
  180.4 14.5 %all-to-all-start.4 = ((f32[32,1,288]{2,1,0:T(1,128)}), f32[32,1,288]{2,1,0:T(1,128)S(1)}, u32[]{:S(2)}, u32[]{:S(2)}) async-start(f32[32,1,288]{2,1,0:T(1,128)} %all_to_all.25), calls=%async_computation.4 | async-start | bytes 98304 | tf_op jit(solution)/shard_map/all_to_all | solution.py:578
  194.9 19.8 %all-to-all-start.5 = ((bf16[8,32,1920]{2,1,0:T(8,128)(2,1)}), bf16[8,32,1920]{2,1,0:T(8,128)(2,1)S(1)}, u32[]{:S(2)}, u32[]{:S(2)}) async-start(bf16[8,32,1920]{2,1,0:T(8,128)(2,1)} %pad_maximum_fusion), calls=%async_computation.5 | async-start | bytes 1966080 | tf_op jit(solution)/shard_map/all_to_all | solution.py:578
  198.9 15.0 %collective-permute-start.7 = (bf16[1,128,1024]{2,1,0:T(8,128)(2,1)S(1)}, bf16[1,128,1024]{2,1,0:T(8,128)(2,1)S(1)}, u32[]{:S(2)}, u32[]{:S(2)}) collective-permute-start(bf16[1,128,1024]{2,1,0:T(8,128)(2,1)S(1)} %fusion.3), channel_id=1, source_target_pairs={{0,2},{1,3},{2,0},{3,1},{4,6},{5,7},{6,4},{7,5},{8,10},{9,11},{10,... | collective-permute-start | bytes 786440 | tf_op jit(solution)/shard_map/ppermute | solution.py:586
  (18 other events, 83.1 us)
Sparse Core Ops, SparseCore 0:
  38.1 45.3 all-gather.2
  86.0 32.3 all-gather.4

commit v3 on v2

--- a/solution.py
+++ b/solution.py
@@ -13,6 +13,7 @@
 
 norm_eps = 1e-05
 masked_score = -1e30
+vmem_limit = 60 * 2**20
 low = jnp.bfloat16
 full = jnp.float32
 
@@ -199,6 +200,10 @@
     )(*tables, qkv, log_total, grad_attended)
 
 
+def as_row(vector):
+    return vector[...].astype(full).reshape(1, -1)
+
+
 def row_stats(values):
     average = jnp.mean(values, axis=-1, keepdims=True)
     centered = values - average
@@ -207,48 +212,55 @@
     return centered * inverse, inverse
 
 
-def project_kernel(width, inputs, grad_out, gain, shift, w_query, w_key, w_value, sent, kept):
-    model = inputs.shape[1]
-
-    @pl.when(pl.program_id(0) == 0)
-    def _():
-        scaled, _ = row_stats(inputs[...].astype(full))
-        normed = scaled * gain[...].astype(full) + shift[...].astype(full)
-        kept[:, :model] = normed.astype(low)
-        kept[:, model:] = grad_out[...]
-
-    rows = kept[:, :model]
-    for part, weight in enumerate((w_query, w_key, w_value)):
-        result = matmul(rows, weight[...]).astype(low)
-        for i in range(sent.shape[0]):
-            sent[i, :, part * width : (part + 1) * width] = result[:, i * width : (i + 1) * width]
-
-
-def project(inputs, grad_out, gain, shift, w_query, w_key, w_value, groups, width):
-    tokens, model = inputs.shape
-    columns = 256
-    per_step = columns // width
-    weight = pl.BlockSpec((model, columns), lambda j: (0, j))
-    row = pl.BlockSpec((1, model), lambda j: (0, 0))
-    whole = pl.BlockSpec((tokens, model), lambda j: (0, 0))
+def project_kernel(count, places, *refs):
+    parts, (gain, shift, w_query, w_key, w_value, qkv, normed) = refs[:count], refs[count:]
+    tokens = parts[0].shape[0]
+    weights = jnp.concatenate([w_query[...], w_key[...], w_value[...]], axis=1)
+    for distance, part in enumerate(parts):
+        scaled, _ = row_stats(part[...].astype(full))
+        rows = (scaled * as_row(gain) + as_row(shift)).astype(low)
+        at = pl.ds(pl.multiple_of((places[0] ^ distance) * tokens, tokens), tokens)
+        normed[at, :] = rows
+        qkv[at, :] = matmul(rows, weights).astype(low)
+
+
+def project(places, parts, gain, shift, w_query, w_key, w_value, width, copies):
+    count = len(parts)
+    tokens, model = parts[0].shape
+    whole = pl.BlockSpec((tokens, model), lambda j, places: (0, 0))
+    row = pl.BlockSpec((model,), lambda j, places: (0,))
+    if width % 128:
+        weights = [
+            lax.dynamic_slice_in_dim(w, places[0] // copies * width, width, axis=1)
+            for w in (w_query, w_key, w_value)
+        ]
+        weight = pl.BlockSpec((model, width), lambda j, places: (0, 0))
+    else:
+        weights = [w_query, w_key, w_value]
+        weight = pl.BlockSpec((model, width), lambda j, places: (0, places[0] // copies))
     return pl.pallas_call(
-        functools.partial(project_kernel, width),
-        grid=(model // columns,),
+        functools.partial(project_kernel, count),
+        grid_spec=pltpu.PrefetchScalarGridSpec(
+            num_scalar_prefetch=1,
+            grid=(1,),
+            in_specs=[whole] * count + [row, row] + [weight] * 3,
+            out_specs=(
+                pl.BlockSpec((count * tokens, 3 * width), lambda j, places: (0, 0)),
+                pl.BlockSpec((count * tokens, model), lambda j, places: (0, 0)),
+            ),
+        ),
         out_shape=(
-            jax.ShapeDtypeStruct((groups, tokens, 3 * width), low),
-            jax.ShapeDtypeStruct((tokens, 2 * model), low),
-        ),
-        in_specs=[whole, whole, row, row, weight, weight, weight],
-        out_specs=(
-            pl.BlockSpec((per_step, tokens, 3 * width), lambda j: (j, 0, 0)),
-            pl.BlockSpec((tokens, 2 * model), lambda j: (0, 0)),
-        ),
-        compiler_params=pltpu.CompilerParams(vmem_limit_bytes=58 * 2**20),
+            jax.ShapeDtypeStruct((count * tokens, 3 * width), low),
+            jax.ShapeDtypeStruct((count * tokens, model), low),
+        ),
+        compiler_params=pltpu.CompilerParams(vmem_limit_bytes=vmem_limit),
         cost_estimate=pl.CostEstimate(
-            flops=6 * tokens * model * model, bytes_accessed=6 * model * model, transcendentals=0
+            flops=6 * count * tokens * model * width,
+            bytes_accessed=4 * count * tokens * model,
+            transcendentals=0,
         ),
         name="project",
-    )(inputs, grad_out, gain, shift, w_query, w_key, w_value)
+    )(places, *parts, gain, shift, *weights)
 
 
 def project_back_kernel(
@@ -272,7 +284,7 @@
     def _():
         grad_normed = total[...]
         scaled, inverse = row_stats(inputs[...].astype(full))
-        back = normalize_back(grad_normed, scaled, inverse, gain[...].astype(full))
+        back = normalize_back(grad_normed, scaled, inverse, as_row(gain))
         input_grad[...] = (grad_middle[...] + back).astype(low)
         gain_grads[0:1, :] = jnp.sum(grad_normed * scaled, axis=0, keepdims=True)
         gain_grads[1:2, :] = jnp.sum(grad_normed, axis=0, keepdims=True)
@@ -284,7 +296,7 @@
     width = received.shape[2] // 3
     per_step = columns // width
     weight = pl.BlockSpec((model, columns), lambda j: (0, j))
-    row = pl.BlockSpec((1, model), lambda j: (0, 0))
+    row = pl.BlockSpec((model,), lambda j: (0,))
     whole = pl.BlockSpec((tokens, model), lambda j: (0, 0))
     return pl.pallas_call(
         functools.partial(project_back_kernel, width),
@@ -304,7 +316,7 @@
         ],
         out_specs=(whole, pl.BlockSpec((2, model), lambda j: (0, 0))),
         scratch_shapes=[pltpu.VMEM((tokens, model), full)],
-        compiler_params=pltpu.CompilerParams(vmem_limit_bytes=58 * 2**20),
+        compiler_params=pltpu.CompilerParams(vmem_limit_bytes=vmem_limit),
         cost_estimate=pl.CostEstimate(
             flops=6 * tokens * model * model, bytes_accessed=6 * model * model, transcendentals=0
         ),
@@ -312,12 +324,12 @@
     )(inputs, gain, grad_middle, received, w_query, w_key, w_value)
 
 
-def middle_kernel(received, inputs, w_out, gain, shift, middle, normed, attended):
-    attended[...] = jnp.concatenate([received[i] for i in range(received.shape[0])], axis=1)
-    rows = inputs[...].astype(full) + matmul(attended[...], w_out[...])
+def middle_kernel(received, inputs, w_out, gain, shift, middle, normed):
+    attended = jnp.concatenate([received[i] for i in range(received.shape[0])], axis=1)
+    rows = inputs[...].astype(full) + matmul(attended, w_out[...])
     middle[...] = rows
     unit, _ = row_stats(rows)
-    normed[...] = (unit * gain[...].astype(full) + shift[...].astype(full)).astype(low)
+    normed[...] = (unit * as_row(gain) + as_row(shift)).astype(low)
 
 
 def attend_out(received, inputs, w_out, gain, shift):
@@ -327,11 +339,10 @@
         out_shape=(
             jax.ShapeDtypeStruct((tokens, model), full),
             jax.ShapeDtypeStruct((tokens, model), low),
-            jax.ShapeDtypeStruct((tokens, model), low),
         ),
         in_specs=[vmem] * 5,
-        out_specs=(vmem, vmem, vmem),
-        compiler_params=pltpu.CompilerParams(vmem_limit_bytes=24 * 2**20),
+        out_specs=(vmem, vmem),
+        compiler_params=pltpu.CompilerParams(vmem_limit_bytes=vmem_limit),
         cost_estimate=pl.CostEstimate(
             flops=2 * tokens * model * model, bytes_accessed=2 * model * model, transcendentals=0
         ),
@@ -340,7 +351,7 @@
 
 
 def hidden(normed, grad_out, w_in, b_in, w_back):
-    inner = matmul(normed, w_in) + b_in.astype(full)
+    inner = matmul(normed, w_in) + as_row(b_in)
     share = 0.5 * (1.0 + lax.erf(inner * 0.7071067811865476))
     density = jnp.exp(inner * inner * -0.5) * 0.3989422804014327
     grad_active = matmul_right(grad_out, w_back)
@@ -372,10 +383,10 @@
 
     @pl.when(step == 0)
     def _():
-        out_total[...] = middle[...] + b_back[...].astype(full)
+        out_total[...] = middle[...] + as_row(b_back)
         grad_total[...] = jnp.zeros_like(grad_total)
 
-    active, grads = hidden(normed[...], grad_out[...], w_in[...], b_in[...], w_back[...])
+    active, grads = hidden(normed[...], grad_out[...], w_in[...], b_in, w_back[...])
     b_in_grad[...] = jnp.sum(grads.astype(full), axis=0, keepdims=True)
     out_total[...] += matmul(active, w_back[...])
     grad_total[...] += matmul_right(grads, w_in[...])
@@ -386,7 +397,7 @@
         grad_normed = grad_total[...]
         unit, rate = row_stats(middle[...])
         grad_full = grad_out[...].astype(full)
-        back = normalize_back(grad_normed, unit, rate, gain[...].astype(full))
+        back = normalize_back(grad_normed, unit, rate, as_row(gain))
         grads_middle = grad_full + back
         grad_middle[...] = grads_middle
         grads_low = grads_middle.astype(low)
@@ -403,7 +414,7 @@
     tokens, model = normed.shape
     ff = w_in.shape[1]
     columns = 512
-    row = pl.BlockSpec((1, model), lambda j: (0, 0))
+    row = pl.BlockSpec((model,), lambda j: (0,))
     whole = pl.BlockSpec((tokens, model), lambda j: (0, 0))
     heads = pl.BlockSpec((groups, tokens, width), lambda j: (0, 0, 0))
     return pl.pallas_call(
@@ -425,7 +436,7 @@
             row,
             row,
             pl.BlockSpec((model, columns), lambda j: (0, j)),
-            pl.BlockSpec((1, columns), lambda j: (0, j)),
+            pl.BlockSpec((columns,), lambda j: (j,)),
             pl.BlockSpec((columns, model), lambda j: (j, 0)),
         ],
         out_specs=(
@@ -437,7 +448,7 @@
             pl.BlockSpec((1, columns), lambda j: (0, j)),
         ),
         scratch_shapes=[pltpu.VMEM((tokens, model), full)] * 2,
-        compiler_params=pltpu.CompilerParams(vmem_limit_bytes=48 * 2**20),
+        compiler_params=pltpu.CompilerParams(vmem_limit_bytes=vmem_limit),
         cost_estimate=pl.CostEstimate(
             flops=8 * tokens * model * ff, bytes_accessed=4 * model * ff, transcendentals=0
         ),
@@ -465,16 +476,20 @@
     return [pl.BlockSpec((2, outer, rows, columns), lambda j, places: (0, 0, 0, 0)), whole, whole]
 
 
+def accumulate(total, value):
+    @pl.when(pl.program_id(0) == 0)
+    def _():
+        total[...] = value.reshape(total.shape)
+
+    @pl.when(pl.program_id(0) > 0)
+    def _():
+        total[...] += value.reshape(total.shape)
+
+
 def product_kernel(places, left, right, sent, own, other, total):
-    step = pl.program_id(0)
-
-    @pl.when(step == 0)
-    def _():
-        total[...] = jnp.zeros_like(total)
-
-    total[...] += matmul_left(left[...], right[...]).reshape(total.shape)
-
-    @pl.when(step == pl.num_programs(0) - 1)
+    accumulate(total, matmul_left(left[...], right[...]))
+
+    @pl.when(pl.program_id(0) == pl.num_programs(0) - 1)
     def _():
         pick_blocks(places[1], total, sent, own, other)
 
@@ -496,7 +511,7 @@
             scratch_shapes=[pltpu.VMEM((outer, 4, rows, columns), full)],
         ),
         out_shape=picked_shapes(outer, rows, columns),
-        compiler_params=pltpu.CompilerParams(vmem_limit_bytes=40 * 2**20),
+        compiler_params=pltpu.CompilerParams(vmem_limit_bytes=vmem_limit),
         cost_estimate=pl.CostEstimate(
             flops=2 * tokens * left_columns * columns,
             bytes_accessed=2 * tokens * (left_columns + columns),
@@ -522,18 +537,11 @@
     in_total,
     back_total,
 ):
-    step = pl.program_id(0)
-
-    @pl.when(step == 0)
-    def _():
-        in_total[...] = jnp.zeros_like(in_total)
-        back_total[...] = jnp.zeros_like(back_total)
-
-    active, grads = hidden(normed[...], grad_out[...], w_in[...], b_in[...], w_back[...])
-    in_total[...] += matmul_left(normed[...], grads).reshape(in_total.shape)
-    back_total[...] += matmul_left(active, grad_out[...]).reshape(back_total.shape)
-
-    @pl.when(step == pl.num_programs(0) - 1)
+    active, grads = hidden(normed[...], grad_out[...], w_in[...], b_in, w_back[...])
+    accumulate(in_total, matmul_left(normed[...], grads))
+    accumulate(back_total, matmul_left(active, grad_out[...]))
+
+    @pl.when(pl.program_id(0) == pl.num_programs(0) - 1)
     def _():
         pick_blocks(places[1], in_total, in_sent, in_own, in_other)
         pick_blocks(places[1], back_total, back_sent, back_own, back_other)
@@ -552,7 +560,7 @@
             grid=(tokens // chunk,),
             in_specs=[
                 pl.BlockSpec((chunk, model), lambda j, places: (j, 0)),
-                pl.BlockSpec((chunk, model), lambda j, places: (j, 1)),
+                pl.BlockSpec((chunk, model), lambda j, places: (j, 0)),
                 pl.BlockSpec((model, columns), lambda j, places: (0, places[0])),
                 pl.BlockSpec((1, columns), lambda j, places: (0, places[0])),
                 pl.BlockSpec((columns, model), lambda j, places: (places[0], 0)),
@@ -564,22 +572,36 @@
             ],
         ),
         out_shape=picked_shapes(seq_count, slim, columns) + picked_shapes(1, back_slim, model),
-        compiler_params=pltpu.CompilerParams(vmem_limit_bytes=48 * 2**20),
+        compiler_params=pltpu.CompilerParams(vmem_limit_bytes=vmem_limit),
         cost_estimate=pl.CostEstimate(
             flops=8 * tokens * model * columns,
             bytes_accessed=4 * tokens * model + 4 * model * columns,
             transcendentals=0,
         ),
         name="feed_products",
-    )(places, normed, kept, w_in, b_in, w_back)
+    )(places, normed, kept, w_in, b_in.reshape(1, -1), w_back)
 
 
 def swap(blocks, axes):
     return lax.all_to_all(blocks, axes, split_axis=0, concat_axis=0, tiled=True)
 
 
-def gather_rows(rows, axis):
-    return lax.all_gather(rows, axis, axis=0, tiled=True)
+def gather_rows(rows):
+    return lax.all_gather(rows, "seq", axis=0, tiled=True)
+
+
+def gather_parts(rows):
+    count = lax.axis_size("seq")
+
+    def move(block, distance):
+        return lax.ppermute(block, "seq", [(i, i ^ distance) for i in range(count)])
+
+    parts = [rows, None] + [None] * (count - 2)
+    for distance in range(2, count, 2):
+        parts[distance] = move(rows, distance)
+    for distance in range(0, count, 2):
+        parts[distance + 1] = move(parts[distance], 1)
+    return parts
 
 
 def trade(block, distance):
@@ -640,78 +662,87 @@
     def to_tokens(rows):
         return swap(rows.reshape(seq_count, token_count, -1), "seq")[::copies]
 
-    def one_row(vector):
-        return vector.reshape(1, -1)
-
     rows_in, grad_out = inputs[0], cotangent[0]
-    gain_one, gain_two = one_row(ln1_gain), one_row(ln2_gain)
+    gain_one, gain_two = ln1_gain, ln2_gain
     places = jnp.stack([lax.axis_index("seq"), lax.axis_index("batch")]).astype(jnp.int32)
-    sent, kept = project(
-        rows_in, grad_out, gain_one, one_row(ln1_shift), w_query, w_key, w_value, head_groups, width
-    )
-    qkv, kept = together(to_heads(sent), kept)
-    kept_all = gather_rows(kept, "seq")
+    parts = gather_parts(rows_in)
+    qkv, normed_all = project(
+        places, parts, gain_one, ln1_shift, w_query, w_key, w_value, width, copies
+    )
+    late_grad_out, qkv = together(grad_out, qkv)
+    grad_out_all = gather_rows(late_grad_out)
     attended_all, log_total = attend(tables, qkv, block_count, head_count, scale)
-    middle, normed_two, attended = attend_out(
-        to_tokens(attended_all), rows_in, w_out, gain_two, one_row(ln2_shift)
-    )
-    normed_two_all = gather_rows(normed_two, "seq")
+    middle, normed_two = attend_out(
+        to_tokens(attended_all), rows_in, w_out, gain_two, ln2_shift
+    )
+    normed_two_all = gather_rows(normed_two)
     output, grad_middle, grad_middle_low, grad_attended, gain_two_grads, grad_b_in = feed(
         normed_two,
         middle,
         grad_out,
         w_out,
         gain_two,
-        one_row(b_back),
+        b_back,
         w_in,
-        one_row(b_in),
+        b_in,
         w_back,
         head_groups,
         width,
     )
-    out_blocks = product(places, attended, model_width, grad_middle_low, seq_count, "out_product")
-    grad_rows, out_blocks = together(to_heads(grad_attended), out_blocks)
-    out_got = trade(out_blocks[0], 1)
+    grad_middle_all = gather_rows(grad_middle_low)
+    grad_rows, grad_out_all = together(to_heads(grad_attended), grad_out_all)
     grad_qkv = attend_back(tables, qkv, log_total, grad_rows, block_count, head_count, scale)
-    out_own, out_other = first_sum(out_got, *out_blocks[1:])
-    out_last = trade(out_other, 2)
     grad_qkv_near = to_tokens(grad_qkv)
 
     slim = model_width // device_count
     inner_columns = ff_width // seq_count
-    qkv_blocks = product(places, kept_all, model_width, grad_qkv, seq_count, "qkv_product")
-    qkv_got = trade(qkv_blocks[0], 1)
+    qkv_sent, qkv_own, qkv_other = product(
+        places, normed_all, model_width, grad_qkv, seq_count, "qkv_product"
+    )
+    qkv_got = trade(qkv_sent, 1)
+    normed_two_all, qkv_own = together(normed_two_all, qkv_own)
     in_sent, in_own, in_other, back_sent, back_own, back_other = feed_products(
-        places, normed_two_all, kept_all, w_in, one_row(b_in), w_back, seq_count
-    )
-    qkv_got, grad_qkv_near, in_sent, back_sent, out_last = together(
-        qkv_got, grad_qkv_near, in_sent, back_sent, out_last
-    )
-    qkv_own, qkv_other = first_sum(qkv_got, *qkv_blocks[1:])
+        places, normed_two_all, grad_out_all, w_in, b_in, w_back, seq_count
+    )
+    in_got = trade(in_sent, 1)
+    qkv_got, in_own = together(qkv_got, in_own)
+    qkv_own, qkv_other = first_sum(qkv_got, qkv_own, qkv_other)
+    grad_qkv_near, qkv_other = together(grad_qkv_near, qkv_other)
     qkv_last = trade(qkv_other, 2)
-    in_got = trade(in_sent, 1)
-    back_got = trade(back_sent, 1)
     input_grad, gain_one_grads = project_back(
         rows_in, gain_one, grad_middle, grad_qkv_near, w_query, w_key, w_value
     )
-    in_got, back_got, qkv_last, gain_one_grads = together(in_got, back_got, qkv_last, gain_one_grads)
+    in_got, qkv_last, back_sent, input_grad, gain_one_grads = together(
+        in_got, qkv_last, back_sent, input_grad, gain_one_grads
+    )
     in_own, in_other = first_sum(in_got, in_own, in_other)
     in_last = trade(in_other, 2)
+    back_got = trade(back_sent, 1)
+    own_rows = width // copies
+    own_attended, in_own = together(attended_all, in_own)
+    if copies > 1:
+        at = lax.axis_index("seq") % copies * own_rows
+        own_attended = lax.dynamic_slice_in_dim(own_attended, at, own_rows, axis=1)
+    out_sent, out_own, out_other = product(
+        places, own_attended, own_rows, grad_middle_all, 1, "out_product"
+    )
+    in_last, back_got, out_sent, gain_one_grads = together(in_last, back_got, out_sent, gain_one_grads)
+    out_got = trade(out_sent, 1)
     back_own, back_other = first_sum(back_got, back_own, back_other)
     back_rows = (back_own + trade(back_other, 2).astype(full))[0]
+    out_own, out_other = first_sum(out_got, out_own, out_other)
+    out_rows = (out_own + trade(out_other, 2).astype(full))[0]
 
     mixed = [
         (own + last.astype(full)).astype(low)
-        for own, last in ((in_own, in_last), (qkv_own, qkv_last), (out_own, out_last))
+        for own, last in ((in_own, in_last), (qkv_own, qkv_last))
     ]
     mixed = swap(jnp.concatenate(mixed, axis=2), "seq")
-    at = inner_columns + 3 * width
     in_rows = mixed[:, :, :inner_columns].transpose(1, 0, 2).reshape(slim, ff_width).astype(full)
-    qkv_rows = mixed[::copies, :, inner_columns:at].transpose(1, 0, 2).astype(full)
+    qkv_rows = mixed[::copies, :, inner_columns:].transpose(1, 0, 2).astype(full)
     qkv_rows = [
         qkv_rows[:, :, i * width : (i + 1) * width].reshape(slim, model_width) for i in range(3)
     ]
-    out_rows = jnp.sum(mixed[:, :, at:].astype(full), axis=0)
     small = [gain_one_grads[0], gain_one_grads[1], *gain_two_grads, grad_b_in[0]]
     packed = jnp.concatenate([v.reshape(device_count, -1) for v in small], axis=1)
     packed = jnp.sum(swap(packed, ("seq", "batch")), axis=0)

time: 226 us -> 209 us (0.925)
  local copies, waits for them, and re-layouts: 21.5 us -> 7.68 us
  Pallas kernels: 68.9 us -> 81.3 us
  other arithmetic: 11.5 us -> 3.54 us
  starting transfers between devices: 33.8 us -> 29 us
  waiting for transfers between devices: 51.7 us -> 48.7 us
    ppermute x0 -> x7, waiting for transfers between devices: none -> 18.8 us  [move(): return lax.ppermute(block, 'seq', [(i, i ^ distance) for i in range(count)])]
    ppermute x8, waiting for transfers between devices: 36.1 us -> 22.7 us  [trade(): return lax.ppermute(block, 'batch', [(i, i ^ distance) for i in range(4)])]
    unnamed x57, local copies, waits for them, and re-layouts: 14.3 us -> 2.52 us
    all_to_all x5 -> x3, starting transfers between devices: 22 us -> 11.7 us  [swap(): return lax.all_to_all(blocks, axes, split_axis=0, concat_axis=0, tiled=True)]
    all_to_all x5 -> x3, waiting for transfers between devices: 15.6 us -> 7.14 us  [swap(): return lax.all_to_all(blocks, axes, split_axis=0, concat_axis=0, tiled=True)]
    ppermute x0 -> x7, starting transfers between devices: none -> 5.05 us  [move(): return lax.ppermute(block, 'seq', [(i, i ^ distance) for i in range(count)])]
    pallas_call x2, Pallas kernels: 5.87 us -> 10.8 us  [product(): pl.pallas_call(product_kernel, grid_spec=pltpu.PrefetchScalarGridSpec(num...]
    convert_element_type x3 -> x2, other arithmetic: 4.34 us -> 0.15 us  [shards(): (own + last.astype(full)).astype(low)]
  transfers between devices with their start and end apart: 15 -> 21, of which waited for: 9 -> 10; matrix products, arithmetic and copies ran while one was open for 5% -> 3% of each run, Pallas kernels for 28% -> 35%
where the time goes in v3:
time: 209 us; the launch traced here: 208 us
  Pallas kernels  81.3 us (39%)
  waiting for transfers between devices  48.7 us (23%)
  starting transfers between devices  29 us (14%)
  blocking collectives  23.1 us (11%)
  between operations  14.8 us (7%)
  local copies, waits for them, and re-layouts  7.68 us (4%)
  other arithmetic  3.54 us (2%)
    all_to_all x2, blocking collectives, swap(): return lax.all_to_all(blocks, axes, split_axis=0, concat_axis=0, tiled=True)  23.1 us
    ppermute x8, waiting for transfers between devices, trade(): return lax.ppermute(block, 'batch', [(i, i ^ distance) for i in range(4)])  22.7 us
    ppermute x7, waiting for transfers between devices, move(): return lax.ppermute(block, 'seq', [(i, i ^ distance) for i in range(count)])  18.8 us
    pallas_call x1, Pallas kernels, feed(): pl.pallas_call(feed_kernel, grid=(ff // columns,), out_shape=(jax.ShapeDt...  17.1 us
    pallas_call x1, Pallas kernels, feed_products(): pl.pallas_call(feed_products_kernel, grid_spec=pltpu.PrefetchScalarGridSp...  13.6 us
    ppermute x8, starting transfers between devices, trade(): return lax.ppermute(block, 'batch', [(i, i ^ distance) for i in range(4)])  12.2 us
    pallas_call x1, Pallas kernels, attend_back(): pl.pallas_call(functools.partial(attend_back_kernel, block_count, head_co...  12.1 us
    all_to_all x3, starting transfers between devices, swap(): return lax.all_to_all(blocks, axes, split_axis=0, concat_axis=0, tiled=True)  11.7 us
  transfers between devices with their start and end apart: 21, of which 10 were waited for; matrix products, arithmetic and copies ran while one was open for 3% of the time, Pallas kernels for 35%

profile of v3, /device:TPU:0, one launch (start us, length us, event | category | flops | bytes accessed | tf_op | source)
XLA Modules:
  0.0 208.1 jit_solution(1370119961045547486)
XLA Ops:
  7.2 3.0 %collective-permute-start.1 = (bf16[192,1024]{1,0:T(8,128)(2,1)}, bf16[192,1024]{1,0:T(8,128)(2,1)S(1)}, u32[]{:S(2)}, u32[]{:S(2)}) collective-permute-start(bf16[192,1024]{1,0:T(8,128)(2,1)} %bitcast.63), channel_id=1, source_target_pairs={{0,8},{4,12},{8,0},{12,4},{16,24},{20,28},{24,16},{28,20},{1,9},{5... | collective-permute-start | bytes 1179656 | tf_op jit(solution)/shard_map/ppermute | solution.py:597
  11.8 8.6 %collective-permute-done.1.refs_2_ = bf16[192,1024]{1,0:T(8,128)(2,1)S(1)} collective-permute-done((bf16[192,1024]{1,0:T(8,128)(2,1)}, bf16[192,1024]{1,0:T(8,128)(2,1)S(1)}, u32[]{:S(2)}, u32[]{:S(2)}) %collective-permute-start.1) | collective-permute-done | bytes 393248 | tf_op jit(solution)/shard_map/ppermute | solution.py:597
  20.4 9.1 %collective-permute-done.3.refs_4_ = bf16[192,1024]{1,0:T(8,128)(2,1)S(1)} collective-permute-done((bf16[192,1024]{1,0:T(8,128)(2,1)}, bf16[192,1024]{1,0:T(8,128)(2,1)S(1)}, u32[]{:S(2)}, u32[]{:S(2)}) %collective-permute-start.3) | collective-permute-done | bytes 393248 | tf_op jit(solution)/shard_map/ppermute | solution.py:597
  32.7 7.7 %project.1 = (bf16[1536,384]{1,0:T(8,128)(2,1)}, bf16[1536,1024]{1,0:T(8,128)(2,1)}) custom-call(s32[2]{0:T(128)} %pad_add_fusion.places, bf16[192,1024]{1,0:T(8,128)(2,1)} %bitcast.67, bf16[192,1024]{1,0:T(8,128)(2,1)} %copy-done.8, bf16[192,1024]{1,0:T(8,128)(2,1)} %copy-done.5, bf16[192,1024]{1,0:T(8,128)(2,1)} %copy-done.9, bf16[192,1024]{1,0:T(8,128)(2,1)} %copy-done.6, ...), custom_call_target="tpu_custom_call" | custom-call | flops 1207959552 | bytes 6291456 | tf_op jit(solution)/shard_map/project/pallas_call | solution.py:241
  42.6 9.2 %attend.1 = (bf16[1536,128]{1,0:T(8,128)(2,1)S(1)}, f32[24,1,128]{2,1,0:T(1,128)S(1)}) custom-call(s32[1,1]{1,0:T(1,128)S(6)} %copy.60.lens, s32[1,24,3]{2,1,0:T(8,128)S(1)} %copy.44.owners, s32[1,24,3]{2,1,0:T(8,128)S(1)} %copy.45.offsets, s32[1,1,2]{2,1,0:T(1,128)S(1)} %copy-done.3, bf16[1536,384]{1,0:T(8,128)(2,1)S(1)} %copy-done.1), custom_call_target="tpu_custom_call" | custom-call | flops 805306368 | bytes 1572864 | tf_op jit(solution)/shard_map/attend/pallas_call | solution.py:170
  51.9 11.4 %all_to_all.29.received = bf16[8,192,128]{2,1,0:T(8,128)(2,1)} all-to-all(bf16[8,192,128]{2,1,0:T(8,128)(2,1)S(1)} %bitcast.61), channel_id=1, replica_groups=mesh['seq'=8,'batch'=4] {'seq'}, dimensions={0} | all-to-all | bytes 786432 | tf_op jit(solution)/shard_map/all_to_all | solution.py:586
  63.3 3.5 %attend_out.1 = (f32[192,1024]{1,0:T(8,128)}, bf16[192,1024]{1,0:T(8,128)(2,1)}) custom-call(bf16[8,192,128]{2,1,0:T(8,128)(2,1)} %all_to_all.29.received, bf16[192,1024]{1,0:T(8,128)(2,1)} %bitcast.68, bf16[1024,1024]{1,0:T(8,128)(2,1)} %w_out.3, bf16[1024]{0:T(1024)(128)(2,1)} %gain.4, bf16[1024]{0:T(1024)(128)(2,1)} %shift.1), custom_call_target="tpu_custom_call" | custom-call | flops 402653184 | bytes 2097152 | tf_op jit(solution)/shard_map/attend_out/pallas_call | solution.py:337
  66.8 17.1 %feed.1 = (bf16[192,1024]{1,0:T(8,128)(2,1)}, f32[192,1024]{1,0:T(8,128)}, bf16[192,1024]{1,0:T(8,128)(2,1)}, bf16[8,192,128]{2,1,0:T(8,128)(2,1)}, f32[3,1024]{1,0:T(4,128)}, /*index=5*/f32[1,4096]{1,0:T(1,128)}) custom-call(bf16[192,1024]{1,0:T(8,128)(2,1)} %get-tuple-element.64.normed, f32[192,1024]{1,0:T(8,128)} %get-tuple-element.65.middle, ...), custom_call_target="tpu_custom_call" | custom-call | flops 6442450944 | bytes 16777216 | tf_op jit(solution)/shard_map/feed/pallas_call | solution.py:420
  83.9 11.7 %all_to_all.30 = bf16[8,192,128]{2,1,0:T(8,128)(2,1)S(1)} all-to-all(bf16[8,192,128]{2,1,0:T(8,128)(2,1)} %get-tuple-element.69), channel_id=1, replica_groups=mesh['seq'=8,'batch'=4] {'seq'}, dimensions={0} | all-to-all | bytes 786432 | tf_op jit(solution)/shard_map/all_to_all | solution.py:586
  95.7 12.1 %attend_back.1.right = bf16[1536,384]{1,0:T(8,128)(2,1)} custom-call(s32[1,1]{1,0:T(1,128)S(6)} %copy.60.lens, s32[1,24,3]{2,1,0:T(8,128)S(1)} %copy.44.owners, s32[1,24,3]{2,1,0:T(8,128)S(1)} %copy.45.offsets, s32[1,1,2]{2,1,0:T(1,128)S(1)} %copy-done.3, bf16[1536,384]{1,0:T(8,128)(2,1)S(1)} %copy-done.2, f32[24,1,128]{2,1,0:T(1,128)S(1)} %get-tuple-element.68.log_total, ...), custom_call_target="tpu_custom_call" | custom-call | flops 2013265920 | bytes 3145728 | tf_op jit(solution)/shard_map/attend_back/pallas_call | solution.py:189
  107.8 3.9 %all-to-all-start.2 = ((bf16[8,192,384]{2,1,0:T(8,128)(2,1)}), bf16[8,192,384]{2,1,0:T(8,128)(2,1)S(1)}, u32[]{:S(2)}, u32[]{:S(2)}) async-start(bf16[8,192,384]{2,1,0:T(8,128)(2,1)} %bitcast.7), calls=%async_computation.2 | async-start | bytes 2359296 | tf_op jit(solution)/shard_map/all_to_all | solution.py:586
  112.3 6.1 %qkv_product.1 = (bf16[2,8,32,384]{3,2,1,0:T(8,128)(2,1)}, bf16[8,32,384]{2,1,0:T(8,128)(2,1)}, bf16[8,32,384]{2,1,0:T(8,128)(2,1)}) custom-call(s32[2]{0:T(128)} %pad_add_fusion.places, bf16[1536,1024]{1,0:T(8,128)(2,1)} %get-tuple-element.67.left, bf16[1536,384]{1,0:T(8,128)(2,1)} %attend_back.1.right), custom_call_target="tpu_custom_call" | custom-call | flops 1207959552 | bytes 4325376 | tf_op jit(solution)/shard_map/qkv_product/pallas_call | solution.py:501
  119.9 13.6 %feed_products.1 = (bf16[2,8,32,512]{3,2,1,0:T(8,128)(2,1)}, bf16[8,32,512]{2,1,0:T(8,128)(2,1)}, bf16[8,32,512]{2,1,0:T(8,128)(2,1)}, bf16[2,1,128,1024]{3,2,1,...) custom-call(s32[2]{0:T(128)} %pad_add_fusion.places, ...), custom_call_target="tpu_custom_call" | custom-call | flops 6442450944 | bytes 8388608 | tf_op jit(solution)/shard_map/feed_products/pallas_call | solution.py:556
  134.1 2.6 %collective-permute-start.9 = (bf16[8,32,384]{2,1,0:T(8,128)(2,1)S(1)}, bf16[8,32,384]{2,1,0:T(8,128)(2,1)S(1)}, u32[]{:S(2)}, u32[]{:S(2)}) collective-permute-start(bf16[8,32,384]{2,1,0:T(8,128)(2,1)S(1)} %fusion.6), channel_id=1, source_target_pairs={{0,2},{1,3},{2,0},{3,1},{4,6},{5,7},{6,4},{7,5},{8,10},{9,11},{10,... | collective-permute-start | bytes 589832 | tf_op jit(solution)/shard_map/ppermute | solution.py:608
  136.9 7.3 %project_back.1 = (bf16[192,1024]{1,0:T(8,128)(2,1)}, f32[2,1024]{1,0:T(2,128)}) custom-call(bf16[192,1024]{1,0:T(8,128)(2,1)} %bitcast.69, bf16[1024]{0:T(1024)(128)(2,1)} %gain.5, f32[192,1024]{1,0:T(8,128)} %get-tuple-element.82.grad_middle, bf16[8,192,384]{2,1,0:T(8,128)(2,1)} %copy-done.4, bf16[1024,1024]{1,0:T(8,128)(2,1)} %w_query.1, ...), custom_call_target="tpu_custom_call" | custom-call | flops 1207959552 | bytes 6291456 | tf_op jit(solution)/shard_map/project_back/pallas_call | solution.py:301
  144.2 7.5 %collective-permute-done.7 = bf16[2,8,32,512]{3,2,1,0:T(8,128)(2,1)S(1)} collective-permute-done((bf16[2,8,32,512]{3,2,1,0:T(8,128)(2,1)}, bf16[2,8,32,512]{3,2,1,0:T(8,128)(2,1)S(1)}, u32[]{:S(2)}, u32[]{:S(2)}) %collective-permute-start.7) | collective-permute-done | bytes 524320 | tf_op jit(solution)/shard_map/ppermute | solution.py:608
  151.7 2.6 %collective-permute-start.11 = (bf16[2,1,128,1024]{3,2,1,0:T(8,128)(2,1)S(1)}, bf16[2,1,128,1024]{3,2,1,0:T(8,128)(2,1)S(1)}, u32[]{:S(2)}, u32[]{:S(2)}) collective-permute-start(bf16[2,1,128,1024]{3,2,1,0:T(8,128)(2,1)S(1)} %copy-done.26), channel_id=1, source_target_pairs={{0,1},{1,0},{2,3},{3,2},{4,5},{5,4},{6,7},{7,6},{8,9},{9,8},{10,11... | collective-permute-start | bytes 1572872 | tf_op jit(solution)/shard_map/ppermute | solution.py:608
  155.0 4.8 %out_product.1 = (bf16[2,1,32,1024]{3,2,1,0:T(8,128)(2,1)}, bf16[1,32,1024]{2,1,0:T(8,128)(2,1)}, bf16[1,32,1024]{2,1,0:T(8,128)(2,1)}) custom-call(s32[2]{0:T(128)} %pad_add_fusion.places, bf16[1536,128]{1,0:T(8,128)(2,1)} %copy-done, bf16[1536,1024]{1,0:T(8,128)(2,1)} %all-gather.8.cloned.1.call-done.right), custom_call_target="tpu_custom_call" | custom-call | flops 402653184 | bytes 3538944 | tf_op jit(solution)/shard_map/out_product/pallas_call | solution.py:501
  159.8 10.5 %collective-permute-done.10 = bf16[8,32,512]{2,1,0:T(8,128)(2,1)S(1)} collective-permute-done((bf16[8,32,512]{2,1,0:T(8,128)(2,1)S(1)}, bf16[8,32,512]{2,1,0:T(8,128)(2,1)S(1)}, u32[]{:S(2)}, u32[]{:S(2)}) %collective-permute-start.10) | collective-permute-done | bytes 262176 | tf_op jit(solution)/shard_map/ppermute | solution.py:608
  171.2 2.7 %collective-permute-start.14 = (bf16[1,128,1024]{2,1,0:T(8,128)(2,1)S(1)}, bf16[1,128,1024]{2,1,0:T(8,128)(2,1)S(1)}, u32[]{:S(2)}, u32[]{:S(2)}) collective-permute-start(bf16[1,128,1024]{2,1,0:T(8,128)(2,1)S(1)} %fusion), channel_id=1, source_target_pairs={{0,2},{1,3},{2,0},{3,1},{4,6},{5,7},{6,4},{7,5},{8,10},{9,11},{10,... | collective-permute-start | bytes 786440 | tf_op jit(solution)/shard_map/ppermute | solution.py:608
  174.8 4.3 %all-to-all-start.3 = ((f32[32,1,288]{2,1,0:T(1,128)}), f32[32,1,288]{2,1,0:T(1,128)S(1)}, u32[]{:S(2)}, u32[]{:S(2)}) async-start(f32[32,1,288]{2,1,0:T(1,128)} %all_to_all.21), calls=%async_computation.3 | async-start | bytes 98304 | tf_op jit(solution)/shard_map/all_to_all | solution.py:586
  180.1 6.7 %all-to-all-done.3 = f32[32,1,288]{2,1,0:T(1,128)S(1)} async-done(((f32[32,1,288]{2,1,0:T(1,128)}), f32[32,1,288]{2,1,0:T(1,128)S(1)}, u32[]{:S(2)}, u32[]{:S(2)}) %all-to-all-start.3) | async-done | bytes 36896 | tf_op jit(solution)/shard_map/all_to_all | solution.py:586
  186.7 3.5 %all-to-all-start.4 = ((bf16[8,32,896]{2,1,0:T(8,128)(2,1)}), bf16[8,32,896]{2,1,0:T(8,128)(2,1)S(1)}, u32[]{:S(2)}, u32[]{:S(2)}) async-start(bf16[8,32,896]{2,1,0:T(8,128)(2,1)} %pad_maximum_fusion), calls=%async_computation.4 | async-start | bytes 917504 | tf_op jit(solution)/shard_map/all_to_all | solution.py:586
  193.2 3.9 %collective-permute-done.13 = bf16[1,32,1024]{2,1,0:T(8,128)(2,1)S(1)} collective-permute-done((bf16[1,32,1024]{2,1,0:T(8,128)(2,1)S(1)}, bf16[1,32,1024]{2,1,0:T(8,128)(2,1)S(1)}, u32[]{:S(2)}, u32[]{:S(2)}) %collective-permute-start.13) | collective-permute-done | bytes 65568 | tf_op jit(solution)/shard_map/ppermute | solution.py:608
  (117 shorter events, 20.1 us)
Async XLA Ops:
  7.2 88.5 %all-gather.6.cloned.1.call-start = ((), (), s32[]{:S(2)}) async-start(), calls=%async_computation.6 | async-start | bytes 3538944 | tf_op jit(solution)/shard_map/all_gather | solution.py:590
  7.2 13.2 %collective-permute-start.1 = (bf16[192,1024]{1,0:T(8,128)(2,1)}, bf16[192,1024]{1,0:T(8,128)(2,1)S(1)}, u32[]{:S(2)}, u32[]{:S(2)}) collective-permute-start(bf16[192,1024]{1,0:T(8,128)(2,1)} %bitcast.63), channel_id=1, source_target_pairs={{0,8},{4,12},{8,0},{12,4},{16,24},{20,28},{24,16},{28,20},{1,9},{5... | collective-permute-start | bytes 1179656 | tf_op jit(solution)/shard_map/ppermute | solution.py:597
  10.2 19.2 %collective-permute-start.3 = (bf16[192,1024]{1,0:T(8,128)(2,1)}, bf16[192,1024]{1,0:T(8,128)(2,1)S(1)}, u32[]{:S(2)}, u32[]{:S(2)}) collective-permute-start(bf16[192,1024]{1,0:T(8,128)(2,1)} %bitcast.64), channel_id=1, source_target_pairs={{0,16},{4,20},{8,24},{12,28},{16,0},{20,4},{24,8},{28,12},{1,17},{... | collective-permute-start | bytes 1179656 | tf_op jit(solution)/shard_map/ppermute | solution.py:597
  11.7 17.7 %collective-permute-start.5 = (bf16[192,1024]{1,0:T(8,128)(2,1)}, bf16[192,1024]{1,0:T(8,128)(2,1)S(1)}, u32[]{:S(2)}, u32[]{:S(2)}) collective-permute-start(bf16[192,1024]{1,0:T(8,128)(2,1)} %bitcast.65), channel_id=1, source_target_pairs={{0,24},{4,28},{8,16},{12,20},{16,8},{20,12},{24,0},{28,4},{1,25},{... | collective-permute-start | bytes 1179656 | tf_op jit(solution)/shard_map/ppermute | solution.py:597
  11.8 18.8 %collective-permute-start = (bf16[192,1024]{1,0:T(8,128)(2,1)}, bf16[192,1024]{1,0:T(8,128)(2,1)S(1)}, u32[]{:S(2)}, u32[]{:S(2)}) collective-permute-start(bf16[192,1024]{1,0:T(8,128)(2,1)} %bitcast.66), channel_id=1, source_target_pairs={{0,4},{4,0},{8,12},{12,8},{16,20},{20,16},{24,28},{28,24},{1,5},{5... | collective-permute-start | bytes 1179656 | tf_op jit(solution)/shard_map/ppermute | solution.py:597
  20.4 10.2 %collective-permute-start.2 = (bf16[192,1024]{1,0:T(8,128)(2,1)S(1)}, bf16[192,1024]{1,0:T(8,128)(2,1)S(1)}, u32[]{:S(2)}, u32[]{:S(2)}) collective-permute-start(bf16[192,1024]{1,0:T(8,128)(2,1)S(1)} %collective-permute-done.1.refs_2_), channel_id=1, source_target_pairs={{0,4},{4,0},{8,12},{12,8},{16,20},{20,16},{24,28},{28,24},{1,5},{5... | collective-permute-start | bytes 1179656 | tf_op jit(solution)/shard_map/ppermute | solution.py:597
  29.4 1.7 collective-permute-start.4
  29.5 2.3 %collective-permute-start.6 = (bf16[192,1024]{1,0:T(8,128)(2,1)S(1)}, bf16[192,1024]{1,0:T(8,128)(2,1)S(1)}, u32[]{:S(2)}, u32[]{:S(2)}) collective-permute-start(bf16[192,1024]{1,0:T(8,128)(2,1)S(1)} %collective-permute-done.5.refs_6_), channel_id=1, source_target_pairs={{0,4},{4,0},{8,12},{12,8},{16,20},{20,16},{24,28},{28,24},{1,5},{5... | collective-permute-start | bytes 1179656 | tf_op jit(solution)/shard_map/ppermute | solution.py:597
  40.4 79.4 %all-gather.4.cloned.1.call-start = ((), (), s32[]{:S(2)}) async-start(), calls=%async_computation.5 | async-start | bytes 3538944 | tf_op jit(solution)/shard_map/all_gather | solution.py:590
  51.9 32.1 %copy-start = (bf16[1536,128]{1,0:T(8,128)(2,1)}, bf16[1536,128]{1,0:T(8,128)(2,1)S(1)}, u32[]{:S(2)}) copy-start(bf16[1536,128]{1,0:T(8,128)(2,1)S(1)} %get-tuple-element.91.left) | copy-start | bytes 1179652
  66.8 88.2 %all-gather.8.cloned.1.call-start = ((), (), s32[]{:S(2)}) async-start(), calls=%async_computation.7 | async-start | bytes 3538944 | tf_op jit(solution)/shard_map/all_gather | solution.py:590
  66.8 28.8 %copy-start.2 = (bf16[1536,384]{1,0:T(8,128)(2,1)S(1)}, bf16[1536,384]{1,0:T(8,128)(2,1)}, u32[]{:S(2)}) copy-start(bf16[1536,384]{1,0:T(8,128)(2,1)} %get-tuple-element.62.qkv) | copy-start | bytes 3538948
  107.8 26.3 %all-to-all-start.2 = ((bf16[8,192,384]{2,1,0:T(8,128)(2,1)}), bf16[8,192,384]{2,1,0:T(8,128)(2,1)S(1)}, u32[]{:S(2)}, u32[]{:S(2)}) async-start(bf16[8,192,384]{2,1,0:T(8,128)(2,1)} %bitcast.7), calls=%async_computation.2 | async-start | bytes 2359296 | tf_op jit(solution)/shard_map/all_to_all | solution.py:586
  118.3 15.6 %collective-permute-start.8 = (bf16[2,8,32,384]{3,2,1,0:T(8,128)(2,1)}, bf16[2,8,32,384]{3,2,1,0:T(8,128)(2,1)S(1)}, u32[]{:S(2)}, u32[]{:S(2)}) collective-permute-start(bf16[2,8,32,384]{3,2,1,0:T(8,128)(2,1)} %get-tuple-element.77), channel_id=1, source_target_pairs={{0,1},{1,0},{2,3},{3,2},{4,5},{5,4},{6,7},{7,6},{8,9},{9,8},{10,11... | collective-permute-start | bytes 1179656 | tf_op jit(solution)/shard_map/ppermute | solution.py:608
  133.5 18.2 %collective-permute-start.7 = (bf16[2,8,32,512]{3,2,1,0:T(8,128)(2,1)}, bf16[2,8,32,512]{3,2,1,0:T(8,128)(2,1)S(1)}, u32[]{:S(2)}, u32[]{:S(2)}) collective-permute-start(bf16[2,8,32,512]{3,2,1,0:T(8,128)(2,1)} %get-tuple-element.75), channel_id=1, source_target_pairs={{0,1},{1,0},{2,3},{3,2},{4,5},{5,4},{6,7},{7,6},{8,9},{9,8},{10,11... | collective-permute-start | bytes 1572872 | tf_op jit(solution)/shard_map/ppermute | solution.py:608
  134.1 17.6 %collective-permute-start.9 = (bf16[8,32,384]{2,1,0:T(8,128)(2,1)S(1)}, bf16[8,32,384]{2,1,0:T(8,128)(2,1)S(1)}, u32[]{:S(2)}, u32[]{:S(2)}) collective-permute-start(bf16[8,32,384]{2,1,0:T(8,128)(2,1)S(1)} %fusion.6), channel_id=1, source_target_pairs={{0,2},{1,3},{2,0},{3,1},{4,6},{5,7},{6,4},{7,5},{8,10},{9,11},{10,... | collective-permute-start | bytes 589832 | tf_op jit(solution)/shard_map/ppermute | solution.py:608
  151.7 19.4 %collective-permute-start.11 = (bf16[2,1,128,1024]{3,2,1,0:T(8,128)(2,1)S(1)}, bf16[2,1,128,1024]{3,2,1,0:T(8,128)(2,1)S(1)}, u32[]{:S(2)}, u32[]{:S(2)}) collective-permute-start(bf16[2,1,128,1024]{3,2,1,0:T(8,128)(2,1)S(1)} %copy-done.26), channel_id=1, source_target_pairs={{0,1},{1,0},{2,3},{3,2},{4,5},{5,4},{6,7},{7,6},{8,9},{9,8},{10,11... | collective-permute-start | bytes 1572872 | tf_op jit(solution)/shard_map/ppermute | solution.py:608
  154.5 15.9 %collective-permute-start.10 = (bf16[8,32,512]{2,1,0:T(8,128)(2,1)S(1)}, bf16[8,32,512]{2,1,0:T(8,128)(2,1)S(1)}, u32[]{:S(2)}, u32[]{:S(2)}) collective-permute-start(bf16[8,32,512]{2,1,0:T(8,128)(2,1)S(1)} %get-tuple-element.114), channel_id=1, source_target_pairs={{0,2},{1,3},{2,0},{3,1},{4,6},{5,7},{6,4},{7,5},{8,10},{9,11},{10,... | collective-permute-start | bytes 786440 | tf_op jit(solution)/shard_map/ppermute | solution.py:608
  159.8 30.5 %copy-start.19 = (bf16[1,32,1024]{2,1,0:T(8,128)(2,1)S(1)}, bf16[1,32,1024]{2,1,0:T(8,128)(2,1)}, u32[]{:S(2)}) copy-start(bf16[1,32,1024]{2,1,0:T(8,128)(2,1)} %get-tuple-element.104) | copy-start | bytes 196612
  171.2 26.6 %collective-permute-start.14 = (bf16[1,128,1024]{2,1,0:T(8,128)(2,1)S(1)}, bf16[1,128,1024]{2,1,0:T(8,128)(2,1)S(1)}, u32[]{:S(2)}, u32[]{:S(2)}) collective-permute-start(bf16[1,128,1024]{2,1,0:T(8,128)(2,1)S(1)} %fusion), channel_id=1, source_target_pairs={{0,2},{1,3},{2,0},{3,1},{4,6},{5,7},{6,4},{7,5},{8,10},{9,11},{10,... | collective-permute-start | bytes 786440 | tf_op jit(solution)/shard_map/ppermute | solution.py:608
  173.9 16.4 %collective-permute-start.12 = (bf16[2,1,32,1024]{3,2,1,0:T(8,128)(2,1)}, bf16[2,1,32,1024]{3,2,1,0:T(8,128)(2,1)S(1)}, u32[]{:S(2)}, u32[]{:S(2)}) collective-permute-start(bf16[2,1,32,1024]{3,2,1,0:T(8,128)(2,1)} %get-tuple-element.103), channel_id=1, source_target_pairs={{0,1},{1,0},{2,3},{3,2},{4,5},{5,4},{6,7},{7,6},{8,9},{9,8},{10,11... | collective-permute-start | bytes 393224 | tf_op jit(solution)/shard_map/ppermute | solution.py:608
  174.8 11.9 %all-to-all-start.3 = ((f32[32,1,288]{2,1,0:T(1,128)}), f32[32,1,288]{2,1,0:T(1,128)S(1)}, u32[]{:S(2)}, u32[]{:S(2)}) async-start(f32[32,1,288]{2,1,0:T(1,128)} %all_to_all.21), calls=%async_computation.3 | async-start | bytes 98304 | tf_op jit(solution)/shard_map/all_to_all | solution.py:586
  186.7 12.5 %all-to-all-start.4 = ((bf16[8,32,896]{2,1,0:T(8,128)(2,1)}), bf16[8,32,896]{2,1,0:T(8,128)(2,1)S(1)}, u32[]{:S(2)}, u32[]{:S(2)}) async-start(bf16[8,32,896]{2,1,0:T(8,128)(2,1)} %pad_maximum_fusion), calls=%async_computation.4 | async-start | bytes 917504 | tf_op jit(solution)/shard_map/all_to_all | solution.py:586
  190.3 6.8 %collective-permute-start.13 = (bf16[1,32,1024]{2,1,0:T(8,128)(2,1)S(1)}, bf16[1,32,1024]{2,1,0:T(8,128)(2,1)S(1)}, u32[]{:S(2)}, u32[]{:S(2)}) collective-permute-start(bf16[1,32,1024]{2,1,0:T(8,128)(2,1)S(1)} %fusion.7), channel_id=1, source_target_pairs={{0,2},{1,3},{2,0},{3,1},{4,6},{5,7},{6,4},{7,5},{8,10},{9,11},{10,... | collective-permute-start | bytes 196616 | tf_op jit(solution)/shard_map/ppermute | solution.py:608
  (24 other events, 252.6 us)
Sparse Core Ops, SparseCore 0:
  40.6 32.6 all-gather.5
  75.7 32.3 all-gather.3
  110.0 39.4 all-gather.7

commit v4 on v3

--- a/solution.py
+++ b/solution.py
@@ -10,6 +10,7 @@
 HEADS = 16
 BLK = 64
 RAND = 3
+KEY_BLOCKS = 3 + RAND + 2
 
 norm_eps = 1e-05
 masked_score = -1e30
@@ -65,8 +66,7 @@
     return merged
 
 
-def masked_scores(keys, query_rows, limits, inner_rows):
-    score_values = matmul_right(keys, query_rows)
+def masked(score_values, limits, inner_rows):
     parts = [
         jnp.where(inner_rows < limit, score_values[j * BLK : (j + 1) * BLK], masked_score)
         for j, limit in enumerate(limits)
@@ -89,7 +89,7 @@
         query_rows = stack_heads(queries, lanes, head_count)
         keys = jnp.concatenate([qkv[pl.ds(s, BLK), width : 2 * width] for s in starts], axis=0)
         values = jnp.concatenate([qkv[pl.ds(s, BLK), 2 * width :] for s in starts], axis=0)
-        score_values = masked_scores(keys, query_rows, limits, inner_rows)
+        score_values = masked(matmul_right(keys, query_rows), limits, inner_rows)
         top = jnp.max(score_values, axis=0, keepdims=True)
         raised = jnp.exp(score_values - top)
         total = jnp.sum(raised, axis=0, keepdims=True)
@@ -119,17 +119,16 @@
     log_total,
     grad_attended,
     grad_qkv,
-    key_sum,
-    value_sum,
+    sums,
+    parts,
 ):
     total_blocks = qkv.shape[0] // BLK
     width = qkv.shape[1] // 3
     lanes = lax.broadcasted_iota(jnp.int32, (BLK, width), 1) // (width // head_count)
     inner_rows = lax.broadcasted_iota(jnp.int32, (BLK, head_count * BLK), 0)
-    key_sum[...] = jnp.zeros_like(key_sum)
-    value_sum[...] = jnp.zeros_like(value_sum)
-
-    def one(step):
+    sums[...] = jnp.zeros_like(sums)
+
+    def one(step, part):
         starts, limits = key_list(step, block_count, total_blocks, lens, owners, offsets, globals_)
         row = pl.multiple_of(step * BLK, BLK)
         queries = qkv[pl.ds(row, BLK), 0:width] * jnp.asarray(scale, low)
@@ -137,27 +136,30 @@
         grad_rows = stack_heads(grad_attended[pl.ds(row, BLK), :], lanes, head_count)
         keys = jnp.concatenate([qkv[pl.ds(s, BLK), width : 2 * width] for s in starts], axis=0)
         values = jnp.concatenate([qkv[pl.ds(s, BLK), 2 * width :] for s in starts], axis=0)
-        score_values = masked_scores(keys, query_rows, limits, inner_rows)
+        score_values = masked(matmul_right(keys, query_rows), limits, inner_rows)
         probs = jnp.exp(score_values - log_total[step])
         grad_probs = matmul_right(values, grad_rows)
         correction = jnp.sum(probs * grad_probs, axis=0, keepdims=True)
         grad_scores = (probs * (grad_probs - correction)).astype(low)
-        grad_keys = matmul(grad_scores, query_rows)
-        grad_values = matmul(probs.astype(low), grad_rows)
+        parts[part, :, :width] = matmul(grad_scores, query_rows)
+        parts[part, :, width:] = matmul(probs.astype(low), grad_rows)
         grad_queries = merge_heads(matmul_left(grad_scores, keys), lanes, head_count) * scale
         grad_qkv[pl.ds(row, BLK), 0:width] = grad_queries.astype(low)
-        for j, s in enumerate(starts):
-            key_sum[pl.ds(s, BLK), :] += grad_keys[j * BLK : (j + 1) * BLK]
-            value_sum[pl.ds(s, BLK), :] += grad_values[j * BLK : (j + 1) * BLK]
+        return starts
 
     def body(index, carry):
-        for part in range(unroll):
-            one(index * unroll + part)
+        lists = [one(index * unroll + part, part) for part in range(unroll)]
+        for part, starts in enumerate(lists):
+            for j, s in enumerate(starts):
+                sums[pl.ds(s, BLK), :] += parts[part, j * BLK : (j + 1) * BLK]
         return carry
 
     lax.fori_loop(0, total_blocks // unroll, body, 0)
-    grad_qkv[:, width : 2 * width] = key_sum[...].astype(low)
-    grad_qkv[:, 2 * width :] = value_sum[...].astype(low)
+    grad_qkv[:, width:] = sums[...].astype(low)
+
+
+def unroll_of(steps, most):
+    return max(u for u in range(1, most + 1) if steps % u == 0)
 
 
 smem = pl.BlockSpec(memory_space=pltpu.SMEM)
@@ -168,7 +170,7 @@
     rows, width = qkv.shape[0], qkv.shape[1] // 3
     total_blocks = rows // BLK
     return pl.pallas_call(
-        functools.partial(attend_kernel, block_count, head_count, scale, 3),
+        functools.partial(attend_kernel, block_count, head_count, scale, unroll_of(total_blocks, 8)),
         out_shape=(
             jax.ShapeDtypeStruct((rows, width), low),
             jax.ShapeDtypeStruct((total_blocks, 1, head_count * BLK), full),
@@ -187,11 +189,14 @@
     rows, width = qkv.shape[0], qkv.shape[1] // 3
     total_blocks = rows // BLK
     return pl.pallas_call(
-        functools.partial(attend_back_kernel, block_count, head_count, scale, 2),
+        functools.partial(attend_back_kernel, block_count, head_count, scale, unroll_of(total_blocks, 8)),
         out_shape=jax.ShapeDtypeStruct((rows, 3 * width), low),
         in_specs=[smem] * 4 + [vmem] * 3,
         out_specs=vmem,
-        scratch_shapes=[pltpu.VMEM((rows, width), full)] * 2,
+        scratch_shapes=[
+            pltpu.VMEM((rows, 2 * width), full),
+            pltpu.VMEM((unroll_of(total_blocks, 8), KEY_BLOCKS * BLK, 2 * width), full),
+        ],
         compiler_params=pltpu.CompilerParams(vmem_limit_bytes=40 * 2**20),
         cost_estimate=pl.CostEstimate(
             flops=total_blocks * 10 * 128 * 128 * 512, bytes_accessed=rows * width * 16, transcendentals=0
@@ -212,41 +217,33 @@
     return centered * inverse, inverse
 
 
-def project_kernel(count, places, *refs):
-    parts, (gain, shift, w_query, w_key, w_value, qkv, normed) = refs[:count], refs[count:]
-    tokens = parts[0].shape[0]
+def project_kernel(count, rows, column, *refs):
+    parts, (gain, shift, w_query, w_key, w_value) = refs[:count], refs[count : count + 5]
+    qkv, normed = refs[-2:]
     weights = jnp.concatenate([w_query[...], w_key[...], w_value[...]], axis=1)
-    for distance, part in enumerate(parts):
+    for i, part in enumerate(parts):
+        at = pl.ds(pl.multiple_of(rows[i] * part.shape[0], part.shape[0]), part.shape[0])
         scaled, _ = row_stats(part[...].astype(full))
-        rows = (scaled * as_row(gain) + as_row(shift)).astype(low)
-        at = pl.ds(pl.multiple_of((places[0] ^ distance) * tokens, tokens), tokens)
-        normed[at, :] = rows
-        qkv[at, :] = matmul(rows, weights).astype(low)
-
-
-def project(places, parts, gain, shift, w_query, w_key, w_value, width, copies):
+        result = (scaled * as_row(gain) + as_row(shift)).astype(low)
+        normed[at, :] = result
+        qkv[at, :] = matmul(result, weights).astype(low)
+
+
+def project(rows, column, parts, gain, shift, weights, width):
     count = len(parts)
     tokens, model = parts[0].shape
-    whole = pl.BlockSpec((tokens, model), lambda j, places: (0, 0))
-    row = pl.BlockSpec((model,), lambda j, places: (0,))
-    if width % 128:
-        weights = [
-            lax.dynamic_slice_in_dim(w, places[0] // copies * width, width, axis=1)
-            for w in (w_query, w_key, w_value)
-        ]
-        weight = pl.BlockSpec((model, width), lambda j, places: (0, 0))
-    else:
-        weights = [w_query, w_key, w_value]
-        weight = pl.BlockSpec((model, width), lambda j, places: (0, places[0] // copies))
+    whole = pl.BlockSpec((tokens, model), lambda j, rows, column: (0, 0))
+    row = pl.BlockSpec((model,), lambda j, rows, column: (0,))
+    weight = pl.BlockSpec((model, width), lambda j, rows, column: (0, column[0]))
     return pl.pallas_call(
         functools.partial(project_kernel, count),
         grid_spec=pltpu.PrefetchScalarGridSpec(
-            num_scalar_prefetch=1,
+            num_scalar_prefetch=2,
             grid=(1,),
             in_specs=[whole] * count + [row, row] + [weight] * 3,
             out_specs=(
-                pl.BlockSpec((count * tokens, 3 * width), lambda j, places: (0, 0)),
-                pl.BlockSpec((count * tokens, model), lambda j, places: (0, 0)),
+                pl.BlockSpec((count * tokens, 3 * width), lambda j, rows, column: (0, 0)),
+                pl.BlockSpec((count * tokens, model), lambda j, rows, column: (0, 0)),
             ),
         ),
         out_shape=(
@@ -260,7 +257,7 @@
             transcendentals=0,
         ),
         name="project",
-    )(places, *parts, gain, shift, *weights)
+    )(rows, column, *parts, gain, shift, *weights)
 
 
 def project_back_kernel(
@@ -413,7 +410,7 @@
 def feed(normed, middle, grad_out, w_out, gain, b_back, w_in, b_in, w_back, groups, width):
     tokens, model = normed.shape
     ff = w_in.shape[1]
-    columns = 512
+    columns = 1024
     row = pl.BlockSpec((model,), lambda j: (0,))
     whole = pl.BlockSpec((tokens, model), lambda j: (0, 0))
     heads = pl.BlockSpec((groups, tokens, width), lambda j: (0, 0, 0))
@@ -496,7 +493,7 @@
 
 def product(places, left, left_columns, right, outer, name):
     tokens, columns = right.shape
-    chunk = min(512, tokens)
+    chunk = 768
     rows = left_columns // (4 * outer)
     return pl.pallas_call(
         product_kernel,
@@ -550,7 +547,7 @@
 def feed_products(places, normed, kept, w_in, b_in, w_back, seq_count):
     tokens, model = normed.shape
     columns = w_in.shape[1] // seq_count
-    chunk = 512
+    chunk = 768
     slim = model // (4 * seq_count)
     back_slim = columns // 4
     return pl.pallas_call(
@@ -666,8 +663,22 @@
     gain_one, gain_two = ln1_gain, ln2_gain
     places = jnp.stack([lax.axis_index("seq"), lax.axis_index("batch")]).astype(jnp.int32)
     parts = gather_parts(rows_in)
+    place = lax.axis_index("seq").astype(jnp.int32)
+    column = (place // copies).reshape(1)
+    weights = [w_query, w_key, w_value]
+    if width % 128:
+        weights = [
+            lax.dynamic_slice_in_dim(w, place // copies * width, width, axis=1) for w in weights
+        ]
+        column = jnp.zeros_like(column)
     qkv, normed_all = project(
-        places, parts, gain_one, ln1_shift, w_query, w_key, w_value, width, copies
+        place ^ jnp.arange(seq_count, dtype=jnp.int32),
+        column,
+        parts,
+        gain_one,
+        ln1_shift,
+        weights,
+        width,
     )
     late_grad_out, qkv = together(grad_out, qkv)
     grad_out_all = gather_rows(late_grad_out)
@@ -712,12 +723,14 @@
     input_grad, gain_one_grads = project_back(
         rows_in, gain_one, grad_middle, grad_qkv_near, w_query, w_key, w_value
     )
-    in_got, qkv_last, back_sent, input_grad, gain_one_grads = together(
-        in_got, qkv_last, back_sent, input_grad, gain_one_grads
-    )
+    small = [gain_one_grads[0], gain_one_grads[1], *gain_two_grads, grad_b_in[0]]
+    packed = jnp.concatenate([v.reshape(device_count, -1) for v in small], axis=1)
+    packed = swap(packed, ("seq", "batch"))
+    input_grad, back_sent = together(input_grad, back_sent)
+    back_got = trade(back_sent, 1)
+    in_got, qkv_last, packed = together(in_got, qkv_last, packed)
     in_own, in_other = first_sum(in_got, in_own, in_other)
     in_last = trade(in_other, 2)
-    back_got = trade(back_sent, 1)
     own_rows = width // copies
     own_attended, in_own = together(attended_all, in_own)
     if copies > 1:
@@ -726,26 +739,25 @@
     out_sent, out_own, out_other = product(
         places, own_attended, own_rows, grad_middle_all, 1, "out_product"
     )
-    in_last, back_got, out_sent, gain_one_grads = together(in_last, back_got, out_sent, gain_one_grads)
     out_got = trade(out_sent, 1)
-    back_own, back_other = first_sum(back_got, back_own, back_other)
-    back_rows = (back_own + trade(back_other, 2).astype(full))[0]
-    out_own, out_other = first_sum(out_got, out_own, out_other)
-    out_rows = (out_own + trade(out_other, 2).astype(full))[0]
-
+    in_last, out_got = together(in_last, out_got)
     mixed = [
         (own + last.astype(full)).astype(low)
         for own, last in ((in_own, in_last), (qkv_own, qkv_last))
     ]
     mixed = swap(jnp.concatenate(mixed, axis=2), "seq")
+    out_own, out_other = first_sum(out_got, out_own, out_other)
+    out_last = trade(out_other, 2)
+    back_own, out_last = together(back_own, out_last)
+    back_own, back_other = first_sum(back_got, back_own, back_other)
+    back_rows = (back_own + trade(back_other, 2).astype(full))[0]
+    out_rows = (out_own + out_last.astype(full))[0]
     in_rows = mixed[:, :, :inner_columns].transpose(1, 0, 2).reshape(slim, ff_width).astype(full)
     qkv_rows = mixed[::copies, :, inner_columns:].transpose(1, 0, 2).astype(full)
     qkv_rows = [
         qkv_rows[:, :, i * width : (i + 1) * width].reshape(slim, model_width) for i in range(3)
     ]
-    small = [gain_one_grads[0], gain_one_grads[1], *gain_two_grads, grad_b_in[0]]
-    packed = jnp.concatenate([v.reshape(device_count, -1) for v in small], axis=1)
-    packed = jnp.sum(swap(packed, ("seq", "batch")), axis=0)
+    packed = jnp.sum(packed, axis=0)
     cuts, at = [], 0
     for v in small:
         size = v.shape[0] // device_count

time: 209 us -> 198 us (0.947)
  blocking collectives: 23.1 us -> 12.1 us
  Pallas kernels: 81.3 us -> 72.9 us
  waiting for transfers between devices: 48.7 us -> 53 us
  starting transfers between devices: 29 us -> 31.6 us
    all_to_all x2 -> x1, blocking collectives: 23.1 us -> 12.1 us  [swap(): return lax.all_to_all(blocks, axes, split_axis=0, concat_axis=0, tiled=True)]
    all_to_all x3 -> x4, waiting for transfers between devices: 7.14 us -> 16 us  [swap(): return lax.all_to_all(blocks, axes, split_axis=0, concat_axis=0, tiled=True)]
    ppermute x8, waiting for transfers between devices: 22.7 us -> 18 us  [trade(): return lax.ppermute(block, 'batch', [(i, i ^ distance) for i in range(4)])]
    all_to_all x3 -> x4, starting transfers between devices: 11.7 us -> 16 us  [swap(): return lax.all_to_all(blocks, axes, split_axis=0, concat_axis=0, tiled=True)]
    pallas_call x1, Pallas kernels: 9.23 us -> 5.8 us  [attend(): pl.pallas_call(functools.partial(attend_kernel, block_count, head_count,...]
  transfers between devices with their start and end apart: 21 -> 22, of which waited for: 10 -> 9; matrix products, arithmetic and copies ran while one was open for 3% -> 4% of each run, Pallas kernels for 35% -> 33%
where the time goes in v4:
time: 198 us; the launch traced here: 197 us
  Pallas kernels  72.9 us (37%)
  waiting for transfers between devices  53 us (27%)
  starting transfers between devices  31.6 us (16%)
  between operations  14.7 us (7%)
  blocking collectives  12.1 us (6%)
  local copies, waits for them, and re-layouts  8.25 us (4%)
  other arithmetic  4.9 us (2%)
    ppermute x7, waiting for transfers between devices, move(): return lax.ppermute(block, 'seq', [(i, i ^ distance) for i in range(count)])  18.9 us
    ppermute x8, waiting for transfers between devices, trade(): return lax.ppermute(block, 'batch', [(i, i ^ distance) for i in range(4)])  18 us
    all_to_all x4, starting transfers between devices, swap(): return lax.all_to_all(blocks, axes, split_axis=0, concat_axis=0, tiled=True)  16 us
    all_to_all x4, waiting for transfers between devices, swap(): return lax.all_to_all(blocks, axes, split_axis=0, concat_axis=0, tiled=True)  16 us
    pallas_call x1, Pallas kernels, feed(): pl.pallas_call(feed_kernel, grid=(ff // columns,), out_shape=(jax.ShapeDt...  16 us
    pallas_call x1, Pallas kernels, feed_products(): pl.pallas_call(feed_products_kernel, grid_spec=pltpu.PrefetchScalarGridSp...  12.8 us
    all_to_all x1, blocking collectives, swap(): return lax.all_to_all(blocks, axes, split_axis=0, concat_axis=0, tiled=True)  12.1 us
    pallas_call x1, Pallas kernels, attend_back(): pl.pallas_call(functools.partial(attend_back_kernel, block_count, head_co...  10.4 us
  transfers between devices with their start and end apart: 22, of which 9 were waited for; matrix products, arithmetic and copies ran while one was open for 4% of the time, Pallas kernels for 33%

profile of v4, /device:TPU:0, one launch (start us, length us, event | category | flops | bytes accessed | tf_op | source)
XLA Modules:
  0.0 197.4 jit_solution(16762110532888730173)
XLA Ops:
  7.2 3.0 %collective-permute-start.1 = (bf16[192,1024]{1,0:T(8,128)(2,1)}, bf16[192,1024]{1,0:T(8,128)(2,1)S(1)}, u32[]{:S(2)}, u32[]{:S(2)}) collective-permute-start(bf16[192,1024]{1,0:T(8,128)(2,1)} %bitcast.66), channel_id=1, source_target_pairs={{0,8},{4,12},{8,0},{12,4},{16,24},{20,28},{24,16},{28,20},{1,9},{5... | collective-permute-start | bytes 1179656 | tf_op jit(solution)/shard_map/ppermute | solution.py:594
  11.8 8.6 %collective-permute-done.1.refs_2_ = bf16[192,1024]{1,0:T(8,128)(2,1)S(1)} collective-permute-done((bf16[192,1024]{1,0:T(8,128)(2,1)}, bf16[192,1024]{1,0:T(8,128)(2,1)S(1)}, u32[]{:S(2)}, u32[]{:S(2)}) %collective-permute-start.1) | collective-permute-done | bytes 393248 | tf_op jit(solution)/shard_map/ppermute | solution.py:594
  20.4 9.1 %collective-permute-done.3.refs_4_ = bf16[192,1024]{1,0:T(8,128)(2,1)S(1)} collective-permute-done((bf16[192,1024]{1,0:T(8,128)(2,1)}, bf16[192,1024]{1,0:T(8,128)(2,1)S(1)}, u32[]{:S(2)}, u32[]{:S(2)}) %collective-permute-start.3) | collective-permute-done | bytes 393248 | tf_op jit(solution)/shard_map/ppermute | solution.py:594
  32.5 7.8 %project.1 = (bf16[1536,384]{1,0:T(8,128)(2,1)}, bf16[1536,1024]{1,0:T(8,128)(2,1)}) custom-call(s32[8]{0:T(128)} %iota_xor_fusion.rows, s32[1]{0:T(128)} %bitcast.1.column, bf16[192,1024]{1,0:T(8,128)(2,1)} %bitcast.70, bf16[192,1024]{1,0:T(8,128)(2,1)} %copy-done.8, bf16[192,1024]{1,0:T(8,128)(2,1)} %copy-done.5, bf16[192,1024]{1,0:T(8,128)(2,1)} %copy-done.9, ...), custom_call_target="tpu_custom_call" | custom-call | flops 1207959552 | bytes 6291456 | tf_op jit(solution)/shard_map/project/pallas_call | solution.py:238
  42.5 5.8 %attend.1 = (bf16[1536,128]{1,0:T(8,128)(2,1)S(1)}, f32[24,1,128]{2,1,0:T(1,128)S(1)}) custom-call(s32[1,1]{1,0:T(1,128)S(6)} %copy.63.lens, s32[1,24,3]{2,1,0:T(8,128)S(1)} %copy.44.owners, s32[1,24,3]{2,1,0:T(8,128)S(1)} %copy.45.offsets, s32[1,1,2]{2,1,0:T(1,128)S(1)} %copy-done.3, bf16[1536,384]{1,0:T(8,128)(2,1)S(1)} %copy-done.1), custom_call_target="tpu_custom_call" | custom-call | flops 805306368 | bytes 1572864 | tf_op jit(solution)/shard_map/attend/pallas_call | solution.py:172
  48.3 12.1 %all_to_all.32.received = bf16[8,192,128]{2,1,0:T(8,128)(2,1)} all-to-all(bf16[8,192,128]{2,1,0:T(8,128)(2,1)S(1)} %bitcast.64), channel_id=1, replica_groups=mesh['seq'=8,'batch'=4] {'seq'}, dimensions={0} | all-to-all | bytes 786432 | tf_op jit(solution)/shard_map/all_to_all | solution.py:583
  60.4 3.5 %attend_out.1 = (f32[192,1024]{1,0:T(8,128)}, bf16[192,1024]{1,0:T(8,128)(2,1)}) custom-call(bf16[8,192,128]{2,1,0:T(8,128)(2,1)} %all_to_all.32.received, bf16[192,1024]{1,0:T(8,128)(2,1)} %bitcast.71, bf16[1024,1024]{1,0:T(8,128)(2,1)} %w_out.3, bf16[1024]{0:T(1024)(128)(2,1)} %gain.4, bf16[1024]{0:T(1024)(128)(2,1)} %shift.1), custom_call_target="tpu_custom_call" | custom-call | flops 402653184 | bytes 2097152 | tf_op jit(solution)/shard_map/attend_out/pallas_call | solution.py:334
  64.0 16.0 %feed.1 = (bf16[192,1024]{1,0:T(8,128)(2,1)}, f32[192,1024]{1,0:T(8,128)}, bf16[192,1024]{1,0:T(8,128)(2,1)}, bf16[8,192,128]{2,1,0:T(8,128)(2,1)}, f32[3,1024]{1,0:T(4,128)}, /*index=5*/f32[1,4096]{1,0:T(1,128)}) custom-call(bf16[192,1024]{1,0:T(8,128)(2,1)} %get-tuple-element.64.normed, f32[192,1024]{1,0:T(8,128)} %get-tuple-element.65.middle, ...), custom_call_target="tpu_custom_call" | custom-call | flops 6442450944 | bytes 16777216 | tf_op jit(solution)/shard_map/feed/pallas_call | solution.py:417
  80.0 3.6 %all-to-all-start.1 = ((bf16[8,192,128]{2,1,0:T(8,128)(2,1)}), bf16[8,192,128]{2,1,0:T(8,128)(2,1)S(1)}, u32[]{:S(2)}, u32[]{:S(2)}) async-start(bf16[8,192,128]{2,1,0:T(8,128)(2,1)} %get-tuple-element.69), calls=%async_computation.1 | async-start | bytes 786432 | tf_op jit(solution)/shard_map/all_to_all | solution.py:583
  84.8 10.2 %all-to-all-done.1 = bf16[8,192,128]{2,1,0:T(8,128)(2,1)S(1)} async-done(((bf16[8,192,128]{2,1,0:T(8,128)(2,1)}), bf16[8,192,128]{2,1,0:T(8,128)(2,1)S(1)}, u32[]{:S(2)}, u32[]{:S(2)}) %all-to-all-start.1) | async-done | bytes 393248 | tf_op jit(solution)/shard_map/all_to_all | solution.py:583
  95.0 10.4 %attend_back.1.right = bf16[1536,384]{1,0:T(8,128)(2,1)} custom-call(s32[1,1]{1,0:T(1,128)S(6)} %copy.63.lens, s32[1,24,3]{2,1,0:T(8,128)S(1)} %copy.44.owners, s32[1,24,3]{2,1,0:T(8,128)S(1)} %copy.45.offsets, s32[1,1,2]{2,1,0:T(1,128)S(1)} %copy-done.3, bf16[1536,384]{1,0:T(8,128)(2,1)S(1)} %copy-done.2, f32[24,1,128]{2,1,0:T(1,128)S(1)} %get-tuple-element.68.log_total, ...), custom_call_target="tpu_custom_call" | custom-call | flops 2013265920 | bytes 3145728 | tf_op jit(solution)/shard_map/attend_back/pallas_call | solution.py:191
  105.4 3.7 %all-to-all-start.2 = ((bf16[8,192,384]{2,1,0:T(8,128)(2,1)}), bf16[8,192,384]{2,1,0:T(8,128)(2,1)S(1)}, u32[]{:S(2)}, u32[]{:S(2)}) async-start(bf16[8,192,384]{2,1,0:T(8,128)(2,1)} %bitcast.6), calls=%async_computation.2 | async-start | bytes 2359296 | tf_op jit(solution)/shard_map/all_to_all | solution.py:583
  109.4 5.5 %qkv_product.1 = (bf16[2,8,32,384]{3,2,1,0:T(8,128)(2,1)}, bf16[8,32,384]{2,1,0:T(8,128)(2,1)}, bf16[8,32,384]{2,1,0:T(8,128)(2,1)}) custom-call(s32[2]{0:T(128)} %pad_add_fusion.places, bf16[1536,1024]{1,0:T(8,128)(2,1)} %get-tuple-element.72.left, bf16[1536,384]{1,0:T(8,128)(2,1)} %attend_back.1.right), custom_call_target="tpu_custom_call" | custom-call | flops 1207959552 | bytes 4325376 | tf_op jit(solution)/shard_map/qkv_product/pallas_call | solution.py:498
  116.5 12.8 %feed_products.1 = (bf16[2,8,32,512]{3,2,1,0:T(8,128)(2,1)}, bf16[8,32,512]{2,1,0:T(8,128)(2,1)}, bf16[8,32,512]{2,1,0:T(8,128)(2,1)}, bf16[2,1,128,1024]{3,2,1,...) custom-call(s32[2]{0:T(128)} %pad_add_fusion.places, ...), custom_call_target="tpu_custom_call" | custom-call | flops 6442450944 | bytes 8388608 | tf_op jit(solution)/shard_map/feed_products/pallas_call | solution.py:553
  129.9 2.5 %collective-permute-start.9 = (bf16[8,32,384]{2,1,0:T(8,128)(2,1)S(1)}, bf16[8,32,384]{2,1,0:T(8,128)(2,1)S(1)}, u32[]{:S(2)}, u32[]{:S(2)}) collective-permute-start(bf16[8,32,384]{2,1,0:T(8,128)(2,1)S(1)} %fusion.6), channel_id=1, source_target_pairs={{0,2},{1,3},{2,0},{3,1},{4,6},{5,7},{6,4},{7,5},{8,10},{9,11},{10,... | collective-permute-start | bytes 589832 | tf_op jit(solution)/shard_map/ppermute | solution.py:605
  132.3 7.2 %project_back.1 = (bf16[192,1024]{1,0:T(8,128)(2,1)}, f32[2,1024]{1,0:T(2,128)}) custom-call(bf16[192,1024]{1,0:T(8,128)(2,1)} %bitcast.72, bf16[1024]{0:T(1024)(128)(2,1)} %gain.5, f32[192,1024]{1,0:T(8,128)} %get-tuple-element.67.grad_middle, bf16[8,192,384]{2,1,0:T(8,128)(2,1)} %copy-done.4, bf16[1024,1024]{1,0:T(8,128)(2,1)} %w_query.1, ...), custom_call_target="tpu_custom_call" | custom-call | flops 1207959552 | bytes 6291456 | tf_op jit(solution)/shard_map/project_back/pallas_call | solution.py:298
  141.2 4.9 %all-to-all-start.3 = ((f32[32,1,288]{2,1,0:T(1,128)}), f32[32,1,288]{2,1,0:T(1,128)S(1)}, u32[]{:S(2)}, u32[]{:S(2)}) async-start(f32[32,1,288]{2,1,0:T(1,128)} %all_to_all.23), calls=%async_computation.3 | async-start | bytes 98304 | tf_op jit(solution)/shard_map/all_to_all | solution.py:583
  147.9 5.9 %all-to-all-done.3 = f32[32,1,288]{2,1,0:T(1,128)S(1)} async-done(((f32[32,1,288]{2,1,0:T(1,128)}), f32[32,1,288]{2,1,0:T(1,128)S(1)}, u32[]{:S(2)}, u32[]{:S(2)}) %all-to-all-start.3) | async-done | bytes 36896 | tf_op jit(solution)/shard_map/all_to_all | solution.py:583
  154.5 3.9 %out_product.1 = (bf16[2,1,32,1024]{3,2,1,0:T(8,128)(2,1)}, bf16[1,32,1024]{2,1,0:T(8,128)(2,1)}, bf16[1,32,1024]{2,1,0:T(8,128)(2,1)}) custom-call(s32[2]{0:T(128)} %pad_add_fusion.places, bf16[1536,128]{1,0:T(8,128)(2,1)} %copy-done, bf16[1536,1024]{1,0:T(8,128)(2,1)} %all-gather.8.cloned.1.call-done.right), custom_call_target="tpu_custom_call" | custom-call | flops 402653184 | bytes 3538944 | tf_op jit(solution)/shard_map/out_product/pallas_call | solution.py:498
  160.1 9.4 %collective-permute-done.11 = bf16[2,1,32,1024]{3,2,1,0:T(8,128)(2,1)S(1)} collective-permute-done((bf16[2,1,32,1024]{3,2,1,0:T(8,128)(2,1)}, bf16[2,1,32,1024]{3,2,1,0:T(8,128)(2,1)S(1)}, u32[]{:S(2)}, u32[]{:S(2)}) %collective-permute-start.11) | collective-permute-done | bytes 131104 | tf_op jit(solution)/shard_map/ppermute | solution.py:605
  170.4 2.4 %collective-permute-start.12 = (bf16[1,32,1024]{2,1,0:T(8,128)(2,1)S(1)}, bf16[1,32,1024]{2,1,0:T(8,128)(2,1)S(1)}, u32[]{:S(2)}, u32[]{:S(2)}) collective-permute-start(bf16[1,32,1024]{2,1,0:T(8,128)(2,1)S(1)} %fusion.7), channel_id=1, source_target_pairs={{0,2},{1,3},{2,0},{3,1},{4,6},{5,7},{6,4},{7,5},{8,10},{9,11},{10,... | collective-permute-start | bytes 196616 | tf_op jit(solution)/shard_map/ppermute | solution.py:605
  174.5 3.8 %all-to-all-start.4 = ((bf16[8,32,896]{2,1,0:T(8,128)(2,1)}), bf16[8,32,896]{2,1,0:T(8,128)(2,1)S(1)}, u32[]{:S(2)}, u32[]{:S(2)}) async-start(bf16[8,32,896]{2,1,0:T(8,128)(2,1)} %pad_maximum_fusion), calls=%async_computation.4 | async-start | bytes 917504 | tf_op jit(solution)/shard_map/all_to_all | solution.py:583
  178.3 3.9 %collective-permute-done.12 = bf16[1,32,1024]{2,1,0:T(8,128)(2,1)S(1)} collective-permute-done((bf16[1,32,1024]{2,1,0:T(8,128)(2,1)S(1)}, bf16[1,32,1024]{2,1,0:T(8,128)(2,1)S(1)}, u32[]{:S(2)}, u32[]{:S(2)}) %collective-permute-start.12) | collective-permute-done | bytes 65568 | tf_op jit(solution)/shard_map/ppermute | solution.py:605
  182.9 4.8 %collective-permute-done.14 = bf16[1,128,1024]{2,1,0:T(8,128)(2,1)S(1)} collective-permute-done((bf16[1,128,1024]{2,1,0:T(8,128)(2,1)S(1)}, bf16[1,128,1024]{2,1,0:T(8,128)(2,1)S(1)}, u32[]{:S(2)}, u32[]{:S(2)}) %collective-permute-start.14) | collective-permute-done | bytes 262176 | tf_op jit(solution)/shard_map/ppermute | solution.py:605
  (114 shorter events, 22.1 us)
Async XLA Ops:
  7.2 87.8 %all-gather.4.cloned.1.call-start = ((), (), s32[]{:S(2)}) async-start(), calls=%async_computation.5 | async-start | bytes 3538944 | tf_op jit(solution)/shard_map/all_gather | solution.py:587
  7.2 13.2 %collective-permute-start.1 = (bf16[192,1024]{1,0:T(8,128)(2,1)}, bf16[192,1024]{1,0:T(8,128)(2,1)S(1)}, u32[]{:S(2)}, u32[]{:S(2)}) collective-permute-start(bf16[192,1024]{1,0:T(8,128)(2,1)} %bitcast.66), channel_id=1, source_target_pairs={{0,8},{4,12},{8,0},{12,4},{16,24},{20,28},{24,16},{28,20},{1,9},{5... | collective-permute-start | bytes 1179656 | tf_op jit(solution)/shard_map/ppermute | solution.py:594
  10.2 19.2 %collective-permute-start.3 = (bf16[192,1024]{1,0:T(8,128)(2,1)}, bf16[192,1024]{1,0:T(8,128)(2,1)S(1)}, u32[]{:S(2)}, u32[]{:S(2)}) collective-permute-start(bf16[192,1024]{1,0:T(8,128)(2,1)} %bitcast.67), channel_id=1, source_target_pairs={{0,16},{4,20},{8,24},{12,28},{16,0},{20,4},{24,8},{28,12},{1,17},{... | collective-permute-start | bytes 1179656 | tf_op jit(solution)/shard_map/ppermute | solution.py:594
  11.7 17.7 %collective-permute-start.5 = (bf16[192,1024]{1,0:T(8,128)(2,1)}, bf16[192,1024]{1,0:T(8,128)(2,1)S(1)}, u32[]{:S(2)}, u32[]{:S(2)}) collective-permute-start(bf16[192,1024]{1,0:T(8,128)(2,1)} %bitcast.68), channel_id=1, source_target_pairs={{0,24},{4,28},{8,16},{12,20},{16,8},{20,12},{24,0},{28,4},{1,25},{... | collective-permute-start | bytes 1179656 | tf_op jit(solution)/shard_map/ppermute | solution.py:594
  11.8 18.7 %collective-permute-start = (bf16[192,1024]{1,0:T(8,128)(2,1)}, bf16[192,1024]{1,0:T(8,128)(2,1)S(1)}, u32[]{:S(2)}, u32[]{:S(2)}) collective-permute-start(bf16[192,1024]{1,0:T(8,128)(2,1)} %bitcast.69), channel_id=1, source_target_pairs={{0,4},{4,0},{8,12},{12,8},{16,20},{20,16},{24,28},{28,24},{1,5},{5... | collective-permute-start | bytes 1179656 | tf_op jit(solution)/shard_map/ppermute | solution.py:594
  20.4 10.1 %collective-permute-start.2 = (bf16[192,1024]{1,0:T(8,128)(2,1)S(1)}, bf16[192,1024]{1,0:T(8,128)(2,1)S(1)}, u32[]{:S(2)}, u32[]{:S(2)}) collective-permute-start(bf16[192,1024]{1,0:T(8,128)(2,1)S(1)} %collective-permute-done.1.refs_2_), channel_id=1, source_target_pairs={{0,4},{4,0},{8,12},{12,8},{16,20},{20,16},{24,28},{28,24},{1,5},{5... | collective-permute-start | bytes 1179656 | tf_op jit(solution)/shard_map/ppermute | solution.py:594
  29.4 1.7 collective-permute-start.4
  29.5 2.3 %collective-permute-start.6 = (bf16[192,1024]{1,0:T(8,128)(2,1)S(1)}, bf16[192,1024]{1,0:T(8,128)(2,1)S(1)}, u32[]{:S(2)}, u32[]{:S(2)}) collective-permute-start(bf16[192,1024]{1,0:T(8,128)(2,1)S(1)} %collective-permute-done.5.refs_6_), channel_id=1, source_target_pairs={{0,4},{4,0},{8,12},{12,8},{16,20},{20,16},{24,28},{28,24},{1,5},{5... | collective-permute-start | bytes 1179656 | tf_op jit(solution)/shard_map/ppermute | solution.py:594
  40.4 76.1 %all-gather.6.cloned.1.call-start = ((), (), s32[]{:S(2)}) async-start(), calls=%async_computation.6 | async-start | bytes 3538944 | tf_op jit(solution)/shard_map/all_gather | solution.py:587
  48.3 31.6 %copy-start = (bf16[1536,128]{1,0:T(8,128)(2,1)}, bf16[1536,128]{1,0:T(8,128)(2,1)S(1)}, u32[]{:S(2)}) copy-start(bf16[1536,128]{1,0:T(8,128)(2,1)S(1)} %get-tuple-element.94.left) | copy-start | bytes 1179652
  63.9 90.5 %all-gather.8.cloned.1.call-start = ((), (), s32[]{:S(2)}) async-start(), calls=%async_computation.7 | async-start | bytes 3538944 | tf_op jit(solution)/shard_map/all_gather | solution.py:587
  64.0 31.0 %copy-start.2 = (bf16[1536,384]{1,0:T(8,128)(2,1)S(1)}, bf16[1536,384]{1,0:T(8,128)(2,1)}, u32[]{:S(2)}) copy-start(bf16[1536,384]{1,0:T(8,128)(2,1)} %get-tuple-element.62.qkv) | copy-start | bytes 3538948
  80.0 15.0 %all-to-all-start.1 = ((bf16[8,192,128]{2,1,0:T(8,128)(2,1)}), bf16[8,192,128]{2,1,0:T(8,128)(2,1)S(1)}, u32[]{:S(2)}, u32[]{:S(2)}) async-start(bf16[8,192,128]{2,1,0:T(8,128)(2,1)} %get-tuple-element.69), calls=%async_computation.1 | async-start | bytes 786432 | tf_op jit(solution)/shard_map/all_to_all | solution.py:583
  105.4 24.4 %all-to-all-start.2 = ((bf16[8,192,384]{2,1,0:T(8,128)(2,1)}), bf16[8,192,384]{2,1,0:T(8,128)(2,1)S(1)}, u32[]{:S(2)}, u32[]{:S(2)}) async-start(bf16[8,192,384]{2,1,0:T(8,128)(2,1)} %bitcast.6), calls=%async_computation.2 | async-start | bytes 2359296 | tf_op jit(solution)/shard_map/all_to_all | solution.py:583
  114.9 14.9 %collective-permute-start.7 = (bf16[2,8,32,384]{3,2,1,0:T(8,128)(2,1)}, bf16[2,8,32,384]{3,2,1,0:T(8,128)(2,1)S(1)}, u32[]{:S(2)}, u32[]{:S(2)}) collective-permute-start(bf16[2,8,32,384]{3,2,1,0:T(8,128)(2,1)} %get-tuple-element.74), channel_id=1, source_target_pairs={{0,1},{1,0},{2,3},{3,2},{4,5},{5,4},{6,7},{7,6},{8,9},{9,8},{10,11... | collective-permute-start | bytes 1179656 | tf_op jit(solution)/shard_map/ppermute | solution.py:605
  129.3 24.5 %collective-permute-start.8 = (bf16[2,8,32,512]{3,2,1,0:T(8,128)(2,1)}, bf16[2,8,32,512]{3,2,1,0:T(8,128)(2,1)S(1)}, u32[]{:S(2)}, u32[]{:S(2)}) collective-permute-start(bf16[2,8,32,512]{3,2,1,0:T(8,128)(2,1)} %get-tuple-element.84), channel_id=1, source_target_pairs={{0,1},{1,0},{2,3},{3,2},{4,5},{5,4},{6,7},{7,6},{8,9},{9,8},{10,11... | collective-permute-start | bytes 1572872 | tf_op jit(solution)/shard_map/ppermute | solution.py:605
  129.9 23.9 %collective-permute-start.9 = (bf16[8,32,384]{2,1,0:T(8,128)(2,1)S(1)}, bf16[8,32,384]{2,1,0:T(8,128)(2,1)S(1)}, u32[]{:S(2)}, u32[]{:S(2)}) collective-permute-start(bf16[8,32,384]{2,1,0:T(8,128)(2,1)S(1)} %fusion.6), channel_id=1, source_target_pairs={{0,2},{1,3},{2,0},{3,1},{4,6},{5,7},{6,4},{7,5},{8,10},{9,11},{10,... | collective-permute-start | bytes 589832 | tf_op jit(solution)/shard_map/ppermute | solution.py:605
  141.2 12.6 %all-to-all-start.3 = ((f32[32,1,288]{2,1,0:T(1,128)}), f32[32,1,288]{2,1,0:T(1,128)S(1)}, u32[]{:S(2)}, u32[]{:S(2)}) async-start(f32[32,1,288]{2,1,0:T(1,128)} %all_to_all.23), calls=%async_computation.3 | async-start | bytes 98304 | tf_op jit(solution)/shard_map/all_to_all | solution.py:583
  146.1 26.8 %collective-permute-start.13 = (bf16[2,1,128,1024]{3,2,1,0:T(8,128)(2,1)}, bf16[2,1,128,1024]{3,2,1,0:T(8,128)(2,1)S(1)}, u32[]{:S(2)}, u32[]{:S(2)}) collective-permute-start(bf16[2,1,128,1024]{3,2,1,0:T(8,128)(2,1)} %get-tuple-element.106), channel_id=1, source_target_pairs={{0,1},{1,0},{2,3},{3,2},{4,5},{5,4},{6,7},{7,6},{8,9},{9,8},{10,11... | collective-permute-start | bytes 1572872 | tf_op jit(solution)/shard_map/ppermute | solution.py:605
  154.0 15.5 %collective-permute-start.10 = (bf16[8,32,512]{2,1,0:T(8,128)(2,1)S(1)}, bf16[8,32,512]{2,1,0:T(8,128)(2,1)S(1)}, u32[]{:S(2)}, u32[]{:S(2)}) collective-permute-start(bf16[8,32,512]{2,1,0:T(8,128)(2,1)S(1)} %get-tuple-element.113), channel_id=1, source_target_pairs={{0,2},{1,3},{2,0},{3,1},{4,6},{5,7},{6,4},{7,5},{8,10},{9,11},{10,... | collective-permute-start | bytes 786440 | tf_op jit(solution)/shard_map/ppermute | solution.py:605
  158.3 11.2 %collective-permute-start.11 = (bf16[2,1,32,1024]{3,2,1,0:T(8,128)(2,1)}, bf16[2,1,32,1024]{3,2,1,0:T(8,128)(2,1)S(1)}, u32[]{:S(2)}, u32[]{:S(2)}) collective-permute-start(bf16[2,1,32,1024]{3,2,1,0:T(8,128)(2,1)} %get-tuple-element.96), channel_id=1, source_target_pairs={{0,1},{1,0},{2,3},{3,2},{4,5},{5,4},{6,7},{7,6},{8,9},{9,8},{10,11... | collective-permute-start | bytes 393224 | tf_op jit(solution)/shard_map/ppermute | solution.py:605
  170.4 11.7 %collective-permute-start.12 = (bf16[1,32,1024]{2,1,0:T(8,128)(2,1)S(1)}, bf16[1,32,1024]{2,1,0:T(8,128)(2,1)S(1)}, u32[]{:S(2)}, u32[]{:S(2)}) collective-permute-start(bf16[1,32,1024]{2,1,0:T(8,128)(2,1)S(1)} %fusion.7), channel_id=1, source_target_pairs={{0,2},{1,3},{2,0},{3,1},{4,6},{5,7},{6,4},{7,5},{8,10},{9,11},{10,... | collective-permute-start | bytes 196616 | tf_op jit(solution)/shard_map/ppermute | solution.py:605
  173.0 14.6 %collective-permute-start.14 = (bf16[1,128,1024]{2,1,0:T(8,128)(2,1)S(1)}, bf16[1,128,1024]{2,1,0:T(8,128)(2,1)S(1)}, u32[]{:S(2)}, u32[]{:S(2)}) collective-permute-start(bf16[1,128,1024]{2,1,0:T(8,128)(2,1)S(1)} %fusion), channel_id=1, source_target_pairs={{0,2},{1,3},{2,0},{3,1},{4,6},{5,7},{6,4},{7,5},{8,10},{9,11},{10,... | collective-permute-start | bytes 786440 | tf_op jit(solution)/shard_map/ppermute | solution.py:605
  174.5 14.1 %all-to-all-start.4 = ((bf16[8,32,896]{2,1,0:T(8,128)(2,1)}), bf16[8,32,896]{2,1,0:T(8,128)(2,1)S(1)}, u32[]{:S(2)}, u32[]{:S(2)}) async-start(bf16[8,32,896]{2,1,0:T(8,128)(2,1)} %pad_maximum_fusion), calls=%async_computation.4 | async-start | bytes 917504 | tf_op jit(solution)/shard_map/all_to_all | solution.py:583
  (22 other events, 202.6 us)
Sparse Core Ops, SparseCore 0:
  40.5 34.8 all-gather.3
  77.9 34.9 all-gather.5
  114.7 32.3 all-gather.7

commit v5 on v4

--- a/solution.py
+++ b/solution.py
@@ -321,32 +321,6 @@
     )(inputs, gain, grad_middle, received, w_query, w_key, w_value)
 
 
-def middle_kernel(received, inputs, w_out, gain, shift, middle, normed):
-    attended = jnp.concatenate([received[i] for i in range(received.shape[0])], axis=1)
-    rows = inputs[...].astype(full) + matmul(attended, w_out[...])
-    middle[...] = rows
-    unit, _ = row_stats(rows)
-    normed[...] = (unit * as_row(gain) + as_row(shift)).astype(low)
-
-
-def attend_out(received, inputs, w_out, gain, shift):
-    tokens, model = inputs.shape
-    return pl.pallas_call(
-        middle_kernel,
-        out_shape=(
-            jax.ShapeDtypeStruct((tokens, model), full),
-            jax.ShapeDtypeStruct((tokens, model), low),
-        ),
-        in_specs=[vmem] * 5,
-        out_specs=(vmem, vmem),
-        compiler_params=pltpu.CompilerParams(vmem_limit_bytes=vmem_limit),
-        cost_estimate=pl.CostEstimate(
-            flops=2 * tokens * model * model, bytes_accessed=2 * model * model, transcendentals=0
-        ),
-        name="attend_out",
-    )(received, inputs, w_out, gain, shift)
-
-
 def hidden(normed, grad_out, w_in, b_in, w_back):
     inner = matmul(normed, w_in) + as_row(b_in)
     share = 0.5 * (1.0 + lax.erf(inner * 0.7071067811865476))
@@ -357,67 +331,94 @@
 
 
 def feed_kernel(
-    normed,
-    middle,
+    received,
+    inputs,
     grad_out,
     w_out,
     gain,
+    shift,
     b_back,
     w_in,
     b_in,
     w_back,
     output,
+    normed,
     grad_middle,
     grad_middle_low,
     grad_attended,
     gain_grads,
     b_in_grad,
+    held_out,
+    held_in,
+    held_back,
+    scaled,
     out_total,
     grad_total,
+    arrived,
 ):
-    step = pl.program_id(0)
-    groups, _, width = grad_attended.shape
-
-    @pl.when(step == 0)
-    def _():
-        out_total[...] = middle[...] + as_row(b_back)
-        grad_total[...] = jnp.zeros_like(grad_total)
-
-    active, grads = hidden(normed[...], grad_out[...], w_in[...], b_in, w_back[...])
-    b_in_grad[...] = jnp.sum(grads.astype(full), axis=0, keepdims=True)
-    out_total[...] += matmul(active, w_back[...])
-    grad_total[...] += matmul_right(grads, w_in[...])
-
-    @pl.when(step == pl.num_programs(0) - 1)
-    def _():
-        output[...] = out_total[...].astype(low)
-        grad_normed = grad_total[...]
-        unit, rate = row_stats(middle[...])
-        grad_full = grad_out[...].astype(full)
-        back = normalize_back(grad_normed, unit, rate, as_row(gain))
-        grads_middle = grad_full + back
-        grad_middle[...] = grads_middle
-        grads_low = grads_middle.astype(low)
-        grad_middle_low[...] = grads_low
-        result = matmul_right(grads_low, w_out[...]).astype(low)
-        for i in range(groups):
-            grad_attended[i] = result[:, i * width : (i + 1) * width]
-        gain_grads[0:1, :] = jnp.sum(grad_normed * unit, axis=0, keepdims=True)
-        gain_grads[1:2, :] = jnp.sum(grad_normed, axis=0, keepdims=True)
-        gain_grads[2:3, :] = jnp.sum(grad_full, axis=0, keepdims=True)
-
-
-def feed(normed, middle, grad_out, w_out, gain, b_back, w_in, b_in, w_back, groups, width):
-    tokens, model = normed.shape
+    groups, _, width = received.shape
+    pieces, _, columns = held_in.shape
+    first = pltpu.make_async_copy(w_out, held_out, arrived.at[2, 0])
+    loads = []
+    for i in range(pieces):
+        at = pl.ds(i * columns, columns)
+        loads.append(
+            (
+                pltpu.make_async_copy(w_in.at[:, at], held_in.at[i], arrived.at[0, i]),
+                pltpu.make_async_copy(w_back.at[at, :], held_back.at[i], arrived.at[1, i]),
+            )
+        )
+    first.start()
+    for pair in loads:
+        for load in pair:
+            load.start()
+    first.wait()
+    attended = jnp.concatenate([received[i] for i in range(groups)], axis=1)
+    rows = inputs[...].astype(full) + matmul(attended, held_out[...])
+    unit, rate = row_stats(rows)
+    scaled[...] = unit
+    normed[...] = (unit * as_row(gain) + as_row(shift)).astype(low)
+    out_total[...] = rows + as_row(b_back)
+    for i, pair in enumerate(loads):
+        at = slice(i * columns, (i + 1) * columns)
+        for load in pair:
+            load.wait()
+        active, grads = hidden(
+            normed[...], grad_out[...], held_in[i], b_in[at], held_back[i]
+        )
+        b_in_grad[:, at] = jnp.sum(grads.astype(full), axis=0, keepdims=True)
+        out_total[...] += matmul(active, held_back[i])
+        back = matmul_right(grads, held_in[i])
+        if i:
+            back += grad_total[...]
+        grad_total[...] = back
+    output[...] = out_total[...].astype(low)
+    grad_normed = grad_total[...]
+    unit = scaled[...]
+    grad_full = grad_out[...].astype(full)
+    grads_middle = grad_full + normalize_back(grad_normed, unit, rate, as_row(gain))
+    grad_middle[...] = grads_middle
+    grads_low = grads_middle.astype(low)
+    grad_middle_low[...] = grads_low
+    result = matmul_right(grads_low, held_out[...]).astype(low)
+    for i in range(groups):
+        grad_attended[i] = result[:, i * width : (i + 1) * width]
+    gain_grads[0:1, :] = jnp.sum(grad_normed * unit, axis=0, keepdims=True)
+    gain_grads[1:2, :] = jnp.sum(grad_normed, axis=0, keepdims=True)
+    gain_grads[2:3, :] = jnp.sum(grad_full, axis=0, keepdims=True)
+
+
+def feed(received, inputs, grad_out, w_out, gain, shift, b_back, w_in, b_in, w_back):
+    tokens, model = inputs.shape
     ff = w_in.shape[1]
+    groups, _, width = received.shape
     columns = 1024
-    row = pl.BlockSpec((model,), lambda j: (0,))
-    whole = pl.BlockSpec((tokens, model), lambda j: (0, 0))
-    heads = pl.BlockSpec((groups, tokens, width), lambda j: (0, 0, 0))
+    pieces = ff // columns
+    anywhere = pl.BlockSpec(memory_space=pl.ANY)
     return pl.pallas_call(
         feed_kernel,
-        grid=(ff // columns,),
         out_shape=(
+            jax.ShapeDtypeStruct((tokens, model), low),
             jax.ShapeDtypeStruct((tokens, model), low),
             jax.ShapeDtypeStruct((tokens, model), full),
             jax.ShapeDtypeStruct((tokens, model), low),
@@ -425,32 +426,23 @@
             jax.ShapeDtypeStruct((3, model), full),
             jax.ShapeDtypeStruct((1, ff), full),
         ),
-        in_specs=[
-            whole,
-            whole,
-            whole,
-            pl.BlockSpec((model, model), lambda j: (0, 0), pipeline_mode=pl.Buffered(1)),
-            row,
-            row,
-            pl.BlockSpec((model, columns), lambda j: (0, j)),
-            pl.BlockSpec((columns,), lambda j: (j,)),
-            pl.BlockSpec((columns, model), lambda j: (j, 0)),
+        in_specs=[vmem, vmem, vmem, anywhere, vmem, vmem, vmem, anywhere, vmem, anywhere],
+        out_specs=(vmem,) * 7,
+        scratch_shapes=[
+            pltpu.VMEM((model, model), low),
+            pltpu.VMEM((pieces, model, columns), low),
+            pltpu.VMEM((pieces, columns, model), low),
+            pltpu.VMEM((tokens, model), full),
+            pltpu.VMEM((tokens, model), full),
+            pltpu.VMEM((tokens, model), full),
+            pltpu.SemaphoreType.DMA((3, pieces)),
         ],
-        out_specs=(
-            whole,
-            whole,
-            whole,
-            heads,
-            pl.BlockSpec((3, model), lambda j: (0, 0)),
-            pl.BlockSpec((1, columns), lambda j: (0, j)),
-        ),
-        scratch_shapes=[pltpu.VMEM((tokens, model), full)] * 2,
         compiler_params=pltpu.CompilerParams(vmem_limit_bytes=vmem_limit),
         cost_estimate=pl.CostEstimate(
             flops=8 * tokens * model * ff, bytes_accessed=4 * model * ff, transcendentals=0
         ),
         name="feed",
-    )(normed, middle, grad_out, w_out, gain, b_back, w_in, b_in, w_back)
+    )(received, inputs, grad_out, w_out, gain, shift, b_back, w_in, b_in, w_back)
 
 
 def pick_blocks(index, total, sent, own, other):
@@ -683,23 +675,19 @@
     late_grad_out, qkv = together(grad_out, qkv)
     grad_out_all = gather_rows(late_grad_out)
     attended_all, log_total = attend(tables, qkv, block_count, head_count, scale)
-    middle, normed_two = attend_out(
-        to_tokens(attended_all), rows_in, w_out, gain_two, ln2_shift
-    )
-    normed_two_all = gather_rows(normed_two)
-    output, grad_middle, grad_middle_low, grad_attended, gain_two_grads, grad_b_in = feed(
-        normed_two,
-        middle,
+    output, normed_two, grad_middle, grad_middle_low, grad_attended, gain_two_grads, grad_b_in = feed(
+        to_tokens(attended_all),
+        rows_in,
         grad_out,
         w_out,
         gain_two,
+        ln2_shift,
         b_back,
         w_in,
         b_in,
         w_back,
-        head_groups,
-        width,
     )
+    normed_two_all = gather_rows(normed_two)
     grad_middle_all = gather_rows(grad_middle_low)
     grad_rows, grad_out_all = together(to_heads(grad_attended), grad_out_all)
     grad_qkv = attend_back(tables, qkv, log_total, grad_rows, block_count, head_count, scale)

time: 198 us -> 196 us (0.990)
  Pallas kernels: 72.9 us -> 69.7 us
  starting transfers between devices: 31.6 us -> 33.7 us
    pallas_call x2 -> x1, Pallas kernels: 19.4 us -> 16.4 us  [feed(): pl.pallas_call(feed_kernel, out_shape=(jax.ShapeDtypeStruct((tokens, mode...]
    all_to_all x4, waiting for transfers between devices: 16 us -> 13.3 us  [swap(): return lax.all_to_all(blocks, axes, split_axis=0, concat_axis=0, tiled=True)]
  transfers between devices with their start and end apart: 22 -> 22, of which waited for: 9 -> 10; matrix products, arithmetic and copies ran while one was open for 4% -> 4% of each run, Pallas kernels for 33% -> 32%
where the time goes in v5:
time: 196 us; the launch traced here: 195 us
  Pallas kernels  69.7 us (36%)
  waiting for transfers between devices  51.3 us (26%)
  starting transfers between devices  33.7 us (17%)
  between operations  14.7 us (8%)
  blocking collectives  12.2 us (6%)
  local copies, waits for them, and re-layouts  8.25 us (4%)
  other arithmetic  4.9 us (3%)
    ppermute x7, waiting for transfers between devices, move(): return lax.ppermute(block, 'seq', [(i, i ^ distance) for i in range(count)])  18.9 us
    ppermute x8, waiting for transfers between devices, trade(): return lax.ppermute(block, 'batch', [(i, i ^ distance) for i in range(4)])  17.5 us
    all_to_all x4, starting transfers between devices, swap(): return lax.all_to_all(blocks, axes, split_axis=0, concat_axis=0, tiled=True)  16.8 us
    pallas_call x1, Pallas kernels, feed(): pl.pallas_call(feed_kernel, out_shape=(jax.ShapeDtypeStruct((tokens, mode...  16.4 us
    all_to_all x4, waiting for transfers between devices, swap(): return lax.all_to_all(blocks, axes, split_axis=0, concat_axis=0, tiled=True)  13.3 us
    pallas_call x1, Pallas kernels, feed_products(): pl.pallas_call(feed_products_kernel, grid_spec=pltpu.PrefetchScalarGridSp...  12.8 us
    all_to_all x1, blocking collectives, swap(): return lax.all_to_all(blocks, axes, split_axis=0, concat_axis=0, tiled=True)  12.2 us
    ppermute x8, starting transfers between devices, trade(): return lax.ppermute(block, 'batch', [(i, i ^ distance) for i in range(4)])  11.8 us
  transfers between devices with their start and end apart: 22, of which 10 were waited for; matrix products, arithmetic and copies ran while one was open for 4% of the time, Pallas kernels for 32%

profile of v5, /device:TPU:0, one launch (start us, length us, event | category | flops | bytes accessed | tf_op | source)
XLA Modules:
  0.0 194.8 jit_solution(1027141622642837389)
XLA Ops:
  7.2 3.0 %collective-permute-start.1 = (bf16[192,1024]{1,0:T(8,128)(2,1)}, bf16[192,1024]{1,0:T(8,128)(2,1)S(1)}, u32[]{:S(2)}, u32[]{:S(2)}) collective-permute-start(bf16[192,1024]{1,0:T(8,128)(2,1)} %bitcast.66), channel_id=1, source_target_pairs={{0,8},{4,12},{8,0},{12,4},{16,24},{20,28},{24,16},{28,20},{1,9},{5... | collective-permute-start | bytes 1179656 | tf_op jit(solution)/shard_map/ppermute | solution.py:586
  11.8 8.6 %collective-permute-done.1.refs_2_ = bf16[192,1024]{1,0:T(8,128)(2,1)S(1)} collective-permute-done((bf16[192,1024]{1,0:T(8,128)(2,1)}, bf16[192,1024]{1,0:T(8,128)(2,1)S(1)}, u32[]{:S(2)}, u32[]{:S(2)}) %collective-permute-start.1) | collective-permute-done | bytes 393248 | tf_op jit(solution)/shard_map/ppermute | solution.py:586
  20.4 9.1 %collective-permute-done.3.refs_4_ = bf16[192,1024]{1,0:T(8,128)(2,1)S(1)} collective-permute-done((bf16[192,1024]{1,0:T(8,128)(2,1)}, bf16[192,1024]{1,0:T(8,128)(2,1)S(1)}, u32[]{:S(2)}, u32[]{:S(2)}) %collective-permute-start.3) | collective-permute-done | bytes 393248 | tf_op jit(solution)/shard_map/ppermute | solution.py:586
  32.5 7.8 %project.1 = (bf16[1536,384]{1,0:T(8,128)(2,1)}, bf16[1536,1024]{1,0:T(8,128)(2,1)}) custom-call(s32[8]{0:T(128)} %iota_xor_fusion.rows, s32[1]{0:T(128)} %bitcast.1.column, bf16[192,1024]{1,0:T(8,128)(2,1)} %bitcast.70, bf16[192,1024]{1,0:T(8,128)(2,1)} %copy-done.8, bf16[192,1024]{1,0:T(8,128)(2,1)} %copy-done.5, bf16[192,1024]{1,0:T(8,128)(2,1)} %copy-done.9, ...), custom_call_target="tpu_custom_call" | custom-call | flops 1207959552 | bytes 6291456 | tf_op jit(solution)/shard_map/project/pallas_call | solution.py:238
  42.5 5.7 %attend.1 = (bf16[1536,128]{1,0:T(8,128)(2,1)S(1)}, f32[24,1,128]{2,1,0:T(1,128)S(1)}) custom-call(s32[1,1]{1,0:T(1,128)S(6)} %copy.63.lens, s32[1,24,3]{2,1,0:T(8,128)S(1)} %copy.44.owners, s32[1,24,3]{2,1,0:T(8,128)S(1)} %copy.45.offsets, s32[1,1,2]{2,1,0:T(1,128)S(1)} %copy-done.3, bf16[1536,384]{1,0:T(8,128)(2,1)S(1)} %copy-done.1), custom_call_target="tpu_custom_call" | custom-call | flops 805306368 | bytes 1572864 | tf_op jit(solution)/shard_map/attend/pallas_call | solution.py:172
  48.2 12.2 %all_to_all.32.received = bf16[8,192,128]{2,1,0:T(8,128)(2,1)} all-to-all(bf16[8,192,128]{2,1,0:T(8,128)(2,1)S(1)} %bitcast.64), channel_id=1, replica_groups=mesh['seq'=8,'batch'=4] {'seq'}, dimensions={0} | all-to-all | bytes 786432 | tf_op jit(solution)/shard_map/all_to_all | solution.py:575
  60.4 16.4 %feed.1 = (bf16[192,1024]{1,0:T(8,128)(2,1)}, bf16[192,1024]{1,0:T(8,128)(2,1)}, f32[192,1024]{1,0:T(8,128)}, bf16[192,1024]{1,0:T(8,128)(2,1)}, bf16[8,192,128]...) custom-call(bf16[8,192,128]{2,1,0:T(8,128)(2,1)} %all_to_all.32.received, bf16[192,1024]{1,0:T(8,128)(2,1)} %bitcast.71, ...), custom_call_target="tpu_custom_call" | custom-call | flops 6442450944 | bytes 16777216 | tf_op jit(solution)/shard_map/feed/pallas_call | solution.py:418
  77.5 3.5 %all-to-all-start.1 = ((bf16[8,192,128]{2,1,0:T(8,128)(2,1)}), bf16[8,192,128]{2,1,0:T(8,128)(2,1)S(1)}, u32[]{:S(2)}, u32[]{:S(2)}) async-start(bf16[8,192,128]{2,1,0:T(8,128)(2,1)} %get-tuple-element.66), calls=%async_computation.1 | async-start | bytes 786432 | tf_op jit(solution)/shard_map/all_to_all | solution.py:575
  82.2 7.5 %all-to-all-done.1 = bf16[8,192,128]{2,1,0:T(8,128)(2,1)S(1)} async-done(((bf16[8,192,128]{2,1,0:T(8,128)(2,1)}), bf16[8,192,128]{2,1,0:T(8,128)(2,1)S(1)}, u32[]{:S(2)}, u32[]{:S(2)}) %all-to-all-start.1) | async-done | bytes 393248 | tf_op jit(solution)/shard_map/all_to_all | solution.py:575
  89.7 10.4 %attend_back.1.right = bf16[1536,384]{1,0:T(8,128)(2,1)} custom-call(s32[1,1]{1,0:T(1,128)S(6)} %copy.63.lens, s32[1,24,3]{2,1,0:T(8,128)S(1)} %copy.44.owners, s32[1,24,3]{2,1,0:T(8,128)S(1)} %copy.45.offsets, s32[1,1,2]{2,1,0:T(1,128)S(1)} %copy-done.3, bf16[1536,384]{1,0:T(8,128)(2,1)S(1)} %copy-done.2, f32[24,1,128]{2,1,0:T(1,128)S(1)} %get-tuple-element.65.log_total, ...), custom_call_target="tpu_custom_call" | custom-call | flops 2013265920 | bytes 3145728 | tf_op jit(solution)/shard_map/attend_back/pallas_call | solution.py:191
  100.1 3.9 %all-to-all-start.2 = ((bf16[8,192,384]{2,1,0:T(8,128)(2,1)}), bf16[8,192,384]{2,1,0:T(8,128)(2,1)S(1)}, u32[]{:S(2)}, u32[]{:S(2)}) async-start(bf16[8,192,384]{2,1,0:T(8,128)(2,1)} %bitcast.6), calls=%async_computation.2 | async-start | bytes 2359296 | tf_op jit(solution)/shard_map/all_to_all | solution.py:575
  104.3 5.5 %qkv_product.1 = (bf16[2,8,32,384]{3,2,1,0:T(8,128)(2,1)}, bf16[8,32,384]{2,1,0:T(8,128)(2,1)}, bf16[8,32,384]{2,1,0:T(8,128)(2,1)}) custom-call(s32[2]{0:T(128)} %pad_add_fusion.places, bf16[1536,1024]{1,0:T(8,128)(2,1)} %get-tuple-element.69.left, bf16[1536,384]{1,0:T(8,128)(2,1)} %attend_back.1.right), custom_call_target="tpu_custom_call" | custom-call | flops 1207959552 | bytes 4325376 | tf_op jit(solution)/shard_map/qkv_product/pallas_call | solution.py:490
  112.2 12.8 %feed_products.1 = (bf16[2,8,32,512]{3,2,1,0:T(8,128)(2,1)}, bf16[8,32,512]{2,1,0:T(8,128)(2,1)}, bf16[8,32,512]{2,1,0:T(8,128)(2,1)}, bf16[2,1,128,1024]{3,2,1,...) custom-call(s32[2]{0:T(128)} %pad_add_fusion.places, ...), custom_call_target="tpu_custom_call" | custom-call | flops 6442450944 | bytes 8388608 | tf_op jit(solution)/shard_map/feed_products/pallas_call | solution.py:545
  126.6 2.5 %collective-permute-start.9 = (bf16[8,32,384]{2,1,0:T(8,128)(2,1)S(1)}, bf16[8,32,384]{2,1,0:T(8,128)(2,1)S(1)}, u32[]{:S(2)}, u32[]{:S(2)}) collective-permute-start(bf16[8,32,384]{2,1,0:T(8,128)(2,1)S(1)} %fusion.6), channel_id=1, source_target_pairs={{0,2},{1,3},{2,0},{3,1},{4,6},{5,7},{6,4},{7,5},{8,10},{9,11},{10,... | collective-permute-start | bytes 589832 | tf_op jit(solution)/shard_map/ppermute | solution.py:597
  129.1 7.2 %project_back.1 = (bf16[192,1024]{1,0:T(8,128)(2,1)}, f32[2,1024]{1,0:T(2,128)}) custom-call(bf16[192,1024]{1,0:T(8,128)(2,1)} %bitcast.72, bf16[1024]{0:T(1024)(128)(2,1)} %gain.3, f32[192,1024]{1,0:T(8,128)} %get-tuple-element.64.grad_middle, bf16[8,192,384]{2,1,0:T(8,128)(2,1)} %copy-done.4, bf16[1024,1024]{1,0:T(8,128)(2,1)} %w_query.1, ...), custom_call_target="tpu_custom_call" | custom-call | flops 1207959552 | bytes 6291456 | tf_op jit(solution)/shard_map/project_back/pallas_call | solution.py:298
  137.9 5.5 %all-to-all-start.3 = ((f32[32,1,288]{2,1,0:T(1,128)}), f32[32,1,288]{2,1,0:T(1,128)S(1)}, u32[]{:S(2)}, u32[]{:S(2)}) async-start(f32[32,1,288]{2,1,0:T(1,128)} %all_to_all.23), calls=%async_computation.3 | async-start | bytes 98304 | tf_op jit(solution)/shard_map/all_to_all | solution.py:575
  143.5 1.8 collective-permute-start.13
  145.3 5.9 %all-to-all-done.3 = f32[32,1,288]{2,1,0:T(1,128)S(1)} async-done(((f32[32,1,288]{2,1,0:T(1,128)}), f32[32,1,288]{2,1,0:T(1,128)S(1)}, u32[]{:S(2)}, u32[]{:S(2)}) %all-to-all-start.3) | async-done | bytes 36896 | tf_op jit(solution)/shard_map/all_to_all | solution.py:575
  151.9 3.9 %out_product.1 = (bf16[2,1,32,1024]{3,2,1,0:T(8,128)(2,1)}, bf16[1,32,1024]{2,1,0:T(8,128)(2,1)}, bf16[1,32,1024]{2,1,0:T(8,128)(2,1)}) custom-call(s32[2]{0:T(128)} %pad_add_fusion.places, bf16[1536,128]{1,0:T(8,128)(2,1)} %copy-done, bf16[1536,1024]{1,0:T(8,128)(2,1)} %all-gather.8.cloned.1.call-done.right), custom_call_target="tpu_custom_call" | custom-call | flops 402653184 | bytes 3538944 | tf_op jit(solution)/shard_map/out_product/pallas_call | solution.py:490
  158.0 8.9 %collective-permute-done.11 = bf16[2,1,32,1024]{3,2,1,0:T(8,128)(2,1)S(1)} collective-permute-done((bf16[2,1,32,1024]{3,2,1,0:T(8,128)(2,1)}, bf16[2,1,32,1024]{3,2,1,0:T(8,128)(2,1)S(1)}, u32[]{:S(2)}, u32[]{:S(2)}) %collective-permute-start.11) | collective-permute-done | bytes 131104 | tf_op jit(solution)/shard_map/ppermute | solution.py:597
  167.8 2.4 %collective-permute-start.12 = (bf16[1,32,1024]{2,1,0:T(8,128)(2,1)S(1)}, bf16[1,32,1024]{2,1,0:T(8,128)(2,1)S(1)}, u32[]{:S(2)}, u32[]{:S(2)}) collective-permute-start(bf16[1,32,1024]{2,1,0:T(8,128)(2,1)S(1)} %fusion.7), channel_id=1, source_target_pairs={{0,2},{1,3},{2,0},{3,1},{4,6},{5,7},{6,4},{7,5},{8,10},{9,11},{10,... | collective-permute-start | bytes 196616 | tf_op jit(solution)/shard_map/ppermute | solution.py:597
  171.9 3.8 %all-to-all-start.4 = ((bf16[8,32,896]{2,1,0:T(8,128)(2,1)}), bf16[8,32,896]{2,1,0:T(8,128)(2,1)S(1)}, u32[]{:S(2)}, u32[]{:S(2)}) async-start(bf16[8,32,896]{2,1,0:T(8,128)(2,1)} %pad_maximum_fusion), calls=%async_computation.4 | async-start | bytes 917504 | tf_op jit(solution)/shard_map/all_to_all | solution.py:575
  175.7 3.8 %collective-permute-done.12 = bf16[1,32,1024]{2,1,0:T(8,128)(2,1)S(1)} collective-permute-done((bf16[1,32,1024]{2,1,0:T(8,128)(2,1)S(1)}, bf16[1,32,1024]{2,1,0:T(8,128)(2,1)S(1)}, u32[]{:S(2)}, u32[]{:S(2)}) %collective-permute-start.12) | collective-permute-done | bytes 65568 | tf_op jit(solution)/shard_map/ppermute | solution.py:597
  180.2 4.8 %collective-permute-done.14 = bf16[1,128,1024]{2,1,0:T(8,128)(2,1)S(1)} collective-permute-done((bf16[1,128,1024]{2,1,0:T(8,128)(2,1)S(1)}, bf16[1,128,1024]{2,1,0:T(8,128)(2,1)S(1)}, u32[]{:S(2)}, u32[]{:S(2)}) %collective-permute-start.14) | collective-permute-done | bytes 262176 | tf_op jit(solution)/shard_map/ppermute | solution.py:597
  (113 shorter events, 23.3 us)
Async XLA Ops:
  7.2 82.5 %all-gather.4.cloned.1.call-start = ((), (), s32[]{:S(2)}) async-start(), calls=%async_computation.5 | async-start | bytes 3538944 | tf_op jit(solution)/shard_map/all_gather | solution.py:579
  7.2 13.2 %collective-permute-start.1 = (bf16[192,1024]{1,0:T(8,128)(2,1)}, bf16[192,1024]{1,0:T(8,128)(2,1)S(1)}, u32[]{:S(2)}, u32[]{:S(2)}) collective-permute-start(bf16[192,1024]{1,0:T(8,128)(2,1)} %bitcast.66), channel_id=1, source_target_pairs={{0,8},{4,12},{8,0},{12,4},{16,24},{20,28},{24,16},{28,20},{1,9},{5... | collective-permute-start | bytes 1179656 | tf_op jit(solution)/shard_map/ppermute | solution.py:586
  10.2 19.2 %collective-permute-start.3 = (bf16[192,1024]{1,0:T(8,128)(2,1)}, bf16[192,1024]{1,0:T(8,128)(2,1)S(1)}, u32[]{:S(2)}, u32[]{:S(2)}) collective-permute-start(bf16[192,1024]{1,0:T(8,128)(2,1)} %bitcast.67), channel_id=1, source_target_pairs={{0,16},{4,20},{8,24},{12,28},{16,0},{20,4},{24,8},{28,12},{1,17},{... | collective-permute-start | bytes 1179656 | tf_op jit(solution)/shard_map/ppermute | solution.py:586
  11.7 17.7 %collective-permute-start.5 = (bf16[192,1024]{1,0:T(8,128)(2,1)}, bf16[192,1024]{1,0:T(8,128)(2,1)S(1)}, u32[]{:S(2)}, u32[]{:S(2)}) collective-permute-start(bf16[192,1024]{1,0:T(8,128)(2,1)} %bitcast.68), channel_id=1, source_target_pairs={{0,24},{4,28},{8,16},{12,20},{16,8},{20,12},{24,0},{28,4},{1,25},{... | collective-permute-start | bytes 1179656 | tf_op jit(solution)/shard_map/ppermute | solution.py:586
  11.8 18.7 %collective-permute-start = (bf16[192,1024]{1,0:T(8,128)(2,1)}, bf16[192,1024]{1,0:T(8,128)(2,1)S(1)}, u32[]{:S(2)}, u32[]{:S(2)}) collective-permute-start(bf16[192,1024]{1,0:T(8,128)(2,1)} %bitcast.69), channel_id=1, source_target_pairs={{0,4},{4,0},{8,12},{12,8},{16,20},{20,16},{24,28},{28,24},{1,5},{5... | collective-permute-start | bytes 1179656 | tf_op jit(solution)/shard_map/ppermute | solution.py:586
  20.4 10.1 %collective-permute-start.2 = (bf16[192,1024]{1,0:T(8,128)(2,1)S(1)}, bf16[192,1024]{1,0:T(8,128)(2,1)S(1)}, u32[]{:S(2)}, u32[]{:S(2)}) collective-permute-start(bf16[192,1024]{1,0:T(8,128)(2,1)S(1)} %collective-permute-done.1.refs_2_), channel_id=1, source_target_pairs={{0,4},{4,0},{8,12},{12,8},{16,20},{20,16},{24,28},{28,24},{1,5},{5... | collective-permute-start | bytes 1179656 | tf_op jit(solution)/shard_map/ppermute | solution.py:586
  29.4 1.7 collective-permute-start.4
  29.5 2.3 %collective-permute-start.6 = (bf16[192,1024]{1,0:T(8,128)(2,1)S(1)}, bf16[192,1024]{1,0:T(8,128)(2,1)S(1)}, u32[]{:S(2)}, u32[]{:S(2)}) collective-permute-start(bf16[192,1024]{1,0:T(8,128)(2,1)S(1)} %collective-permute-done.5.refs_6_), channel_id=1, source_target_pairs={{0,4},{4,0},{8,12},{12,8},{16,20},{20,16},{24,28},{28,24},{1,5},{5... | collective-permute-start | bytes 1179656 | tf_op jit(solution)/shard_map/ppermute | solution.py:586
  40.4 71.8 %all-gather.6.cloned.1.call-start = ((), (), s32[]{:S(2)}) async-start(), calls=%async_computation.6 | async-start | bytes 3538944 | tf_op jit(solution)/shard_map/all_gather | solution.py:579
  48.2 28.6 %copy-start = (bf16[1536,128]{1,0:T(8,128)(2,1)}, bf16[1536,128]{1,0:T(8,128)(2,1)S(1)}, u32[]{:S(2)}) copy-start(bf16[1536,128]{1,0:T(8,128)(2,1)S(1)} %get-tuple-element.92.left) | copy-start | bytes 1179652
  60.4 29.3 %copy-start.2 = (bf16[1536,384]{1,0:T(8,128)(2,1)S(1)}, bf16[1536,384]{1,0:T(8,128)(2,1)}, u32[]{:S(2)}) copy-start(bf16[1536,384]{1,0:T(8,128)(2,1)} %get-tuple-element.61.qkv) | copy-start | bytes 3538948
  76.8 75.0 %all-gather.8.cloned.1.call-start = ((), (), s32[]{:S(2)}) async-start(), calls=%async_computation.7 | async-start | bytes 3538944 | tf_op jit(solution)/shard_map/all_gather | solution.py:579
  77.5 12.2 %all-to-all-start.1 = ((bf16[8,192,128]{2,1,0:T(8,128)(2,1)}), bf16[8,192,128]{2,1,0:T(8,128)(2,1)S(1)}, u32[]{:S(2)}, u32[]{:S(2)}) async-start(bf16[8,192,128]{2,1,0:T(8,128)(2,1)} %get-tuple-element.66), calls=%async_computation.1 | async-start | bytes 786432 | tf_op jit(solution)/shard_map/all_to_all | solution.py:575
  100.1 26.5 %all-to-all-start.2 = ((bf16[8,192,384]{2,1,0:T(8,128)(2,1)}), bf16[8,192,384]{2,1,0:T(8,128)(2,1)S(1)}, u32[]{:S(2)}, u32[]{:S(2)}) async-start(bf16[8,192,384]{2,1,0:T(8,128)(2,1)} %bitcast.6), calls=%async_computation.2 | async-start | bytes 2359296 | tf_op jit(solution)/shard_map/all_to_all | solution.py:575
  109.8 16.7 %collective-permute-start.7 = (bf16[2,8,32,384]{3,2,1,0:T(8,128)(2,1)}, bf16[2,8,32,384]{3,2,1,0:T(8,128)(2,1)S(1)}, u32[]{:S(2)}, u32[]{:S(2)}) collective-permute-start(bf16[2,8,32,384]{3,2,1,0:T(8,128)(2,1)} %get-tuple-element.71), channel_id=1, source_target_pairs={{0,1},{1,0},{2,3},{3,2},{4,5},{5,4},{6,7},{7,6},{8,9},{9,8},{10,11... | collective-permute-start | bytes 1179656 | tf_op jit(solution)/shard_map/ppermute | solution.py:597
  125.0 26.2 %collective-permute-start.8 = (bf16[2,8,32,512]{3,2,1,0:T(8,128)(2,1)}, bf16[2,8,32,512]{3,2,1,0:T(8,128)(2,1)S(1)}, u32[]{:S(2)}, u32[]{:S(2)}) collective-permute-start(bf16[2,8,32,512]{3,2,1,0:T(8,128)(2,1)} %get-tuple-element.82), channel_id=1, source_target_pairs={{0,1},{1,0},{2,3},{3,2},{4,5},{5,4},{6,7},{7,6},{8,9},{9,8},{10,11... | collective-permute-start | bytes 1572872 | tf_op jit(solution)/shard_map/ppermute | solution.py:597
  126.6 24.6 %collective-permute-start.9 = (bf16[8,32,384]{2,1,0:T(8,128)(2,1)S(1)}, bf16[8,32,384]{2,1,0:T(8,128)(2,1)S(1)}, u32[]{:S(2)}, u32[]{:S(2)}) collective-permute-start(bf16[8,32,384]{2,1,0:T(8,128)(2,1)S(1)} %fusion.6), channel_id=1, source_target_pairs={{0,2},{1,3},{2,0},{3,1},{4,6},{5,7},{6,4},{7,5},{8,10},{9,11},{10,... | collective-permute-start | bytes 589832 | tf_op jit(solution)/shard_map/ppermute | solution.py:597
  137.9 13.2 %all-to-all-start.3 = ((f32[32,1,288]{2,1,0:T(1,128)}), f32[32,1,288]{2,1,0:T(1,128)S(1)}, u32[]{:S(2)}, u32[]{:S(2)}) async-start(f32[32,1,288]{2,1,0:T(1,128)} %all_to_all.23), calls=%async_computation.3 | async-start | bytes 98304 | tf_op jit(solution)/shard_map/all_to_all | solution.py:575
  143.5 26.8 %collective-permute-start.13 = (bf16[2,1,128,1024]{3,2,1,0:T(8,128)(2,1)}, bf16[2,1,128,1024]{3,2,1,0:T(8,128)(2,1)S(1)}, u32[]{:S(2)}, u32[]{:S(2)}) collective-permute-start(bf16[2,1,128,1024]{3,2,1,0:T(8,128)(2,1)} %get-tuple-element.104), channel_id=1, source_target_pairs={{0,1},{1,0},{2,3},{3,2},{4,5},{5,4},{6,7},{7,6},{8,9},{9,8},{10,11... | collective-permute-start | bytes 1572872 | tf_op jit(solution)/shard_map/ppermute | solution.py:597
  151.4 15.5 %collective-permute-start.10 = (bf16[8,32,512]{2,1,0:T(8,128)(2,1)S(1)}, bf16[8,32,512]{2,1,0:T(8,128)(2,1)S(1)}, u32[]{:S(2)}, u32[]{:S(2)}) collective-permute-start(bf16[8,32,512]{2,1,0:T(8,128)(2,1)S(1)} %get-tuple-element.111), channel_id=1, source_target_pairs={{0,2},{1,3},{2,0},{3,1},{4,6},{5,7},{6,4},{7,5},{8,10},{9,11},{10,... | collective-permute-start | bytes 786440 | tf_op jit(solution)/shard_map/ppermute | solution.py:597
  155.8 11.2 %collective-permute-start.11 = (bf16[2,1,32,1024]{3,2,1,0:T(8,128)(2,1)}, bf16[2,1,32,1024]{3,2,1,0:T(8,128)(2,1)S(1)}, u32[]{:S(2)}, u32[]{:S(2)}) collective-permute-start(bf16[2,1,32,1024]{3,2,1,0:T(8,128)(2,1)} %get-tuple-element.94), channel_id=1, source_target_pairs={{0,1},{1,0},{2,3},{3,2},{4,5},{5,4},{6,7},{7,6},{8,9},{9,8},{10,11... | collective-permute-start | bytes 393224 | tf_op jit(solution)/shard_map/ppermute | solution.py:597
  167.8 11.7 %collective-permute-start.12 = (bf16[1,32,1024]{2,1,0:T(8,128)(2,1)S(1)}, bf16[1,32,1024]{2,1,0:T(8,128)(2,1)S(1)}, u32[]{:S(2)}, u32[]{:S(2)}) collective-permute-start(bf16[1,32,1024]{2,1,0:T(8,128)(2,1)S(1)} %fusion.7), channel_id=1, source_target_pairs={{0,2},{1,3},{2,0},{3,1},{4,6},{5,7},{6,4},{7,5},{8,10},{9,11},{10,... | collective-permute-start | bytes 196616 | tf_op jit(solution)/shard_map/ppermute | solution.py:597
  170.4 14.6 %collective-permute-start.14 = (bf16[1,128,1024]{2,1,0:T(8,128)(2,1)S(1)}, bf16[1,128,1024]{2,1,0:T(8,128)(2,1)S(1)}, u32[]{:S(2)}, u32[]{:S(2)}) collective-permute-start(bf16[1,128,1024]{2,1,0:T(8,128)(2,1)S(1)} %fusion), channel_id=1, source_target_pairs={{0,2},{1,3},{2,0},{3,1},{4,6},{5,7},{6,4},{7,5},{8,10},{9,11},{10,... | collective-permute-start | bytes 786440 | tf_op jit(solution)/shard_map/ppermute | solution.py:597
  171.9 14.1 %all-to-all-start.4 = ((bf16[8,32,896]{2,1,0:T(8,128)(2,1)}), bf16[8,32,896]{2,1,0:T(8,128)(2,1)S(1)}, u32[]{:S(2)}, u32[]{:S(2)}) async-start(bf16[8,32,896]{2,1,0:T(8,128)(2,1)} %pad_maximum_fusion), calls=%async_computation.4 | async-start | bytes 917504 | tf_op jit(solution)/shard_map/all_to_all | solution.py:575
  (22 other events, 206.0 us)
Sparse Core Ops, SparseCore 0:
  40.5 34.9 all-gather.3
  77.9 34.2 all-gather.5
  114.1 35.8 all-gather.7

commit v6 on v5

--- a/solution.py
+++ b/solution.py
@@ -510,6 +510,38 @@
     )(places, left, right)
 
 
+def whole_product_kernel(left, right, result, total):
+    accumulate(total, matmul_left(left[...], right[...]))
+
+    @pl.when(pl.program_id(0) == pl.num_programs(0) - 1)
+    def _():
+        result[...] = total[...].astype(low)
+
+
+def whole_product(left, right, name):
+    tokens, columns = right.shape
+    rows = left.shape[1]
+    chunk = 768
+    return pl.pallas_call(
+        whole_product_kernel,
+        grid=(tokens // chunk,),
+        in_specs=[
+            pl.BlockSpec((chunk, rows), lambda j: (j, 0)),
+            pl.BlockSpec((chunk, columns), lambda j: (j, 0)),
+        ],
+        out_specs=pl.BlockSpec((rows, columns), lambda j: (0, 0)),
+        out_shape=jax.ShapeDtypeStruct((rows, columns), low),
+        scratch_shapes=[pltpu.VMEM((rows, columns), full)],
+        compiler_params=pltpu.CompilerParams(vmem_limit_bytes=vmem_limit),
+        cost_estimate=pl.CostEstimate(
+            flops=2 * tokens * rows * columns,
+            bytes_accessed=2 * tokens * (rows + columns),
+            transcendentals=0,
+        ),
+        name=name,
+    )(left, right)
+
+
 def feed_products_kernel(
     places,
     normed,
@@ -720,26 +752,20 @@
     in_own, in_other = first_sum(in_got, in_own, in_other)
     in_last = trade(in_other, 2)
     own_rows = width // copies
+    back_own, back_other = first_sum(back_got, back_own, back_other)
     own_attended, in_own = together(attended_all, in_own)
     if copies > 1:
         at = lax.axis_index("seq") % copies * own_rows
         own_attended = lax.dynamic_slice_in_dim(own_attended, at, own_rows, axis=1)
-    out_sent, out_own, out_other = product(
-        places, own_attended, own_rows, grad_middle_all, 1, "out_product"
-    )
-    out_got = trade(out_sent, 1)
-    in_last, out_got = together(in_last, out_got)
+    out_partial = whole_product(own_attended, grad_middle_all, "out_product")
+    out_rows = lax.psum_scatter(out_partial, "batch", scatter_dimension=0, tiled=True).astype(full)
+    in_last, back_other = together(in_last, back_other)
     mixed = [
         (own + last.astype(full)).astype(low)
         for own, last in ((in_own, in_last), (qkv_own, qkv_last))
     ]
     mixed = swap(jnp.concatenate(mixed, axis=2), "seq")
-    out_own, out_other = first_sum(out_got, out_own, out_other)
-    out_last = trade(out_other, 2)
-    back_own, out_last = together(back_own, out_last)
-    back_own, back_other = first_sum(back_got, back_own, back_other)
     back_rows = (back_own + trade(back_other, 2).astype(full))[0]
-    out_rows = (out_own + out_last.astype(full))[0]
     in_rows = mixed[:, :, :inner_columns].transpose(1, 0, 2).reshape(slim, ff_width).astype(full)
     qkv_rows = mixed[::copies, :, inner_columns:].transpose(1, 0, 2).astype(full)
     qkv_rows = [

time: 196 us -> 192 us (0.980)
  starting transfers between devices: 33.7 us -> 31.6 us
    pallas_call x2 -> x1, Pallas kernels: 9.45 us -> 5.55 us  [product(): pl.pallas_call(product_kernel, grid_spec=pltpu.PrefetchScalarGridSpec(num...]
    pallas_call x0 -> x1, Pallas kernels: none -> 3.23 us  [whole_product(): pl.pallas_call(whole_product_kernel, grid=(tokens // chunk,), in_specs=[p...]
    ppermute x8 -> x6, waiting for transfers between devices: 17.5 us -> 14.4 us  [trade(): return lax.ppermute(block, 'batch', [(i, i ^ distance) for i in range(4)])]
    reduce_scatter x0 -> x1, waiting for transfers between devices: none -> 2.32 us  [shards(): lax.psum_scatter(out_partial, 'batch', scatter_dimension=0, tiled=True)]
    ppermute x8 -> x6, starting transfers between devices: 11.8 us -> 9.93 us  [trade(): return lax.ppermute(block, 'batch', [(i, i ^ distance) for i in range(4)])]
  transfers between devices with their start and end apart: 22 -> 21, of which waited for: 10 -> 10; matrix products, arithmetic and copies ran while one was open for 4% -> 4% of each run, Pallas kernels for 32% -> 32%
where the time goes in v6:
time: 192 us; the launch traced here: 191 us
  Pallas kernels  69 us (36%)
  waiting for transfers between devices  50.6 us (26%)
  starting transfers between devices  31.6 us (16%)
  between operations  14.7 us (8%)
  blocking collectives  12.2 us (6%)
  local copies, waits for them, and re-layouts  8.23 us (4%)
  other arithmetic  4.82 us (3%)
    ppermute x7, waiting for transfers between devices, move(): return lax.ppermute(block, 'seq', [(i, i ^ distance) for i in range(count)])  18.9 us
    all_to_all x4, starting transfers between devices, swap(): return lax.all_to_all(blocks, axes, split_axis=0, concat_axis=0, tiled=True)  16.5 us
    pallas_call x1, Pallas kernels, feed(): pl.pallas_call(feed_kernel, out_shape=(jax.ShapeDtypeStruct((tokens, mode...  16.3 us
    ppermute x6, waiting for transfers between devices, trade(): return lax.ppermute(block, 'batch', [(i, i ^ distance) for i in range(4)])  14.4 us
    all_to_all x4, waiting for transfers between devices, swap(): return lax.all_to_all(blocks, axes, split_axis=0, concat_axis=0, tiled=True)  13.3 us
    pallas_call x1, Pallas kernels, feed_products(): pl.pallas_call(feed_products_kernel, grid_spec=pltpu.PrefetchScalarGridSp...  12.8 us
    all_to_all x1, blocking collectives, swap(): return lax.all_to_all(blocks, axes, split_axis=0, concat_axis=0, tiled=True)  12.2 us
    pallas_call x1, Pallas kernels, attend_back(): pl.pallas_call(functools.partial(attend_back_kernel, block_count, head_co...  10.4 us
  transfers between devices with their start and end apart: 21, of which 10 were waited for; matrix products, arithmetic and copies ran while one was open for 4% of the time, Pallas kernels for 32%

profile of v6, /device:TPU:0, one launch (start us, length us, event | category | flops | bytes accessed | tf_op | source)
XLA Modules:
  0.0 191.2 jit_solution(10877507341802411106)
XLA Ops:
  7.2 3.0 %collective-permute-start.1 = (bf16[192,1024]{1,0:T(8,128)(2,1)}, bf16[192,1024]{1,0:T(8,128)(2,1)S(1)}, u32[]{:S(2)}, u32[]{:S(2)}) collective-permute-start(bf16[192,1024]{1,0:T(8,128)(2,1)} %bitcast.58), channel_id=1, source_target_pairs={{0,8},{4,12},{8,0},{12,4},{16,24},{20,28},{24,16},{28,20},{1,9},{5... | collective-permute-start | bytes 1179656 | tf_op jit(solution)/shard_map/ppermute | solution.py:618
  11.8 8.6 %collective-permute-done.1.refs_2_ = bf16[192,1024]{1,0:T(8,128)(2,1)S(1)} collective-permute-done((bf16[192,1024]{1,0:T(8,128)(2,1)}, bf16[192,1024]{1,0:T(8,128)(2,1)S(1)}, u32[]{:S(2)}, u32[]{:S(2)}) %collective-permute-start.1) | collective-permute-done | bytes 393248 | tf_op jit(solution)/shard_map/ppermute | solution.py:618
  20.4 9.1 %collective-permute-done.3.refs_4_ = bf16[192,1024]{1,0:T(8,128)(2,1)S(1)} collective-permute-done((bf16[192,1024]{1,0:T(8,128)(2,1)}, bf16[192,1024]{1,0:T(8,128)(2,1)S(1)}, u32[]{:S(2)}, u32[]{:S(2)}) %collective-permute-start.3) | collective-permute-done | bytes 393248 | tf_op jit(solution)/shard_map/ppermute | solution.py:618
  32.5 7.8 %project.1 = (bf16[1536,384]{1,0:T(8,128)(2,1)}, bf16[1536,1024]{1,0:T(8,128)(2,1)}) custom-call(s32[8]{0:T(128)} %iota_xor_fusion.rows, s32[1]{0:T(128)} %bitcast.1.column, bf16[192,1024]{1,0:T(8,128)(2,1)} %bitcast.62, bf16[192,1024]{1,0:T(8,128)(2,1)} %copy-done.8, bf16[192,1024]{1,0:T(8,128)(2,1)} %copy-done.5, bf16[192,1024]{1,0:T(8,128)(2,1)} %copy-done.9, ...), custom_call_target="tpu_custom_call" | custom-call | flops 1207959552 | bytes 6291456 | tf_op jit(solution)/shard_map/project/pallas_call | solution.py:238
  42.5 5.7 %attend.1 = (bf16[1536,128]{1,0:T(8,128)(2,1)S(1)}, f32[24,1,128]{2,1,0:T(1,128)S(1)}) custom-call(s32[1,1]{1,0:T(1,128)S(6)} %copy.63.lens, s32[1,24,3]{2,1,0:T(8,128)S(1)} %copy.44.owners, s32[1,24,3]{2,1,0:T(8,128)S(1)} %copy.45.offsets, s32[1,1,2]{2,1,0:T(1,128)S(1)} %copy-done.3, bf16[1536,384]{1,0:T(8,128)(2,1)S(1)} %copy-done.1), custom_call_target="tpu_custom_call" | custom-call | flops 805306368 | bytes 1572864 | tf_op jit(solution)/shard_map/attend/pallas_call | solution.py:172
  48.2 12.2 %all_to_all.32.received = bf16[8,192,128]{2,1,0:T(8,128)(2,1)} all-to-all(bf16[8,192,128]{2,1,0:T(8,128)(2,1)S(1)} %bitcast.56), channel_id=1, replica_groups=mesh['seq'=8,'batch'=4] {'seq'}, dimensions={0} | all-to-all | bytes 786432 | tf_op jit(solution)/shard_map/all_to_all | solution.py:607
  60.4 16.3 %feed.1 = (bf16[192,1024]{1,0:T(8,128)(2,1)}, bf16[192,1024]{1,0:T(8,128)(2,1)}, f32[192,1024]{1,0:T(8,128)}, bf16[192,1024]{1,0:T(8,128)(2,1)}, bf16[8,192,128]...) custom-call(bf16[8,192,128]{2,1,0:T(8,128)(2,1)} %all_to_all.32.received, bf16[192,1024]{1,0:T(8,128)(2,1)} %bitcast.63, ...), custom_call_target="tpu_custom_call" | custom-call | flops 6442450944 | bytes 16777216 | tf_op jit(solution)/shard_map/feed/pallas_call | solution.py:418
  77.5 3.5 %all-to-all-start.1 = ((bf16[8,192,128]{2,1,0:T(8,128)(2,1)}), bf16[8,192,128]{2,1,0:T(8,128)(2,1)S(1)}, u32[]{:S(2)}, u32[]{:S(2)}) async-start(bf16[8,192,128]{2,1,0:T(8,128)(2,1)} %get-tuple-element.61), calls=%async_computation.1 | async-start | bytes 786432 | tf_op jit(solution)/shard_map/all_to_all | solution.py:607
  82.2 7.4 %all-to-all-done.1 = bf16[8,192,128]{2,1,0:T(8,128)(2,1)S(1)} async-done(((bf16[8,192,128]{2,1,0:T(8,128)(2,1)}), bf16[8,192,128]{2,1,0:T(8,128)(2,1)S(1)}, u32[]{:S(2)}, u32[]{:S(2)}) %all-to-all-start.1) | async-done | bytes 393248 | tf_op jit(solution)/shard_map/all_to_all | solution.py:607
  89.7 10.4 %attend_back.1.right = bf16[1536,384]{1,0:T(8,128)(2,1)} custom-call(s32[1,1]{1,0:T(1,128)S(6)} %copy.63.lens, s32[1,24,3]{2,1,0:T(8,128)S(1)} %copy.44.owners, s32[1,24,3]{2,1,0:T(8,128)S(1)} %copy.45.offsets, s32[1,1,2]{2,1,0:T(1,128)S(1)} %copy-done.3, bf16[1536,384]{1,0:T(8,128)(2,1)S(1)} %copy-done.2, f32[24,1,128]{2,1,0:T(1,128)S(1)} %get-tuple-element.60.log_total, ...), custom_call_target="tpu_custom_call" | custom-call | flops 2013265920 | bytes 3145728 | tf_op jit(solution)/shard_map/attend_back/pallas_call | solution.py:191
  100.1 3.9 %all-to-all-start.2 = ((bf16[8,192,384]{2,1,0:T(8,128)(2,1)}), bf16[8,192,384]{2,1,0:T(8,128)(2,1)S(1)}, u32[]{:S(2)}, u32[]{:S(2)}) async-start(bf16[8,192,384]{2,1,0:T(8,128)(2,1)} %bitcast.6), calls=%async_computation.2 | async-start | bytes 2359296 | tf_op jit(solution)/shard_map/all_to_all | solution.py:607
  104.3 5.6 %qkv_product.1 = (bf16[2,8,32,384]{3,2,1,0:T(8,128)(2,1)}, bf16[8,32,384]{2,1,0:T(8,128)(2,1)}, bf16[8,32,384]{2,1,0:T(8,128)(2,1)}) custom-call(s32[2]{0:T(128)} %pad_add_fusion.places, bf16[1536,1024]{1,0:T(8,128)(2,1)} %get-tuple-element.64.left, bf16[1536,384]{1,0:T(8,128)(2,1)} %attend_back.1.right), custom_call_target="tpu_custom_call" | custom-call | flops 1207959552 | bytes 4325376 | tf_op jit(solution)/shard_map/qkv_product/pallas_call | solution.py:490
  112.2 12.8 %feed_products.1 = (bf16[2,8,32,512]{3,2,1,0:T(8,128)(2,1)}, bf16[8,32,512]{2,1,0:T(8,128)(2,1)}, bf16[8,32,512]{2,1,0:T(8,128)(2,1)}, bf16[2,1,128,1024]{3,2,1,...) custom-call(s32[2]{0:T(128)} %pad_add_fusion.places, ...), custom_call_target="tpu_custom_call" | custom-call | flops 6442450944 | bytes 8388608 | tf_op jit(solution)/shard_map/feed_products/pallas_call | solution.py:577
  126.6 2.5 %collective-permute-start.9 = (bf16[8,32,384]{2,1,0:T(8,128)(2,1)S(1)}, bf16[8,32,384]{2,1,0:T(8,128)(2,1)S(1)}, u32[]{:S(2)}, u32[]{:S(2)}) collective-permute-start(bf16[8,32,384]{2,1,0:T(8,128)(2,1)S(1)} %fusion.6), channel_id=1, source_target_pairs={{0,2},{1,3},{2,0},{3,1},{4,6},{5,7},{6,4},{7,5},{8,10},{9,11},{10,... | collective-permute-start | bytes 589832 | tf_op jit(solution)/shard_map/ppermute | solution.py:629
  129.1 7.2 %project_back.1 = (bf16[192,1024]{1,0:T(8,128)(2,1)}, f32[2,1024]{1,0:T(2,128)}) custom-call(bf16[192,1024]{1,0:T(8,128)(2,1)} %bitcast.64, bf16[1024]{0:T(1024)(128)(2,1)} %gain.3, f32[192,1024]{1,0:T(8,128)} %get-tuple-element.59.grad_middle, bf16[8,192,384]{2,1,0:T(8,128)(2,1)} %copy-done.4, bf16[1024,1024]{1,0:T(8,128)(2,1)} %w_query.1, ...), custom_call_target="tpu_custom_call" | custom-call | flops 1207959552 | bytes 6291456 | tf_op jit(solution)/shard_map/project_back/pallas_call | solution.py:298
  138.0 5.5 %all-to-all-start.3 = ((f32[32,1,288]{2,1,0:T(1,128)}), f32[32,1,288]{2,1,0:T(1,128)S(1)}, u32[]{:S(2)}, u32[]{:S(2)}) async-start(f32[32,1,288]{2,1,0:T(1,128)} %all_to_all.23), calls=%async_computation.3 | async-start | bytes 98304 | tf_op jit(solution)/shard_map/all_to_all | solution.py:607
  143.6 1.8 collective-permute-start.11
  145.4 5.8 %all-to-all-done.3 = f32[32,1,288]{2,1,0:T(1,128)S(1)} async-done(((f32[32,1,288]{2,1,0:T(1,128)}), f32[32,1,288]{2,1,0:T(1,128)S(1)}, u32[]{:S(2)}, u32[]{:S(2)}) %all-to-all-start.3) | async-done | bytes 36896 | tf_op jit(solution)/shard_map/all_to_all | solution.py:607
  151.9 3.2 %out_product.1 = bf16[128,1024]{1,0:T(8,128)(2,1)} custom-call(bf16[1536,128]{1,0:T(8,128)(2,1)} %copy-done, bf16[1536,1024]{1,0:T(8,128)(2,1)} %all-gather.8.cloned.1.call-done.right), custom_call_target="tpu_custom_call" | custom-call | flops 402653184 | bytes 3538944 | tf_op jit(solution)/shard_map/out_product/pallas_call | solution.py:525
  155.9 9.5 %collective-permute-done.11 = bf16[2,1,128,1024]{3,2,1,0:T(8,128)(2,1)S(1)} collective-permute-done((bf16[2,1,128,1024]{3,2,1,0:T(8,128)(2,1)}, bf16[2,1,128,1024]{3,2,1,0:T(8,128)(2,1)S(1)}, u32[]{:S(2)}, u32[]{:S(2)}) %collective-permute-start.11) | collective-permute-done | bytes 524320 | tf_op jit(solution)/shard_map/ppermute | solution.py:629
  165.4 2.2 %collective-permute-start.12 = (bf16[1,128,1024]{2,1,0:T(8,128)(2,1)S(1)}, bf16[1,128,1024]{2,1,0:T(8,128)(2,1)S(1)}, u32[]{:S(2)}, u32[]{:S(2)}) collective-permute-start(bf16[1,128,1024]{2,1,0:T(8,128)(2,1)S(1)} %fusion.2), channel_id=1, source_target_pairs={{0,2},{1,3},{2,0},{3,1},{4,6},{5,7},{6,4},{7,5},{8,10},{9,11},{10,... | collective-permute-start | bytes 786440 | tf_op jit(solution)/shard_map/ppermute | solution.py:629
  168.5 3.6 %all-to-all-start.4 = ((bf16[8,32,896]{2,1,0:T(8,128)(2,1)}), bf16[8,32,896]{2,1,0:T(8,128)(2,1)S(1)}, u32[]{:S(2)}, u32[]{:S(2)}) async-start(bf16[8,32,896]{2,1,0:T(8,128)(2,1)} %pad_maximum_fusion), calls=%async_computation.4 | async-start | bytes 917504 | tf_op jit(solution)/shard_map/all_to_all | solution.py:607
  172.7 2.3 %reduce-scatter.2.cloned.1.call-done = bf16[32,1024]{1,0:T(8,128)(2,1)} async-done(((bf16[128,1024]{1,0:T(8,128)(2,1)}), bf16[32,1024]{1,0:T(8,128)(2,1)}) %reduce-scatter.2.cloned.1.call-update) | async-done | bytes 65552 | tf_op jit(solution)/shard_map/reduce_scatter | solution.py:761
  176.5 4.9 %collective-permute-done.12 = bf16[1,128,1024]{2,1,0:T(8,128)(2,1)S(1)} collective-permute-done((bf16[1,128,1024]{2,1,0:T(8,128)(2,1)S(1)}, bf16[1,128,1024]{2,1,0:T(8,128)(2,1)S(1)}, u32[]{:S(2)}, u32[]{:S(2)}) %collective-permute-start.12) | collective-permute-done | bytes 262176 | tf_op jit(solution)/shard_map/ppermute | solution.py:629
  (109 shorter events, 21.6 us)
Async XLA Ops:
  7.2 82.5 %all-gather.4.cloned.1.call-start = ((), (), s32[]{:S(2)}) async-start(), calls=%async_computation.6 | async-start | bytes 3538944 | tf_op jit(solution)/shard_map/all_gather | solution.py:611
  7.2 13.2 %collective-permute-start.1 = (bf16[192,1024]{1,0:T(8,128)(2,1)}, bf16[192,1024]{1,0:T(8,128)(2,1)S(1)}, u32[]{:S(2)}, u32[]{:S(2)}) collective-permute-start(bf16[192,1024]{1,0:T(8,128)(2,1)} %bitcast.58), channel_id=1, source_target_pairs={{0,8},{4,12},{8,0},{12,4},{16,24},{20,28},{24,16},{28,20},{1,9},{5... | collective-permute-start | bytes 1179656 | tf_op jit(solution)/shard_map/ppermute | solution.py:618
  10.2 19.2 %collective-permute-start.3 = (bf16[192,1024]{1,0:T(8,128)(2,1)}, bf16[192,1024]{1,0:T(8,128)(2,1)S(1)}, u32[]{:S(2)}, u32[]{:S(2)}) collective-permute-start(bf16[192,1024]{1,0:T(8,128)(2,1)} %bitcast.59), channel_id=1, source_target_pairs={{0,16},{4,20},{8,24},{12,28},{16,0},{20,4},{24,8},{28,12},{1,17},{... | collective-permute-start | bytes 1179656 | tf_op jit(solution)/shard_map/ppermute | solution.py:618
  11.7 17.7 %collective-permute-start.5 = (bf16[192,1024]{1,0:T(8,128)(2,1)}, bf16[192,1024]{1,0:T(8,128)(2,1)S(1)}, u32[]{:S(2)}, u32[]{:S(2)}) collective-permute-start(bf16[192,1024]{1,0:T(8,128)(2,1)} %bitcast.60), channel_id=1, source_target_pairs={{0,24},{4,28},{8,16},{12,20},{16,8},{20,12},{24,0},{28,4},{1,25},{... | collective-permute-start | bytes 1179656 | tf_op jit(solution)/shard_map/ppermute | solution.py:618
  11.8 18.7 %collective-permute-start = (bf16[192,1024]{1,0:T(8,128)(2,1)}, bf16[192,1024]{1,0:T(8,128)(2,1)S(1)}, u32[]{:S(2)}, u32[]{:S(2)}) collective-permute-start(bf16[192,1024]{1,0:T(8,128)(2,1)} %bitcast.61), channel_id=1, source_target_pairs={{0,4},{4,0},{8,12},{12,8},{16,20},{20,16},{24,28},{28,24},{1,5},{5... | collective-permute-start | bytes 1179656 | tf_op jit(solution)/shard_map/ppermute | solution.py:618
  20.4 10.1 %collective-permute-start.2 = (bf16[192,1024]{1,0:T(8,128)(2,1)S(1)}, bf16[192,1024]{1,0:T(8,128)(2,1)S(1)}, u32[]{:S(2)}, u32[]{:S(2)}) collective-permute-start(bf16[192,1024]{1,0:T(8,128)(2,1)S(1)} %collective-permute-done.1.refs_2_), channel_id=1, source_target_pairs={{0,4},{4,0},{8,12},{12,8},{16,20},{20,16},{24,28},{28,24},{1,5},{5... | collective-permute-start | bytes 1179656 | tf_op jit(solution)/shard_map/ppermute | solution.py:618
  29.4 1.7 collective-permute-start.4
  29.5 2.3 %collective-permute-start.6 = (bf16[192,1024]{1,0:T(8,128)(2,1)S(1)}, bf16[192,1024]{1,0:T(8,128)(2,1)S(1)}, u32[]{:S(2)}, u32[]{:S(2)}) collective-permute-start(bf16[192,1024]{1,0:T(8,128)(2,1)S(1)} %collective-permute-done.5.refs_6_), channel_id=1, source_target_pairs={{0,4},{4,0},{8,12},{12,8},{16,20},{20,16},{24,28},{28,24},{1,5},{5... | collective-permute-start | bytes 1179656 | tf_op jit(solution)/shard_map/ppermute | solution.py:618
  40.3 71.9 %all-gather.6.cloned.1.call-start = ((), (), s32[]{:S(2)}) async-start(), calls=%async_computation.7 | async-start | bytes 3538944 | tf_op jit(solution)/shard_map/all_gather | solution.py:611
  48.2 28.6 %copy-start = (bf16[1536,128]{1,0:T(8,128)(2,1)}, bf16[1536,128]{1,0:T(8,128)(2,1)S(1)}, u32[]{:S(2)}) copy-start(bf16[1536,128]{1,0:T(8,128)(2,1)S(1)} %get-tuple-element.92.left) | copy-start | bytes 1179652
  60.4 29.3 %copy-start.2 = (bf16[1536,384]{1,0:T(8,128)(2,1)S(1)}, bf16[1536,384]{1,0:T(8,128)(2,1)}, u32[]{:S(2)}) copy-start(bf16[1536,384]{1,0:T(8,128)(2,1)} %get-tuple-element.56.qkv) | copy-start | bytes 3538948
  76.8 75.1 %all-gather.8.cloned.1.call-start = ((), (), s32[]{:S(2)}) async-start(), calls=%async_computation.8 | async-start | bytes 3538944 | tf_op jit(solution)/shard_map/all_gather | solution.py:611
  77.5 12.1 %all-to-all-start.1 = ((bf16[8,192,128]{2,1,0:T(8,128)(2,1)}), bf16[8,192,128]{2,1,0:T(8,128)(2,1)S(1)}, u32[]{:S(2)}, u32[]{:S(2)}) async-start(bf16[8,192,128]{2,1,0:T(8,128)(2,1)} %get-tuple-element.61), calls=%async_computation.1 | async-start | bytes 786432 | tf_op jit(solution)/shard_map/all_to_all | solution.py:607
  100.1 26.5 %all-to-all-start.2 = ((bf16[8,192,384]{2,1,0:T(8,128)(2,1)}), bf16[8,192,384]{2,1,0:T(8,128)(2,1)S(1)}, u32[]{:S(2)}, u32[]{:S(2)}) async-start(bf16[8,192,384]{2,1,0:T(8,128)(2,1)} %bitcast.6), calls=%async_computation.2 | async-start | bytes 2359296 | tf_op jit(solution)/shard_map/all_to_all | solution.py:607
  109.8 16.7 %collective-permute-start.7 = (bf16[2,8,32,384]{3,2,1,0:T(8,128)(2,1)}, bf16[2,8,32,384]{3,2,1,0:T(8,128)(2,1)S(1)}, u32[]{:S(2)}, u32[]{:S(2)}) collective-permute-start(bf16[2,8,32,384]{3,2,1,0:T(8,128)(2,1)} %get-tuple-element.66), channel_id=1, source_target_pairs={{0,1},{1,0},{2,3},{3,2},{4,5},{5,4},{6,7},{7,6},{8,9},{9,8},{10,11... | collective-permute-start | bytes 1179656 | tf_op jit(solution)/shard_map/ppermute | solution.py:629
  125.0 26.2 %collective-permute-start.8 = (bf16[2,8,32,512]{3,2,1,0:T(8,128)(2,1)}, bf16[2,8,32,512]{3,2,1,0:T(8,128)(2,1)S(1)}, u32[]{:S(2)}, u32[]{:S(2)}) collective-permute-start(bf16[2,8,32,512]{3,2,1,0:T(8,128)(2,1)} %get-tuple-element.77), channel_id=1, source_target_pairs={{0,1},{1,0},{2,3},{3,2},{4,5},{5,4},{6,7},{7,6},{8,9},{9,8},{10,11... | collective-permute-start | bytes 1572872 | tf_op jit(solution)/shard_map/ppermute | solution.py:629
  126.6 24.6 %collective-permute-start.9 = (bf16[8,32,384]{2,1,0:T(8,128)(2,1)S(1)}, bf16[8,32,384]{2,1,0:T(8,128)(2,1)S(1)}, u32[]{:S(2)}, u32[]{:S(2)}) collective-permute-start(bf16[8,32,384]{2,1,0:T(8,128)(2,1)S(1)} %fusion.6), channel_id=1, source_target_pairs={{0,2},{1,3},{2,0},{3,1},{4,6},{5,7},{6,4},{7,5},{8,10},{9,11},{10,... | collective-permute-start | bytes 589832 | tf_op jit(solution)/shard_map/ppermute | solution.py:629
  138.0 13.2 %all-to-all-start.3 = ((f32[32,1,288]{2,1,0:T(1,128)}), f32[32,1,288]{2,1,0:T(1,128)S(1)}, u32[]{:S(2)}, u32[]{:S(2)}) async-start(f32[32,1,288]{2,1,0:T(1,128)} %all_to_all.23), calls=%async_computation.3 | async-start | bytes 98304 | tf_op jit(solution)/shard_map/all_to_all | solution.py:607
  143.5 31.5 %reduce-scatter.2.cloned.1.call-start = ((), (), s32[]{:S(2)}) async-start(), calls=%async_computation.9 | async-start | bytes 327680 | tf_op jit(solution)/shard_map/reduce_scatter | solution.py:761
  143.6 21.8 %collective-permute-start.11 = (bf16[2,1,128,1024]{3,2,1,0:T(8,128)(2,1)}, bf16[2,1,128,1024]{3,2,1,0:T(8,128)(2,1)S(1)}, u32[]{:S(2)}, u32[]{:S(2)}) collective-permute-start(bf16[2,1,128,1024]{3,2,1,0:T(8,128)(2,1)} %get-tuple-element.88), channel_id=1, source_target_pairs={{0,1},{1,0},{2,3},{3,2},{4,5},{5,4},{6,7},{7,6},{8,9},{9,8},{10,11... | collective-permute-start | bytes 1572872 | tf_op jit(solution)/shard_map/ppermute | solution.py:629
  151.4 14.0 %collective-permute-start.10 = (bf16[8,32,512]{2,1,0:T(8,128)(2,1)S(1)}, bf16[8,32,512]{2,1,0:T(8,128)(2,1)S(1)}, u32[]{:S(2)}, u32[]{:S(2)}) collective-permute-start(bf16[8,32,512]{2,1,0:T(8,128)(2,1)S(1)} %get-tuple-element.101), channel_id=1, source_target_pairs={{0,2},{1,3},{2,0},{3,1},{4,6},{5,7},{6,4},{7,5},{8,10},{9,11},{10,... | collective-permute-start | bytes 786440 | tf_op jit(solution)/shard_map/ppermute | solution.py:629
  155.3 26.2 %copy-start.12 = (bf16[1,128,1024]{2,1,0:T(8,128)(2,1)S(1)}, bf16[1,128,1024]{2,1,0:T(8,128)(2,1)}, u32[]{:S(2)}) copy-start(bf16[1,128,1024]{2,1,0:T(8,128)(2,1)} %get-tuple-element.94) | copy-start | bytes 786436
  165.4 16.0 %collective-permute-start.12 = (bf16[1,128,1024]{2,1,0:T(8,128)(2,1)S(1)}, bf16[1,128,1024]{2,1,0:T(8,128)(2,1)S(1)}, u32[]{:S(2)}, u32[]{:S(2)}) collective-permute-start(bf16[1,128,1024]{2,1,0:T(8,128)(2,1)S(1)} %fusion.2), channel_id=1, source_target_pairs={{0,2},{1,3},{2,0},{3,1},{4,6},{5,7},{6,4},{7,5},{8,10},{9,11},{10,... | collective-permute-start | bytes 786440 | tf_op jit(solution)/shard_map/ppermute | solution.py:629
  168.5 13.8 %all-to-all-start.4 = ((bf16[8,32,896]{2,1,0:T(8,128)(2,1)}), bf16[8,32,896]{2,1,0:T(8,128)(2,1)S(1)}, u32[]{:S(2)}, u32[]{:S(2)}) async-start(bf16[8,32,896]{2,1,0:T(8,128)(2,1)} %pad_maximum_fusion), calls=%async_computation.4 | async-start | bytes 917504 | tf_op jit(solution)/shard_map/all_to_all | solution.py:607
  (20 other events, 158.6 us)
Sparse Core Ops, SparseCore 0:
  40.5 34.9 all-gather.3
  77.9 34.2 all-gather.5
  114.1 35.8 all-gather.7
  155.3 19.6 reduce-scatter.1

commit v7 on v6

--- a/solution.py
+++ b/solution.py
@@ -555,41 +555,82 @@
     back_sent,
     back_own,
     back_other,
+    held_normed,
+    held_grad,
+    held_in,
+    held_back,
+    active,
+    grads,
     in_total,
     back_total,
+    arrived,
 ):
-    active, grads = hidden(normed[...], grad_out[...], w_in[...], b_in, w_back[...])
-    accumulate(in_total, matmul_left(normed[...], grads))
-    accumulate(back_total, matmul_left(active, grad_out[...]))
-
-    @pl.when(pl.program_id(0) == pl.num_programs(0) - 1)
-    def _():
-        pick_blocks(places[1], in_total, in_sent, in_own, in_other)
-        pick_blocks(places[1], back_total, back_sent, back_own, back_other)
-
-
-def feed_products(places, normed, kept, w_in, b_in, w_back, seq_count):
+    pieces, chunk, _ = held_normed.shape
+    columns = held_in.shape[1]
+    own = pl.ds(pl.multiple_of(places[0] * columns, columns), columns)
+    weights = (
+        pltpu.make_async_copy(w_in.at[:, own], held_in, arrived.at[0, pieces]),
+        pltpu.make_async_copy(w_back.at[own, :], held_back, arrived.at[1, pieces]),
+    )
+    loads = [
+        (
+            pltpu.make_async_copy(normed.at[pl.ds(i * chunk, chunk)], held_normed.at[i], arrived.at[0, i]),
+            pltpu.make_async_copy(grad_out.at[pl.ds(i * chunk, chunk)], held_grad.at[i], arrived.at[1, i]),
+        )
+        for i in range(pieces)
+    ]
+    for pair in (weights, *loads):
+        for load in pair:
+            load.start()
+    for load in weights:
+        load.wait()
+    for i, pair in enumerate(loads):
+        for load in pair:
+            load.wait()
+        active[i], grads[i] = hidden(held_normed[i], held_grad[i], held_in[...], b_in, held_back[...])
+    rows = pieces * chunk
+    model = held_normed.shape[2]
+    in_total[...] = matmul_left(
+        held_normed[...].reshape(rows, model), grads[...].reshape(rows, columns)
+    ).reshape(in_total.shape)
+    pick_blocks(places[1], in_total, in_sent, in_own, in_other)
+    back_total[...] = matmul_left(
+        active[...].reshape(rows, columns), held_grad[...].reshape(rows, model)
+    ).reshape(back_total.shape)
+    pick_blocks(places[1], back_total, back_sent, back_own, back_other)
+
+
+def feed_products(places, normed, grad_out, w_in, b_in, w_back, seq_count):
     tokens, model = normed.shape
     columns = w_in.shape[1] // seq_count
-    chunk = 768
+    chunk = 384
+    pieces = tokens // chunk
     slim = model // (4 * seq_count)
     back_slim = columns // 4
+    anywhere = pl.BlockSpec(memory_space=pl.ANY)
     return pl.pallas_call(
         feed_products_kernel,
         grid_spec=pltpu.PrefetchScalarGridSpec(
             num_scalar_prefetch=1,
-            grid=(tokens // chunk,),
+            grid=(1,),
             in_specs=[
-                pl.BlockSpec((chunk, model), lambda j, places: (j, 0)),
-                pl.BlockSpec((chunk, model), lambda j, places: (j, 0)),
-                pl.BlockSpec((model, columns), lambda j, places: (0, places[0])),
+                anywhere,
+                anywhere,
+                anywhere,
                 pl.BlockSpec((1, columns), lambda j, places: (0, places[0])),
-                pl.BlockSpec((columns, model), lambda j, places: (places[0], 0)),
+                anywhere,
             ],
             out_specs=picked_specs(seq_count, slim, columns) + picked_specs(1, back_slim, model),
             scratch_shapes=[
+                pltpu.VMEM((pieces, chunk, model), low),
+                pltpu.VMEM((pieces, chunk, model), low),
+                pltpu.VMEM((model, columns), low),
+                pltpu.VMEM((columns, model), low),
+                pltpu.VMEM((pieces, chunk, columns), low),
+                pltpu.VMEM((pieces, chunk, columns), low),
                 pltpu.VMEM((seq_count, 4, slim, columns), full),
                 pltpu.VMEM((1, 4, back_slim, model), full),
+                pltpu.SemaphoreType.DMA((2, pieces + 1)),
             ],
         ),
         out_shape=picked_shapes(seq_count, slim, columns) + picked_shapes(1, back_slim, model),
@@ -600,7 +641,7 @@
             transcendentals=0,
         ),
         name="feed_products",
-    )(places, normed, kept, w_in, b_in.reshape(1, -1), w_back)
+    )(places, normed, grad_out, w_in, b_in.reshape(1, -1), w_back)
 
 
 def swap(blocks, axes):
@@ -738,7 +779,8 @@
     in_got = trade(in_sent, 1)
     qkv_got, in_own = together(qkv_got, in_own)
     qkv_own, qkv_other = first_sum(qkv_got, qkv_own, qkv_other)
-    grad_qkv_near, qkv_other = together(grad_qkv_near, qkv_other)
+    grad_qkv_near, qkv_other, back_sent = together(grad_qkv_near, qkv_other, back_sent)
+    back_got = trade(back_sent, 1)
     qkv_last = trade(qkv_other, 2)
     input_grad, gain_one_grads = project_back(
         rows_in, gain_one, grad_middle, grad_qkv_near, w_query, w_key, w_value
@@ -746,8 +788,6 @@
     small = [gain_one_grads[0], gain_one_grads[1], *gain_two_grads, grad_b_in[0]]
     packed = jnp.concatenate([v.reshape(device_count, -1) for v in small], axis=1)
     packed = swap(packed, ("seq", "batch"))
-    input_grad, back_sent = together(input_grad, back_sent)
-    back_got = trade(back_sent, 1)
     in_got, qkv_last, packed = together(in_got, qkv_last, packed)
     in_own, in_other = first_sum(in_got, in_own, in_other)
     in_last = trade(in_other, 2)

time: 192 us -> 191 us (level)
  no operation moved by 1% of the time
where the time goes in v7:
time: 191 us; the launch traced here: 190 us
  Pallas kernels  68.2 us (36%)
  waiting for transfers between devices  50.4 us (26%)
  starting transfers between devices  31.9 us (17%)
  between operations  14.7 us (8%)
  blocking collectives  12.2 us (6%)
  local copies, waits for them, and re-layouts  8.24 us (4%)
  other arithmetic  4.82 us (3%)
    ppermute x7, waiting for transfers between devices, move(): return lax.ppermute(block, 'seq', [(i, i ^ distance) for i in range(count)])  18.9 us
    all_to_all x4, starting transfers between devices, swap(): return lax.all_to_all(blocks, axes, split_axis=0, concat_axis=0, tiled=True)  16.5 us
    pallas_call x1, Pallas kernels, feed(): pl.pallas_call(feed_kernel, out_shape=(jax.ShapeDtypeStruct((tokens, mode...  16.3 us
    ppermute x6, waiting for transfers between devices, trade(): return lax.ppermute(block, 'batch', [(i, i ^ distance) for i in range(4)])  13.6 us
    all_to_all x4, waiting for transfers between devices, swap(): return lax.all_to_all(blocks, axes, split_axis=0, concat_axis=0, tiled=True)  13.3 us
    all_to_all x1, blocking collectives, swap(): return lax.all_to_all(blocks, axes, split_axis=0, concat_axis=0, tiled=True)  12.2 us
    pallas_call x1, Pallas kernels, feed_products(): pl.pallas_call(feed_products_kernel, grid_spec=pltpu.PrefetchScalarGridSp...  12 us
    pallas_call x1, Pallas kernels, attend_back(): pl.pallas_call(functools.partial(attend_back_kernel, block_count, head_co...  10.4 us
  transfers between devices with their start and end apart: 21, of which 10 were waited for; matrix products, arithmetic and copies ran while one was open for 4% of the time, Pallas kernels for 32%

profile of v7, /device:TPU:0, one launch (start us, length us, event | category | flops | bytes accessed | tf_op | source)
XLA Modules:
  0.0 190.5 jit_solution(5676595074102985939)
XLA Ops:
  7.2 3.0 %collective-permute-start.1 = (bf16[192,1024]{1,0:T(8,128)(2,1)}, bf16[192,1024]{1,0:T(8,128)(2,1)S(1)}, u32[]{:S(2)}, u32[]{:S(2)}) collective-permute-start(bf16[192,1024]{1,0:T(8,128)(2,1)} %bitcast.58), channel_id=1, source_target_pairs={{0,8},{4,12},{8,0},{12,4},{16,24},{20,28},{24,16},{28,20},{1,9},{5... | collective-permute-start | bytes 1179656 | tf_op jit(solution)/shard_map/ppermute | solution.py:659
  11.8 8.6 %collective-permute-done.1.refs_2_ = bf16[192,1024]{1,0:T(8,128)(2,1)S(1)} collective-permute-done((bf16[192,1024]{1,0:T(8,128)(2,1)}, bf16[192,1024]{1,0:T(8,128)(2,1)S(1)}, u32[]{:S(2)}, u32[]{:S(2)}) %collective-permute-start.1) | collective-permute-done | bytes 393248 | tf_op jit(solution)/shard_map/ppermute | solution.py:659
  20.4 9.1 %collective-permute-done.3.refs_4_ = bf16[192,1024]{1,0:T(8,128)(2,1)S(1)} collective-permute-done((bf16[192,1024]{1,0:T(8,128)(2,1)}, bf16[192,1024]{1,0:T(8,128)(2,1)S(1)}, u32[]{:S(2)}, u32[]{:S(2)}) %collective-permute-start.3) | collective-permute-done | bytes 393248 | tf_op jit(solution)/shard_map/ppermute | solution.py:659
  32.5 7.8 %project.1 = (bf16[1536,384]{1,0:T(8,128)(2,1)}, bf16[1536,1024]{1,0:T(8,128)(2,1)}) custom-call(s32[8]{0:T(128)} %iota_xor_fusion.rows, s32[1]{0:T(128)} %bitcast.1.column, bf16[192,1024]{1,0:T(8,128)(2,1)} %bitcast.62, bf16[192,1024]{1,0:T(8,128)(2,1)} %copy-done.8, bf16[192,1024]{1,0:T(8,128)(2,1)} %copy-done.5, bf16[192,1024]{1,0:T(8,128)(2,1)} %copy-done.9, ...), custom_call_target="tpu_custom_call" | custom-call | flops 1207959552 | bytes 6291456 | tf_op jit(solution)/shard_map/project/pallas_call | solution.py:238
  42.5 5.7 %attend.1 = (bf16[1536,128]{1,0:T(8,128)(2,1)S(1)}, f32[24,1,128]{2,1,0:T(1,128)S(1)}) custom-call(s32[1,1]{1,0:T(1,128)S(6)} %copy.63.lens, s32[1,24,3]{2,1,0:T(8,128)S(1)} %copy.44.owners, s32[1,24,3]{2,1,0:T(8,128)S(1)} %copy.45.offsets, s32[1,1,2]{2,1,0:T(1,128)S(1)} %copy-done.3, bf16[1536,384]{1,0:T(8,128)(2,1)S(1)} %copy-done.1), custom_call_target="tpu_custom_call" | custom-call | flops 805306368 | bytes 1572864 | tf_op jit(solution)/shard_map/attend/pallas_call | solution.py:172
  48.2 12.2 %all_to_all.32.received = bf16[8,192,128]{2,1,0:T(8,128)(2,1)} all-to-all(bf16[8,192,128]{2,1,0:T(8,128)(2,1)S(1)} %bitcast.56), channel_id=1, replica_groups=mesh['seq'=8,'batch'=4] {'seq'}, dimensions={0} | all-to-all | bytes 786432 | tf_op jit(solution)/shard_map/all_to_all | solution.py:648
  60.4 16.3 %feed.1 = (bf16[192,1024]{1,0:T(8,128)(2,1)}, bf16[192,1024]{1,0:T(8,128)(2,1)}, f32[192,1024]{1,0:T(8,128)}, bf16[192,1024]{1,0:T(8,128)(2,1)}, bf16[8,192,128]...) custom-call(bf16[8,192,128]{2,1,0:T(8,128)(2,1)} %all_to_all.32.received, bf16[192,1024]{1,0:T(8,128)(2,1)} %bitcast.63, ...), custom_call_target="tpu_custom_call" | custom-call | flops 6442450944 | bytes 16777216 | tf_op jit(solution)/shard_map/feed/pallas_call | solution.py:418
  77.5 3.5 %all-to-all-start.1 = ((bf16[8,192,128]{2,1,0:T(8,128)(2,1)}), bf16[8,192,128]{2,1,0:T(8,128)(2,1)S(1)}, u32[]{:S(2)}, u32[]{:S(2)}) async-start(bf16[8,192,128]{2,1,0:T(8,128)(2,1)} %get-tuple-element.60), calls=%async_computation.1 | async-start | bytes 786432 | tf_op jit(solution)/shard_map/all_to_all | solution.py:648
  82.2 7.4 %all-to-all-done.1 = bf16[8,192,128]{2,1,0:T(8,128)(2,1)S(1)} async-done(((bf16[8,192,128]{2,1,0:T(8,128)(2,1)}), bf16[8,192,128]{2,1,0:T(8,128)(2,1)S(1)}, u32[]{:S(2)}, u32[]{:S(2)}) %all-to-all-start.1) | async-done | bytes 393248 | tf_op jit(solution)/shard_map/all_to_all | solution.py:648
  89.7 10.4 %attend_back.1.right = bf16[1536,384]{1,0:T(8,128)(2,1)} custom-call(s32[1,1]{1,0:T(1,128)S(6)} %copy.63.lens, s32[1,24,3]{2,1,0:T(8,128)S(1)} %copy.44.owners, s32[1,24,3]{2,1,0:T(8,128)S(1)} %copy.45.offsets, s32[1,1,2]{2,1,0:T(1,128)S(1)} %copy-done.3, bf16[1536,384]{1,0:T(8,128)(2,1)S(1)} %copy-done.2, f32[24,1,128]{2,1,0:T(1,128)S(1)} %get-tuple-element.59.log_total, ...), custom_call_target="tpu_custom_call" | custom-call | flops 2013265920 | bytes 3145728 | tf_op jit(solution)/shard_map/attend_back/pallas_call | solution.py:191
  100.1 3.9 %all-to-all-start.2 = ((bf16[8,192,384]{2,1,0:T(8,128)(2,1)}), bf16[8,192,384]{2,1,0:T(8,128)(2,1)S(1)}, u32[]{:S(2)}, u32[]{:S(2)}) async-start(bf16[8,192,384]{2,1,0:T(8,128)(2,1)} %bitcast.6), calls=%async_computation.2 | async-start | bytes 2359296 | tf_op jit(solution)/shard_map/all_to_all | solution.py:648
  104.3 5.6 %qkv_product.1 = (bf16[2,8,32,384]{3,2,1,0:T(8,128)(2,1)}, bf16[8,32,384]{2,1,0:T(8,128)(2,1)}, bf16[8,32,384]{2,1,0:T(8,128)(2,1)}) custom-call(s32[2]{0:T(128)} %pad_add_fusion.places, bf16[1536,1024]{1,0:T(8,128)(2,1)} %get-tuple-element.63.left, bf16[1536,384]{1,0:T(8,128)(2,1)} %attend_back.1.right), custom_call_target="tpu_custom_call" | custom-call | flops 1207959552 | bytes 4325376 | tf_op jit(solution)/shard_map/qkv_product/pallas_call | solution.py:490
  112.2 12.0 %feed_products.1 = (bf16[2,8,32,512]{3,2,1,0:T(8,128)(2,1)}, bf16[8,32,512]{2,1,0:T(8,128)(2,1)}, bf16[8,32,512]{2,1,0:T(8,128)(2,1)}, bf16[2,1,128,1024]{3,2,1,...) custom-call(s32[2]{0:T(128)} %pad_add_fusion.places, ...), custom_call_target="tpu_custom_call" | custom-call | flops 6442450944 | bytes 8388608 | tf_op jit(solution)/shard_map/feed_products/pallas_call | solution.py:611
  125.9 2.4 %collective-permute-start.9 = (bf16[8,32,384]{2,1,0:T(8,128)(2,1)S(1)}, bf16[8,32,384]{2,1,0:T(8,128)(2,1)S(1)}, u32[]{:S(2)}, u32[]{:S(2)}) collective-permute-start(bf16[8,32,384]{2,1,0:T(8,128)(2,1)S(1)} %fusion.6), channel_id=1, source_target_pairs={{0,2},{1,3},{2,0},{3,1},{4,6},{5,7},{6,4},{7,5},{8,10},{9,11},{10,... | collective-permute-start | bytes 589832 | tf_op jit(solution)/shard_map/ppermute | solution.py:670
  128.3 7.2 %project_back.1 = (bf16[192,1024]{1,0:T(8,128)(2,1)}, f32[2,1024]{1,0:T(2,128)}) custom-call(bf16[192,1024]{1,0:T(8,128)(2,1)} %bitcast.64, bf16[1024]{0:T(1024)(128)(2,1)} %gain.3, f32[192,1024]{1,0:T(8,128)} %get-tuple-element.58.grad_middle, bf16[8,192,384]{2,1,0:T(8,128)(2,1)} %copy-done.4, bf16[1024,1024]{1,0:T(8,128)(2,1)} %w_query.1, ...), custom_call_target="tpu_custom_call" | custom-call | flops 1207959552 | bytes 6291456 | tf_op jit(solution)/shard_map/project_back/pallas_call | solution.py:298
  137.2 5.5 %all-to-all-start.3 = ((f32[32,1,288]{2,1,0:T(1,128)}), f32[32,1,288]{2,1,0:T(1,128)S(1)}, u32[]{:S(2)}, u32[]{:S(2)}) async-start(f32[32,1,288]{2,1,0:T(1,128)} %all_to_all.23), calls=%async_computation.3 | async-start | bytes 98304 | tf_op jit(solution)/shard_map/all_to_all | solution.py:648
  142.8 1.8 collective-permute-start.11
  144.6 5.8 %all-to-all-done.3 = f32[32,1,288]{2,1,0:T(1,128)S(1)} async-done(((f32[32,1,288]{2,1,0:T(1,128)}), f32[32,1,288]{2,1,0:T(1,128)S(1)}, u32[]{:S(2)}, u32[]{:S(2)}) %all-to-all-start.3) | async-done | bytes 36896 | tf_op jit(solution)/shard_map/all_to_all | solution.py:648
  151.1 3.2 %out_product.1 = bf16[128,1024]{1,0:T(8,128)(2,1)} custom-call(bf16[1536,128]{1,0:T(8,128)(2,1)} %copy-done, bf16[1536,1024]{1,0:T(8,128)(2,1)} %all-gather.8.cloned.1.call-done.right), custom_call_target="tpu_custom_call" | custom-call | flops 402653184 | bytes 3538944 | tf_op jit(solution)/shard_map/out_product/pallas_call | solution.py:525
  155.1 9.2 %collective-permute-done.11 = bf16[2,1,128,1024]{3,2,1,0:T(8,128)(2,1)S(1)} collective-permute-done((bf16[2,1,128,1024]{3,2,1,0:T(8,128)(2,1)}, bf16[2,1,128,1024]{3,2,1,0:T(8,128)(2,1)S(1)}, u32[]{:S(2)}, u32[]{:S(2)}) %collective-permute-start.11) | collective-permute-done | bytes 524320 | tf_op jit(solution)/shard_map/ppermute | solution.py:670
  164.3 2.4 %collective-permute-start.12 = (bf16[1,128,1024]{2,1,0:T(8,128)(2,1)S(1)}, bf16[1,128,1024]{2,1,0:T(8,128)(2,1)S(1)}, u32[]{:S(2)}, u32[]{:S(2)}) collective-permute-start(bf16[1,128,1024]{2,1,0:T(8,128)(2,1)S(1)} %fusion.2), channel_id=1, source_target_pairs={{0,2},{1,3},{2,0},{3,1},{4,6},{5,7},{6,4},{7,5},{8,10},{9,11},{10,... | collective-permute-start | bytes 786440 | tf_op jit(solution)/shard_map/ppermute | solution.py:670
  167.7 3.5 %all-to-all-start.4 = ((bf16[8,32,896]{2,1,0:T(8,128)(2,1)}), bf16[8,32,896]{2,1,0:T(8,128)(2,1)S(1)}, u32[]{:S(2)}, u32[]{:S(2)}) async-start(bf16[8,32,896]{2,1,0:T(8,128)(2,1)} %pad_maximum_fusion), calls=%async_computation.4 | async-start | bytes 917504 | tf_op jit(solution)/shard_map/all_to_all | solution.py:648
  171.8 3.0 %reduce-scatter.2.cloned.1.call-done = bf16[32,1024]{1,0:T(8,128)(2,1)} async-done(((bf16[128,1024]{1,0:T(8,128)(2,1)}), bf16[32,1024]{1,0:T(8,128)(2,1)}) %reduce-scatter.2.cloned.1.call-update) | async-done | bytes 65552 | tf_op jit(solution)/shard_map/reduce_scatter | solution.py:801
  176.3 4.4 %collective-permute-done.12 = bf16[1,128,1024]{2,1,0:T(8,128)(2,1)S(1)} collective-permute-done((bf16[1,128,1024]{2,1,0:T(8,128)(2,1)S(1)}, bf16[1,128,1024]{2,1,0:T(8,128)(2,1)S(1)}, u32[]{:S(2)}, u32[]{:S(2)}) %collective-permute-start.12) | collective-permute-done | bytes 262176 | tf_op jit(solution)/shard_map/ppermute | solution.py:670
  (109 shorter events, 21.7 us)
Async XLA Ops:
  7.2 82.5 %all-gather.4.cloned.1.call-start = ((), (), s32[]{:S(2)}) async-start(), calls=%async_computation.6 | async-start | bytes 3538944 | tf_op jit(solution)/shard_map/all_gather | solution.py:652
  7.2 13.2 %collective-permute-start.1 = (bf16[192,1024]{1,0:T(8,128)(2,1)}, bf16[192,1024]{1,0:T(8,128)(2,1)S(1)}, u32[]{:S(2)}, u32[]{:S(2)}) collective-permute-start(bf16[192,1024]{1,0:T(8,128)(2,1)} %bitcast.58), channel_id=1, source_target_pairs={{0,8},{4,12},{8,0},{12,4},{16,24},{20,28},{24,16},{28,20},{1,9},{5... | collective-permute-start | bytes 1179656 | tf_op jit(solution)/shard_map/ppermute | solution.py:659
  10.2 19.2 %collective-permute-start.3 = (bf16[192,1024]{1,0:T(8,128)(2,1)}, bf16[192,1024]{1,0:T(8,128)(2,1)S(1)}, u32[]{:S(2)}, u32[]{:S(2)}) collective-permute-start(bf16[192,1024]{1,0:T(8,128)(2,1)} %bitcast.59), channel_id=1, source_target_pairs={{0,16},{4,20},{8,24},{12,28},{16,0},{20,4},{24,8},{28,12},{1,17},{... | collective-permute-start | bytes 1179656 | tf_op jit(solution)/shard_map/ppermute | solution.py:659
  11.7 17.7 %collective-permute-start.5 = (bf16[192,1024]{1,0:T(8,128)(2,1)}, bf16[192,1024]{1,0:T(8,128)(2,1)S(1)}, u32[]{:S(2)}, u32[]{:S(2)}) collective-permute-start(bf16[192,1024]{1,0:T(8,128)(2,1)} %bitcast.60), channel_id=1, source_target_pairs={{0,24},{4,28},{8,16},{12,20},{16,8},{20,12},{24,0},{28,4},{1,25},{... | collective-permute-start | bytes 1179656 | tf_op jit(solution)/shard_map/ppermute | solution.py:659
  11.8 18.7 %collective-permute-start = (bf16[192,1024]{1,0:T(8,128)(2,1)}, bf16[192,1024]{1,0:T(8,128)(2,1)S(1)}, u32[]{:S(2)}, u32[]{:S(2)}) collective-permute-start(bf16[192,1024]{1,0:T(8,128)(2,1)} %bitcast.61), channel_id=1, source_target_pairs={{0,4},{4,0},{8,12},{12,8},{16,20},{20,16},{24,28},{28,24},{1,5},{5... | collective-permute-start | bytes 1179656 | tf_op jit(solution)/shard_map/ppermute | solution.py:659
  20.4 10.1 %collective-permute-start.2 = (bf16[192,1024]{1,0:T(8,128)(2,1)S(1)}, bf16[192,1024]{1,0:T(8,128)(2,1)S(1)}, u32[]{:S(2)}, u32[]{:S(2)}) collective-permute-start(bf16[192,1024]{1,0:T(8,128)(2,1)S(1)} %collective-permute-done.1.refs_2_), channel_id=1, source_target_pairs={{0,4},{4,0},{8,12},{12,8},{16,20},{20,16},{24,28},{28,24},{1,5},{5... | collective-permute-start | bytes 1179656 | tf_op jit(solution)/shard_map/ppermute | solution.py:659
  29.4 1.7 collective-permute-start.4
  29.5 2.3 %collective-permute-start.6 = (bf16[192,1024]{1,0:T(8,128)(2,1)S(1)}, bf16[192,1024]{1,0:T(8,128)(2,1)S(1)}, u32[]{:S(2)}, u32[]{:S(2)}) collective-permute-start(bf16[192,1024]{1,0:T(8,128)(2,1)S(1)} %collective-permute-done.5.refs_6_), channel_id=1, source_target_pairs={{0,4},{4,0},{8,12},{12,8},{16,20},{20,16},{24,28},{28,24},{1,5},{5... | collective-permute-start | bytes 1179656 | tf_op jit(solution)/shard_map/ppermute | solution.py:659
  40.3 71.9 %all-gather.6.cloned.1.call-start = ((), (), s32[]{:S(2)}) async-start(), calls=%async_computation.7 | async-start | bytes 3538944 | tf_op jit(solution)/shard_map/all_gather | solution.py:652
  48.2 28.6 %copy-start = (bf16[1536,128]{1,0:T(8,128)(2,1)}, bf16[1536,128]{1,0:T(8,128)(2,1)S(1)}, u32[]{:S(2)}) copy-start(bf16[1536,128]{1,0:T(8,128)(2,1)S(1)} %get-tuple-element.90.left) | copy-start | bytes 1179652
  60.4 29.3 %copy-start.2 = (bf16[1536,384]{1,0:T(8,128)(2,1)S(1)}, bf16[1536,384]{1,0:T(8,128)(2,1)}, u32[]{:S(2)}) copy-start(bf16[1536,384]{1,0:T(8,128)(2,1)} %get-tuple-element.55.qkv) | copy-start | bytes 3538948
  76.8 74.3 %all-gather.8.cloned.1.call-start = ((), (), s32[]{:S(2)}) async-start(), calls=%async_computation.8 | async-start | bytes 3538944 | tf_op jit(solution)/shard_map/all_gather | solution.py:652
  77.5 12.1 %all-to-all-start.1 = ((bf16[8,192,128]{2,1,0:T(8,128)(2,1)}), bf16[8,192,128]{2,1,0:T(8,128)(2,1)S(1)}, u32[]{:S(2)}, u32[]{:S(2)}) async-start(bf16[8,192,128]{2,1,0:T(8,128)(2,1)} %get-tuple-element.60), calls=%async_computation.1 | async-start | bytes 786432 | tf_op jit(solution)/shard_map/all_to_all | solution.py:648
  100.1 25.8 %all-to-all-start.2 = ((bf16[8,192,384]{2,1,0:T(8,128)(2,1)}), bf16[8,192,384]{2,1,0:T(8,128)(2,1)S(1)}, u32[]{:S(2)}, u32[]{:S(2)}) async-start(bf16[8,192,384]{2,1,0:T(8,128)(2,1)} %bitcast.6), calls=%async_computation.2 | async-start | bytes 2359296 | tf_op jit(solution)/shard_map/all_to_all | solution.py:648
  109.8 16.0 %collective-permute-start.7 = (bf16[2,8,32,384]{3,2,1,0:T(8,128)(2,1)}, bf16[2,8,32,384]{3,2,1,0:T(8,128)(2,1)S(1)}, u32[]{:S(2)}, u32[]{:S(2)}) collective-permute-start(bf16[2,8,32,384]{3,2,1,0:T(8,128)(2,1)} %get-tuple-element.65), channel_id=1, source_target_pairs={{0,1},{1,0},{2,3},{3,2},{4,5},{5,4},{6,7},{7,6},{8,9},{9,8},{10,11... | collective-permute-start | bytes 1179656 | tf_op jit(solution)/shard_map/ppermute | solution.py:670
  124.2 26.2 %collective-permute-start.8 = (bf16[2,8,32,512]{3,2,1,0:T(8,128)(2,1)}, bf16[2,8,32,512]{3,2,1,0:T(8,128)(2,1)S(1)}, u32[]{:S(2)}, u32[]{:S(2)}) collective-permute-start(bf16[2,8,32,512]{3,2,1,0:T(8,128)(2,1)} %get-tuple-element.75), channel_id=1, source_target_pairs={{0,1},{1,0},{2,3},{3,2},{4,5},{5,4},{6,7},{7,6},{8,9},{9,8},{10,11... | collective-permute-start | bytes 1572872 | tf_op jit(solution)/shard_map/ppermute | solution.py:670
  125.9 24.5 %collective-permute-start.9 = (bf16[8,32,384]{2,1,0:T(8,128)(2,1)S(1)}, bf16[8,32,384]{2,1,0:T(8,128)(2,1)S(1)}, u32[]{:S(2)}, u32[]{:S(2)}) collective-permute-start(bf16[8,32,384]{2,1,0:T(8,128)(2,1)S(1)} %fusion.6), channel_id=1, source_target_pairs={{0,2},{1,3},{2,0},{3,1},{4,6},{5,7},{6,4},{7,5},{8,10},{9,11},{10,... | collective-permute-start | bytes 589832 | tf_op jit(solution)/shard_map/ppermute | solution.py:670
  137.2 13.2 %all-to-all-start.3 = ((f32[32,1,288]{2,1,0:T(1,128)}), f32[32,1,288]{2,1,0:T(1,128)S(1)}, u32[]{:S(2)}, u32[]{:S(2)}) async-start(f32[32,1,288]{2,1,0:T(1,128)} %all_to_all.23), calls=%async_computation.3 | async-start | bytes 98304 | tf_op jit(solution)/shard_map/all_to_all | solution.py:648
  142.7 32.1 %reduce-scatter.2.cloned.1.call-start = ((), (), s32[]{:S(2)}) async-start(), calls=%async_computation.9 | async-start | bytes 327680 | tf_op jit(solution)/shard_map/reduce_scatter | solution.py:801
  142.8 21.5 %collective-permute-start.11 = (bf16[2,1,128,1024]{3,2,1,0:T(8,128)(2,1)}, bf16[2,1,128,1024]{3,2,1,0:T(8,128)(2,1)S(1)}, u32[]{:S(2)}, u32[]{:S(2)}) collective-permute-start(bf16[2,1,128,1024]{3,2,1,0:T(8,128)(2,1)} %get-tuple-element.86), channel_id=1, source_target_pairs={{0,1},{1,0},{2,3},{3,2},{4,5},{5,4},{6,7},{7,6},{8,9},{9,8},{10,11... | collective-permute-start | bytes 1572872 | tf_op jit(solution)/shard_map/ppermute | solution.py:670
  150.6 13.7 %collective-permute-start.10 = (bf16[8,32,512]{2,1,0:T(8,128)(2,1)S(1)}, bf16[8,32,512]{2,1,0:T(8,128)(2,1)S(1)}, u32[]{:S(2)}, u32[]{:S(2)}) collective-permute-start(bf16[8,32,512]{2,1,0:T(8,128)(2,1)S(1)} %get-tuple-element.99), channel_id=1, source_target_pairs={{0,2},{1,3},{2,0},{3,1},{4,6},{5,7},{6,4},{7,5},{8,10},{9,11},{10,... | collective-permute-start | bytes 786440 | tf_op jit(solution)/shard_map/ppermute | solution.py:670
  154.4 26.2 %copy-start.12 = (bf16[1,128,1024]{2,1,0:T(8,128)(2,1)S(1)}, bf16[1,128,1024]{2,1,0:T(8,128)(2,1)}, u32[]{:S(2)}) copy-start(bf16[1,128,1024]{2,1,0:T(8,128)(2,1)} %get-tuple-element.92) | copy-start | bytes 786436
  164.3 16.3 %collective-permute-start.12 = (bf16[1,128,1024]{2,1,0:T(8,128)(2,1)S(1)}, bf16[1,128,1024]{2,1,0:T(8,128)(2,1)S(1)}, u32[]{:S(2)}, u32[]{:S(2)}) collective-permute-start(bf16[1,128,1024]{2,1,0:T(8,128)(2,1)S(1)} %fusion.2), channel_id=1, source_target_pairs={{0,2},{1,3},{2,0},{3,1},{4,6},{5,7},{6,4},{7,5},{8,10},{9,11},{10,... | collective-permute-start | bytes 786440 | tf_op jit(solution)/shard_map/ppermute | solution.py:670
  167.7 13.9 %all-to-all-start.4 = ((bf16[8,32,896]{2,1,0:T(8,128)(2,1)}), bf16[8,32,896]{2,1,0:T(8,128)(2,1)S(1)}, u32[]{:S(2)}, u32[]{:S(2)}) async-start(bf16[8,32,896]{2,1,0:T(8,128)(2,1)} %pad_maximum_fusion), calls=%async_computation.4 | async-start | bytes 917504 | tf_op jit(solution)/shard_map/all_to_all | solution.py:648
  (20 other events, 157.5 us)
Sparse Core Ops, SparseCore 0:
  40.5 34.9 all-gather.3
  77.9 34.2 all-gather.5
  114.1 35.9 all-gather.7
  154.5 20.3 reduce-scatter.1

commit v8 on v7

--- a/solution.py
+++ b/solution.py
@@ -170,7 +170,7 @@
     rows, width = qkv.shape[0], qkv.shape[1] // 3
     total_blocks = rows // BLK
     return pl.pallas_call(
-        functools.partial(attend_kernel, block_count, head_count, scale, unroll_of(total_blocks, 8)),
+        functools.partial(attend_kernel, block_count, head_count, scale, unroll_of(total_blocks, 6)),
         out_shape=(
             jax.ShapeDtypeStruct((rows, width), low),
             jax.ShapeDtypeStruct((total_blocks, 1, head_count * BLK), full),

time: 191 us -> 190 us (level)
  transfers between devices with their start and end apart: 21 -> 21, of which waited for: 10 -> 9; matrix products, arithmetic and copies ran while one was open for 4% -> 4% of each run, Pallas kernels for 32% -> 32%
where the time goes in v8:
time: 190 us; the launch traced here: 189 us
  Pallas kernels  68.4 us (36%)
  waiting for transfers between devices  50.4 us (27%)
  starting transfers between devices  31.1 us (16%)
  between operations  14.7 us (8%)
  blocking collectives  11.7 us (6%)
  local copies, waits for them, and re-layouts  8.23 us (4%)
  other arithmetic  4.82 us (3%)
    ppermute x7, waiting for transfers between devices, move(): return lax.ppermute(block, 'seq', [(i, i ^ distance) for i in range(count)])  18.9 us
    all_to_all x4, starting transfers between devices, swap(): return lax.all_to_all(blocks, axes, split_axis=0, concat_axis=0, tiled=True)  16.1 us
    pallas_call x1, Pallas kernels, feed(): pl.pallas_call(feed_kernel, out_shape=(jax.ShapeDtypeStruct((tokens, mode...  16 us
    all_to_all x4, waiting for transfers between devices, swap(): return lax.all_to_all(blocks, axes, split_axis=0, concat_axis=0, tiled=True)  14.2 us
    ppermute x6, waiting for transfers between devices, trade(): return lax.ppermute(block, 'batch', [(i, i ^ distance) for i in range(4)])  13.7 us
    pallas_call x1, Pallas kernels, feed_products(): pl.pallas_call(feed_products_kernel, grid_spec=pltpu.PrefetchScalarGridSp...  12 us
    all_to_all x1, blocking collectives, swap(): return lax.all_to_all(blocks, axes, split_axis=0, concat_axis=0, tiled=True)  11.7 us
    pallas_call x1, Pallas kernels, attend_back(): pl.pallas_call(functools.partial(attend_back_kernel, block_count, head_co...  10.4 us
  transfers between devices with their start and end apart: 21, of which 9 were waited for; matrix products, arithmetic and copies ran while one was open for 4% of the time, Pallas kernels for 32%

profile of v8, /device:TPU:0, one launch (start us, length us, event | category | flops | bytes accessed | tf_op | source)
XLA Modules:
  0.0 189.4 jit_solution(10583944569277276570)
XLA Ops:
  7.2 3.0 %collective-permute-start.1 = (bf16[192,1024]{1,0:T(8,128)(2,1)}, bf16[192,1024]{1,0:T(8,128)(2,1)S(1)}, u32[]{:S(2)}, u32[]{:S(2)}) collective-permute-start(bf16[192,1024]{1,0:T(8,128)(2,1)} %bitcast.58), channel_id=1, source_target_pairs={{0,8},{4,12},{8,0},{12,4},{16,24},{20,28},{24,16},{28,20},{1,9},{5... | collective-permute-start | bytes 1179656 | tf_op jit(solution)/shard_map/ppermute | solution.py:659
  11.8 8.6 %collective-permute-done.1.refs_2_ = bf16[192,1024]{1,0:T(8,128)(2,1)S(1)} collective-permute-done((bf16[192,1024]{1,0:T(8,128)(2,1)}, bf16[192,1024]{1,0:T(8,128)(2,1)S(1)}, u32[]{:S(2)}, u32[]{:S(2)}) %collective-permute-start.1) | collective-permute-done | bytes 393248 | tf_op jit(solution)/shard_map/ppermute | solution.py:659
  20.4 9.1 %collective-permute-done.3.refs_4_ = bf16[192,1024]{1,0:T(8,128)(2,1)S(1)} collective-permute-done((bf16[192,1024]{1,0:T(8,128)(2,1)}, bf16[192,1024]{1,0:T(8,128)(2,1)S(1)}, u32[]{:S(2)}, u32[]{:S(2)}) %collective-permute-start.3) | collective-permute-done | bytes 393248 | tf_op jit(solution)/shard_map/ppermute | solution.py:659
  32.5 7.8 %project.1 = (bf16[1536,384]{1,0:T(8,128)(2,1)}, bf16[1536,1024]{1,0:T(8,128)(2,1)}) custom-call(s32[8]{0:T(128)} %iota_xor_fusion.rows, s32[1]{0:T(128)} %bitcast.1.column, bf16[192,1024]{1,0:T(8,128)(2,1)} %bitcast.62, bf16[192,1024]{1,0:T(8,128)(2,1)} %copy-done.8, bf16[192,1024]{1,0:T(8,128)(2,1)} %copy-done.5, bf16[192,1024]{1,0:T(8,128)(2,1)} %copy-done.9, ...), custom_call_target="tpu_custom_call" | custom-call | flops 1207959552 | bytes 6291456 | tf_op jit(solution)/shard_map/project/pallas_call | solution.py:238
  42.5 6.3 %attend.1 = (bf16[1536,128]{1,0:T(8,128)(2,1)S(1)}, f32[24,1,128]{2,1,0:T(1,128)S(1)}) custom-call(s32[1,1]{1,0:T(1,128)S(6)} %copy.63.lens, s32[1,24,3]{2,1,0:T(8,128)S(1)} %copy.44.owners, s32[1,24,3]{2,1,0:T(8,128)S(1)} %copy.45.offsets, s32[1,1,2]{2,1,0:T(1,128)S(1)} %copy-done.3, bf16[1536,384]{1,0:T(8,128)(2,1)S(1)} %copy-done.1), custom_call_target="tpu_custom_call" | custom-call | flops 805306368 | bytes 1572864 | tf_op jit(solution)/shard_map/attend/pallas_call | solution.py:172
  48.8 11.7 %all_to_all.32.received = bf16[8,192,128]{2,1,0:T(8,128)(2,1)} all-to-all(bf16[8,192,128]{2,1,0:T(8,128)(2,1)S(1)} %bitcast.56), channel_id=1, replica_groups=mesh['seq'=8,'batch'=4] {'seq'}, dimensions={0} | all-to-all | bytes 786432 | tf_op jit(solution)/shard_map/all_to_all | solution.py:648
  60.5 16.0 %feed.1 = (bf16[192,1024]{1,0:T(8,128)(2,1)}, bf16[192,1024]{1,0:T(8,128)(2,1)}, f32[192,1024]{1,0:T(8,128)}, bf16[192,1024]{1,0:T(8,128)(2,1)}, bf16[8,192,128]...) custom-call(bf16[8,192,128]{2,1,0:T(8,128)(2,1)} %all_to_all.32.received, bf16[192,1024]{1,0:T(8,128)(2,1)} %bitcast.63, ...), custom_call_target="tpu_custom_call" | custom-call | flops 6442450944 | bytes 16777216 | tf_op jit(solution)/shard_map/feed/pallas_call | solution.py:418
  77.3 3.5 %all-to-all-start.1 = ((bf16[8,192,128]{2,1,0:T(8,128)(2,1)}), bf16[8,192,128]{2,1,0:T(8,128)(2,1)S(1)}, u32[]{:S(2)}, u32[]{:S(2)}) async-start(bf16[8,192,128]{2,1,0:T(8,128)(2,1)} %get-tuple-element.60), calls=%async_computation.1 | async-start | bytes 786432 | tf_op jit(solution)/shard_map/all_to_all | solution.py:648
  81.9 8.4 %all-to-all-done.1 = bf16[8,192,128]{2,1,0:T(8,128)(2,1)S(1)} async-done(((bf16[8,192,128]{2,1,0:T(8,128)(2,1)}), bf16[8,192,128]{2,1,0:T(8,128)(2,1)S(1)}, u32[]{:S(2)}, u32[]{:S(2)}) %all-to-all-start.1) | async-done | bytes 393248 | tf_op jit(solution)/shard_map/all_to_all | solution.py:648
  90.3 10.4 %attend_back.1.right = bf16[1536,384]{1,0:T(8,128)(2,1)} custom-call(s32[1,1]{1,0:T(1,128)S(6)} %copy.63.lens, s32[1,24,3]{2,1,0:T(8,128)S(1)} %copy.44.owners, s32[1,24,3]{2,1,0:T(8,128)S(1)} %copy.45.offsets, s32[1,1,2]{2,1,0:T(1,128)S(1)} %copy-done.3, bf16[1536,384]{1,0:T(8,128)(2,1)S(1)} %copy-done.2, f32[24,1,128]{2,1,0:T(1,128)S(1)} %get-tuple-element.59.log_total, ...), custom_call_target="tpu_custom_call" | custom-call | flops 2013265920 | bytes 3145728 | tf_op jit(solution)/shard_map/attend_back/pallas_call | solution.py:191
  100.7 3.9 %all-to-all-start.2 = ((bf16[8,192,384]{2,1,0:T(8,128)(2,1)}), bf16[8,192,384]{2,1,0:T(8,128)(2,1)S(1)}, u32[]{:S(2)}, u32[]{:S(2)}) async-start(bf16[8,192,384]{2,1,0:T(8,128)(2,1)} %bitcast.6), calls=%async_computation.2 | async-start | bytes 2359296 | tf_op jit(solution)/shard_map/all_to_all | solution.py:648
  104.9 5.5 %qkv_product.1 = (bf16[2,8,32,384]{3,2,1,0:T(8,128)(2,1)}, bf16[8,32,384]{2,1,0:T(8,128)(2,1)}, bf16[8,32,384]{2,1,0:T(8,128)(2,1)}) custom-call(s32[2]{0:T(128)} %pad_add_fusion.places, bf16[1536,1024]{1,0:T(8,128)(2,1)} %get-tuple-element.63.left, bf16[1536,384]{1,0:T(8,128)(2,1)} %attend_back.1.right), custom_call_target="tpu_custom_call" | custom-call | flops 1207959552 | bytes 4325376 | tf_op jit(solution)/shard_map/qkv_product/pallas_call | solution.py:490
  110.4 2.1 %collective-permute-start.7 = (bf16[2,8,32,384]{3,2,1,0:T(8,128)(2,1)}, bf16[2,8,32,384]{3,2,1,0:T(8,128)(2,1)S(1)}, u32[]{:S(2)}, u32[]{:S(2)}) collective-permute-start(bf16[2,8,32,384]{3,2,1,0:T(8,128)(2,1)} %get-tuple-element.65), channel_id=1, source_target_pairs={{0,1},{1,0},{2,3},{3,2},{4,5},{5,4},{6,7},{7,6},{8,9},{9,8},{10,11... | collective-permute-start | bytes 1179656 | tf_op jit(solution)/shard_map/ppermute | solution.py:670
  112.5 12.0 %feed_products.1 = (bf16[2,8,32,512]{3,2,1,0:T(8,128)(2,1)}, bf16[8,32,512]{2,1,0:T(8,128)(2,1)}, bf16[8,32,512]{2,1,0:T(8,128)(2,1)}, bf16[2,1,128,1024]{3,2,1,...) custom-call(s32[2]{0:T(128)} %pad_add_fusion.places, ...), custom_call_target="tpu_custom_call" | custom-call | flops 6442450944 | bytes 8388608 | tf_op jit(solution)/shard_map/feed_products/pallas_call | solution.py:611
  124.7 2.9 %collective-permute-start.9 = (bf16[8,32,384]{2,1,0:T(8,128)(2,1)S(1)}, bf16[8,32,384]{2,1,0:T(8,128)(2,1)S(1)}, u32[]{:S(2)}, u32[]{:S(2)}) collective-permute-start(bf16[8,32,384]{2,1,0:T(8,128)(2,1)S(1)} %fusion.6), channel_id=1, source_target_pairs={{0,2},{1,3},{2,0},{3,1},{4,6},{5,7},{6,4},{7,5},{8,10},{9,11},{10,... | collective-permute-start | bytes 589832 | tf_op jit(solution)/shard_map/ppermute | solution.py:670
  127.7 7.2 %project_back.1 = (bf16[192,1024]{1,0:T(8,128)(2,1)}, f32[2,1024]{1,0:T(2,128)}) custom-call(bf16[192,1024]{1,0:T(8,128)(2,1)} %bitcast.64, bf16[1024]{0:T(1024)(128)(2,1)} %gain.3, f32[192,1024]{1,0:T(8,128)} %get-tuple-element.58.grad_middle, bf16[8,192,384]{2,1,0:T(8,128)(2,1)} %copy-done.4, bf16[1024,1024]{1,0:T(8,128)(2,1)} %w_query.1, ...), custom_call_target="tpu_custom_call" | custom-call | flops 1207959552 | bytes 6291456 | tf_op jit(solution)/shard_map/project_back/pallas_call | solution.py:298
  136.5 5.2 %all-to-all-start.3 = ((f32[32,1,288]{2,1,0:T(1,128)}), f32[32,1,288]{2,1,0:T(1,128)S(1)}, u32[]{:S(2)}, u32[]{:S(2)}) async-start(f32[32,1,288]{2,1,0:T(1,128)} %all_to_all.23), calls=%async_computation.3 | async-start | bytes 98304 | tf_op jit(solution)/shard_map/all_to_all | solution.py:648
  143.6 5.8 %all-to-all-done.3 = f32[32,1,288]{2,1,0:T(1,128)S(1)} async-done(((f32[32,1,288]{2,1,0:T(1,128)}), f32[32,1,288]{2,1,0:T(1,128)S(1)}, u32[]{:S(2)}, u32[]{:S(2)}) %all-to-all-start.3) | async-done | bytes 36896 | tf_op jit(solution)/shard_map/all_to_all | solution.py:648
  150.1 3.2 %out_product.1 = bf16[128,1024]{1,0:T(8,128)(2,1)} custom-call(bf16[1536,128]{1,0:T(8,128)(2,1)} %copy-done, bf16[1536,1024]{1,0:T(8,128)(2,1)} %all-gather.8.cloned.1.call-done.right), custom_call_target="tpu_custom_call" | custom-call | flops 402653184 | bytes 3538944 | tf_op jit(solution)/shard_map/out_product/pallas_call | solution.py:525
  154.1 9.3 %collective-permute-done.11 = bf16[2,1,128,1024]{3,2,1,0:T(8,128)(2,1)S(1)} collective-permute-done((bf16[2,1,128,1024]{3,2,1,0:T(8,128)(2,1)}, bf16[2,1,128,1024]{3,2,1,0:T(8,128)(2,1)S(1)}, u32[]{:S(2)}, u32[]{:S(2)}) %collective-permute-start.11) | collective-permute-done | bytes 524320 | tf_op jit(solution)/shard_map/ppermute | solution.py:670
  163.5 2.3 %collective-permute-start.12 = (bf16[1,128,1024]{2,1,0:T(8,128)(2,1)S(1)}, bf16[1,128,1024]{2,1,0:T(8,128)(2,1)S(1)}, u32[]{:S(2)}, u32[]{:S(2)}) collective-permute-start(bf16[1,128,1024]{2,1,0:T(8,128)(2,1)S(1)} %fusion.2), channel_id=1, source_target_pairs={{0,2},{1,3},{2,0},{3,1},{4,6},{5,7},{6,4},{7,5},{8,10},{9,11},{10,... | collective-permute-start | bytes 786440 | tf_op jit(solution)/shard_map/ppermute | solution.py:670
  166.7 3.6 %all-to-all-start.4 = ((bf16[8,32,896]{2,1,0:T(8,128)(2,1)}), bf16[8,32,896]{2,1,0:T(8,128)(2,1)S(1)}, u32[]{:S(2)}, u32[]{:S(2)}) async-start(bf16[8,32,896]{2,1,0:T(8,128)(2,1)} %pad_maximum_fusion), calls=%async_computation.4 | async-start | bytes 917504 | tf_op jit(solution)/shard_map/all_to_all | solution.py:648
  170.8 2.9 %reduce-scatter.2.cloned.1.call-done = bf16[32,1024]{1,0:T(8,128)(2,1)} async-done(((bf16[128,1024]{1,0:T(8,128)(2,1)}), bf16[32,1024]{1,0:T(8,128)(2,1)}) %reduce-scatter.2.cloned.1.call-update) | async-done | bytes 65552 | tf_op jit(solution)/shard_map/reduce_scatter | solution.py:801
  175.2 4.4 %collective-permute-done.12 = bf16[1,128,1024]{2,1,0:T(8,128)(2,1)S(1)} collective-permute-done((bf16[1,128,1024]{2,1,0:T(8,128)(2,1)S(1)}, bf16[1,128,1024]{2,1,0:T(8,128)(2,1)S(1)}, u32[]{:S(2)}, u32[]{:S(2)}) %collective-permute-start.12) | collective-permute-done | bytes 262176 | tf_op jit(solution)/shard_map/ppermute | solution.py:670
  (109 shorter events, 19.7 us)
Async XLA Ops:
  7.2 83.1 %all-gather.4.cloned.1.call-start = ((), (), s32[]{:S(2)}) async-start(), calls=%async_computation.6 | async-start | bytes 3538944 | tf_op jit(solution)/shard_map/all_gather | solution.py:652
  7.2 13.2 %collective-permute-start.1 = (bf16[192,1024]{1,0:T(8,128)(2,1)}, bf16[192,1024]{1,0:T(8,128)(2,1)S(1)}, u32[]{:S(2)}, u32[]{:S(2)}) collective-permute-start(bf16[192,1024]{1,0:T(8,128)(2,1)} %bitcast.58), channel_id=1, source_target_pairs={{0,8},{4,12},{8,0},{12,4},{16,24},{20,28},{24,16},{28,20},{1,9},{5... | collective-permute-start | bytes 1179656 | tf_op jit(solution)/shard_map/ppermute | solution.py:659
  10.2 19.2 %collective-permute-start.3 = (bf16[192,1024]{1,0:T(8,128)(2,1)}, bf16[192,1024]{1,0:T(8,128)(2,1)S(1)}, u32[]{:S(2)}, u32[]{:S(2)}) collective-permute-start(bf16[192,1024]{1,0:T(8,128)(2,1)} %bitcast.59), channel_id=1, source_target_pairs={{0,16},{4,20},{8,24},{12,28},{16,0},{20,4},{24,8},{28,12},{1,17},{... | collective-permute-start | bytes 1179656 | tf_op jit(solution)/shard_map/ppermute | solution.py:659
  11.7 17.7 %collective-permute-start.5 = (bf16[192,1024]{1,0:T(8,128)(2,1)}, bf16[192,1024]{1,0:T(8,128)(2,1)S(1)}, u32[]{:S(2)}, u32[]{:S(2)}) collective-permute-start(bf16[192,1024]{1,0:T(8,128)(2,1)} %bitcast.60), channel_id=1, source_target_pairs={{0,24},{4,28},{8,16},{12,20},{16,8},{20,12},{24,0},{28,4},{1,25},{... | collective-permute-start | bytes 1179656 | tf_op jit(solution)/shard_map/ppermute | solution.py:659
  11.8 18.7 %collective-permute-start = (bf16[192,1024]{1,0:T(8,128)(2,1)}, bf16[192,1024]{1,0:T(8,128)(2,1)S(1)}, u32[]{:S(2)}, u32[]{:S(2)}) collective-permute-start(bf16[192,1024]{1,0:T(8,128)(2,1)} %bitcast.61), channel_id=1, source_target_pairs={{0,4},{4,0},{8,12},{12,8},{16,20},{20,16},{24,28},{28,24},{1,5},{5... | collective-permute-start | bytes 1179656 | tf_op jit(solution)/shard_map/ppermute | solution.py:659
  20.4 10.1 %collective-permute-start.2 = (bf16[192,1024]{1,0:T(8,128)(2,1)S(1)}, bf16[192,1024]{1,0:T(8,128)(2,1)S(1)}, u32[]{:S(2)}, u32[]{:S(2)}) collective-permute-start(bf16[192,1024]{1,0:T(8,128)(2,1)S(1)} %collective-permute-done.1.refs_2_), channel_id=1, source_target_pairs={{0,4},{4,0},{8,12},{12,8},{16,20},{20,16},{24,28},{28,24},{1,5},{5... | collective-permute-start | bytes 1179656 | tf_op jit(solution)/shard_map/ppermute | solution.py:659
  29.4 1.7 collective-permute-start.4
  29.5 2.3 %collective-permute-start.6 = (bf16[192,1024]{1,0:T(8,128)(2,1)S(1)}, bf16[192,1024]{1,0:T(8,128)(2,1)S(1)}, u32[]{:S(2)}, u32[]{:S(2)}) collective-permute-start(bf16[192,1024]{1,0:T(8,128)(2,1)S(1)} %collective-permute-done.5.refs_6_), channel_id=1, source_target_pairs={{0,4},{4,0},{8,12},{12,8},{16,20},{20,16},{24,28},{28,24},{1,5},{5... | collective-permute-start | bytes 1179656 | tf_op jit(solution)/shard_map/ppermute | solution.py:659
  40.3 72.1 %all-gather.6.cloned.1.call-start = ((), (), s32[]{:S(2)}) async-start(), calls=%async_computation.7 | async-start | bytes 3538944 | tf_op jit(solution)/shard_map/all_gather | solution.py:652
  48.8 27.7 %copy-start = (bf16[1536,128]{1,0:T(8,128)(2,1)}, bf16[1536,128]{1,0:T(8,128)(2,1)S(1)}, u32[]{:S(2)}) copy-start(bf16[1536,128]{1,0:T(8,128)(2,1)S(1)} %get-tuple-element.90.left) | copy-start | bytes 1179652
  60.5 29.8 %copy-start.2 = (bf16[1536,384]{1,0:T(8,128)(2,1)S(1)}, bf16[1536,384]{1,0:T(8,128)(2,1)}, u32[]{:S(2)}) copy-start(bf16[1536,384]{1,0:T(8,128)(2,1)} %get-tuple-element.55.qkv) | copy-start | bytes 3538948
  76.5 73.6 %all-gather.8.cloned.1.call-start = ((), (), s32[]{:S(2)}) async-start(), calls=%async_computation.8 | async-start | bytes 3538944 | tf_op jit(solution)/shard_map/all_gather | solution.py:652
  77.3 13.0 %all-to-all-start.1 = ((bf16[8,192,128]{2,1,0:T(8,128)(2,1)}), bf16[8,192,128]{2,1,0:T(8,128)(2,1)S(1)}, u32[]{:S(2)}, u32[]{:S(2)}) async-start(bf16[8,192,128]{2,1,0:T(8,128)(2,1)} %get-tuple-element.60), calls=%async_computation.1 | async-start | bytes 786432 | tf_op jit(solution)/shard_map/all_to_all | solution.py:648
  100.7 24.0 %all-to-all-start.2 = ((bf16[8,192,384]{2,1,0:T(8,128)(2,1)}), bf16[8,192,384]{2,1,0:T(8,128)(2,1)S(1)}, u32[]{:S(2)}, u32[]{:S(2)}) async-start(bf16[8,192,384]{2,1,0:T(8,128)(2,1)} %bitcast.6), calls=%async_computation.2 | async-start | bytes 2359296 | tf_op jit(solution)/shard_map/all_to_all | solution.py:648
  110.4 14.2 %collective-permute-start.7 = (bf16[2,8,32,384]{3,2,1,0:T(8,128)(2,1)}, bf16[2,8,32,384]{3,2,1,0:T(8,128)(2,1)S(1)}, u32[]{:S(2)}, u32[]{:S(2)}) collective-permute-start(bf16[2,8,32,384]{3,2,1,0:T(8,128)(2,1)} %get-tuple-element.65), channel_id=1, source_target_pairs={{0,1},{1,0},{2,3},{3,2},{4,5},{5,4},{6,7},{7,6},{8,9},{9,8},{10,11... | collective-permute-start | bytes 1179656 | tf_op jit(solution)/shard_map/ppermute | solution.py:670
  124.5 24.9 %collective-permute-start.8 = (bf16[2,8,32,512]{3,2,1,0:T(8,128)(2,1)}, bf16[2,8,32,512]{3,2,1,0:T(8,128)(2,1)S(1)}, u32[]{:S(2)}, u32[]{:S(2)}) collective-permute-start(bf16[2,8,32,512]{3,2,1,0:T(8,128)(2,1)} %get-tuple-element.75), channel_id=1, source_target_pairs={{0,1},{1,0},{2,3},{3,2},{4,5},{5,4},{6,7},{7,6},{8,9},{9,8},{10,11... | collective-permute-start | bytes 1572872 | tf_op jit(solution)/shard_map/ppermute | solution.py:670
  124.7 24.7 %collective-permute-start.9 = (bf16[8,32,384]{2,1,0:T(8,128)(2,1)S(1)}, bf16[8,32,384]{2,1,0:T(8,128)(2,1)S(1)}, u32[]{:S(2)}, u32[]{:S(2)}) collective-permute-start(bf16[8,32,384]{2,1,0:T(8,128)(2,1)S(1)} %fusion.6), channel_id=1, source_target_pairs={{0,2},{1,3},{2,0},{3,1},{4,6},{5,7},{6,4},{7,5},{8,10},{9,11},{10,... | collective-permute-start | bytes 589832 | tf_op jit(solution)/shard_map/ppermute | solution.py:670
  136.5 12.9 %all-to-all-start.3 = ((f32[32,1,288]{2,1,0:T(1,128)}), f32[32,1,288]{2,1,0:T(1,128)S(1)}, u32[]{:S(2)}, u32[]{:S(2)}) async-start(f32[32,1,288]{2,1,0:T(1,128)} %all_to_all.23), calls=%async_computation.3 | async-start | bytes 98304 | tf_op jit(solution)/shard_map/all_to_all | solution.py:648
  141.7 32.0 %reduce-scatter.2.cloned.1.call-start = ((), (), s32[]{:S(2)}) async-start(), calls=%async_computation.9 | async-start | bytes 327680 | tf_op jit(solution)/shard_map/reduce_scatter | solution.py:801
  141.8 21.6 %collective-permute-start.11 = (bf16[2,1,128,1024]{3,2,1,0:T(8,128)(2,1)}, bf16[2,1,128,1024]{3,2,1,0:T(8,128)(2,1)S(1)}, u32[]{:S(2)}, u32[]{:S(2)}) collective-permute-start(bf16[2,1,128,1024]{3,2,1,0:T(8,128)(2,1)} %get-tuple-element.86), channel_id=1, source_target_pairs={{0,1},{1,0},{2,3},{3,2},{4,5},{5,4},{6,7},{7,6},{8,9},{9,8},{10,11... | collective-permute-start | bytes 1572872 | tf_op jit(solution)/shard_map/ppermute | solution.py:670
  149.6 13.9 %collective-permute-start.10 = (bf16[8,32,512]{2,1,0:T(8,128)(2,1)S(1)}, bf16[8,32,512]{2,1,0:T(8,128)(2,1)S(1)}, u32[]{:S(2)}, u32[]{:S(2)}) collective-permute-start(bf16[8,32,512]{2,1,0:T(8,128)(2,1)S(1)} %get-tuple-element.99), channel_id=1, source_target_pairs={{0,2},{1,3},{2,0},{3,1},{4,6},{5,7},{6,4},{7,5},{8,10},{9,11},{10,... | collective-permute-start | bytes 786440 | tf_op jit(solution)/shard_map/ppermute | solution.py:670
  153.4 26.2 %copy-start.12 = (bf16[1,128,1024]{2,1,0:T(8,128)(2,1)S(1)}, bf16[1,128,1024]{2,1,0:T(8,128)(2,1)}, u32[]{:S(2)}) copy-start(bf16[1,128,1024]{2,1,0:T(8,128)(2,1)} %get-tuple-element.92) | copy-start | bytes 786436
  163.5 16.1 %collective-permute-start.12 = (bf16[1,128,1024]{2,1,0:T(8,128)(2,1)S(1)}, bf16[1,128,1024]{2,1,0:T(8,128)(2,1)S(1)}, u32[]{:S(2)}, u32[]{:S(2)}) collective-permute-start(bf16[1,128,1024]{2,1,0:T(8,128)(2,1)S(1)} %fusion.2), channel_id=1, source_target_pairs={{0,2},{1,3},{2,0},{3,1},{4,6},{5,7},{6,4},{7,5},{8,10},{9,11},{10,... | collective-permute-start | bytes 786440 | tf_op jit(solution)/shard_map/ppermute | solution.py:670
  166.7 13.9 %all-to-all-start.4 = ((bf16[8,32,896]{2,1,0:T(8,128)(2,1)}), bf16[8,32,896]{2,1,0:T(8,128)(2,1)S(1)}, u32[]{:S(2)}, u32[]{:S(2)}) async-start(bf16[8,32,896]{2,1,0:T(8,128)(2,1)} %pad_maximum_fusion), calls=%async_computation.4 | async-start | bytes 917504 | tf_op jit(solution)/shard_map/all_to_all | solution.py:648
  (20 other events, 155.7 us)
Sparse Core Ops, SparseCore 0:
  40.5 34.0 all-gather.3
  77.0 34.6 all-gather.5
  113.5 35.3 all-gather.7
  153.5 20.2 reduce-scatter.1
